TPU v7x, 32 devices: a whole 2x2x4 slice. The times are simulated.
32 devices in a mesh: dp: 8 (over z, y), head: 4 (over x, core).
Axes of the slice: x: 2, y: 2, z: 4, core: 2. Of those that a mesh axis runs over, the one named last changes fastest.
Arguments:
- tokens: bfloat16 [32768, 512], P(('dp', 'head')), may hold values from -6 to 6
- segments: int32 [32768], P('dp'), may hold values from 0 to 255, never falling along the last dimension, each value on 1 to 256 neighbouring positions
- out_grad: bfloat16 [32768, 512], P(('dp', 'head')), may hold values from -6 to 6
- norm_params: float32 [4, 512], replicated, may hold values from -0.6 to 1.3
- norm_first: float32 [4, 512], replicated, may hold values from -0.0024414062 to 0.0024414062
- norm_second: float32 [4, 512], replicated, may hold values from 7.947286e-08 to 1.2715658e-06
- qkv_weight: float32 [512, 1536], P(None, 'head'), may hold values from -0.25 to 0.25
- qkv_moment: float32 [512, 1536], P(None, 'head'), may hold values from -0.0078125 to 0.0078125
- out_weight: float32 [512, 512], P('head'), may hold values from -2 to 2
- out_moment: float32 [512, 512], P('head'), may hold values from -0.0078125 to 0.0078125
- up_weight: float32 [512, 2048], P(None, ('dp', 'head')), may hold values from -0.25 to 0.25
- up_moment: float32 [512, 2048], P(None, ('dp', 'head')), may hold values from -0.0078125 to 0.0078125
- down_weight: float32 [512, 2048], P(None, ('dp', 'head')), may hold values from -0.125 to 0.125
- down_moment: float32 [512, 2048], P(None, ('dp', 'head')), may hold values from -0.0078125 to 0.0078125
Outputs:
- layer_out: bfloat16 [32768, 512], P(('dp', 'head'))
- input_grad: float32 [32768, 512], P(('dp', 'head'))
- grad_norm: float32 [], replicated
- clipped_grads: float32 [4, 512], replicated
- new_norm_first: float32 [4, 512], replicated
- new_norm_second: float32 [4, 512], replicated
- new_qkv_weight: float32 [512, 1536], P(None, 'head')
- new_qkv_moment: float32 [512, 1536], P(None, 'head')
- new_out_weight: float32 [512, 512], P('head')
- new_out_moment: float32 [512, 512], P('head')
- new_up_weight: float32 [512, 2048], P(None, ('dp', 'head'))
- new_up_moment: float32 [512, 2048], P(None, ('dp', 'head'))
- new_down_weight: float32 [512, 2048], P(None, ('dp', 'head'))
- new_down_moment: float32 [512, 2048], P(None, ('dp', 'head'))
Inputs may be any that keep to these rules, and one draw needn't show every extreme that they name: `segments`: segment ids never fall along the rows; each id covers 1 to 256 consecutive rows.
All inputs are finite; a program needn't handle non-finite values.
Results may differ from a plain program's by a relative error of at most 0.028.
Values may be sent and summed in bfloat16 or wider, within the bound.
A program may use at most 128 MiB of HBM per device.

v0:
```python
import math

import jax
import jax.numpy as jnp
from jax import lax
from jax.sharding import PartitionSpec as P

HEAD_DIM = 64
FF = 2048
SEQ = 512
NS_STEPS = 5


neg_fill = -1000000000.0
norm_eps = 1e-05
ns_a = 3.4445
ns_b = -4.775
ns_c = 2.0315
momentum_decay = 0.95
muon_rate = 0.5
muon_decay = 0.01
beta_one = 0.9
beta_two = 0.95


def normalize(values, gain, shift):
    mean = jnp.mean(values, axis=-1, keepdims=True)
    centered = values - mean
    factor = lax.rsqrt(jnp.mean(centered * centered, axis=-1, keepdims=True) + norm_eps)
    plain = centered * factor
    return (plain * gain + shift, plain, factor)


def normalize_back(upper, plain, factor, gain):
    inner = upper * gain
    lower = factor * (
        inner
        - jnp.mean(inner, axis=-1, keepdims=True)
        - plain * jnp.mean(inner * plain, axis=-1, keepdims=True)
    )
    return (lower, jnp.sum(upper * plain, axis=0), jnp.sum(upper, axis=0))


def masked_scores(query, keys, segment):
    scores = jnp.einsum(
        "qhd,khd->hqk", query, keys, preferred_element_type=jnp.float32
    ) * HEAD_DIM ** (-0.5)
    same = segment[:, None] == segment[None, :]
    return jnp.where(same[None], scores, neg_fill)


def attend_forward(block):
    query, keys, values, segment = block
    scores = masked_scores(query, keys, segment)
    top = jnp.max(scores, axis=-1, keepdims=True)
    weights = jnp.exp(scores - top)
    total = jnp.sum(weights, axis=-1, keepdims=True)
    probs = (weights / total).astype(jnp.bfloat16)
    context = jnp.einsum("hqk,khd->qhd", probs, values, preferred_element_type=jnp.float32)
    return (context.astype(jnp.bfloat16), top + jnp.log(total))


def attend_backward(block):
    query, keys, values, segment, context_grad, lse = block
    scores = masked_scores(query, keys, segment)
    probs = jnp.exp(scores - lse)
    probs_low = probs.astype(jnp.bfloat16)
    probs_grad = jnp.einsum(
        "qhd,khd->hqk", context_grad, values, preferred_element_type=jnp.float32
    )
    inner = jnp.sum(probs * probs_grad, axis=-1, keepdims=True)
    score_grad = (probs * (probs_grad - inner)).astype(jnp.bfloat16)
    query_grad = jnp.einsum(
        "hqk,khd->qhd", score_grad, keys, preferred_element_type=jnp.float32
    ) * HEAD_DIM ** (-0.5)
    key_grad = jnp.einsum(
        "hqk,qhd->khd", score_grad, query, preferred_element_type=jnp.float32
    ) * HEAD_DIM ** (-0.5)
    value_grad = jnp.einsum(
        "hqk,qhd->khd", probs_low, context_grad, preferred_element_type=jnp.float32
    )
    return jnp.stack([query_grad, key_grad, value_grad], axis=2).astype(jnp.bfloat16)


def gram_left(block):
    return lax.dot_general(
        block, block, (((1,), (1,)), ((), ())), preferred_element_type=jnp.float32
    )


def gram_right(block):
    return lax.dot_general(
        block, block, (((0,), (0,)), ((), ())), preferred_element_type=jnp.float32
    )


def squares_of(moment, grad, weight):
    return (
        jnp.stack([jnp.sum(moment * moment), jnp.sum(moment * grad), jnp.sum(grad * grad)]) * weight
    )


def shards(
    tokens,
    segments,
    out_grad,
    norm_params,
    norm_first,
    norm_second,
    qkv_weight,
    qkv_moment,
    out_weight,
    out_moment,
    up_weight,
    up_moment,
    down_weight,
    down_moment,
):
    width = tokens.shape[1]
    group = segments.shape[0]
    narrow = out_weight.shape[0]
    heads_here = narrow // HEAD_DIM
    sequences = group // SEQ
    inputs = tokens.astype(jnp.float32)
    first, first_plain, first_factor = normalize(inputs, norm_params[0], norm_params[1])
    first_all = lax.all_gather(first.astype(jnp.bfloat16), "head", axis=0, tiled=True)
    qkv_low = qkv_weight.astype(jnp.bfloat16)
    out_low = out_weight.astype(jnp.bfloat16)
    mixed = jnp.dot(first_all, qkv_low, preferred_element_type=jnp.float32).astype(jnp.bfloat16)
    mixed = mixed.reshape(sequences, SEQ, heads_here, 3, HEAD_DIM)
    segment_rows = segments.reshape(sequences, SEQ)
    query = mixed[:, :, :, 0]
    keys = mixed[:, :, :, 1]
    values = mixed[:, :, :, 2]
    context, lse = lax.map(attend_forward, (query, keys, values, segment_rows))
    context = context.reshape(group, narrow)
    context_rows = lax.all_to_all(context, "head", split_axis=0, concat_axis=1, tiled=True)
    out_full = lax.all_gather(out_low, "head", axis=0, tiled=True)
    attended = jnp.dot(context_rows, out_full, preferred_element_type=jnp.float32)
    middle = inputs + attended
    second, second_plain, second_factor = normalize(middle, norm_params[2], norm_params[3])
    second_low = second.astype(jnp.bfloat16)
    up_all, down_all = (
        lax.all_gather(up_weight.astype(jnp.bfloat16), ("dp", "head"), axis=1, tiled=True),
        lax.all_gather(down_weight.astype(jnp.bfloat16), ("dp", "head"), axis=1, tiled=True),
    )
    hidden = jnp.dot(second_low, up_all, preferred_element_type=jnp.float32)
    switch = jax.nn.sigmoid(1.702 * hidden)
    active = (hidden * switch).astype(jnp.bfloat16)
    result = middle + lax.dot_general(
        active, down_all, (((1,), (1,)), ((), ())), preferred_element_type=jnp.float32
    )
    layer_out = result.astype(jnp.bfloat16)
    down_grad = lax.dot_general(
        out_grad, active, (((0,), (0,)), ((), ())), preferred_element_type=jnp.float32
    )
    active_grad = jnp.dot(out_grad, down_all, preferred_element_type=jnp.float32)
    hidden_grad = (active_grad * (switch + 1.702 * hidden * switch * (1.0 - switch))).astype(
        jnp.bfloat16
    )
    up_grad = lax.dot_general(
        second_low, hidden_grad, (((0,), (0,)), ((), ())), preferred_element_type=jnp.float32
    )
    second_grad = lax.dot_general(
        hidden_grad, up_all, (((1,), (1,)), ((), ())), preferred_element_type=jnp.float32
    )
    up_part, down_part = (
        lax.psum_scatter(up_grad, ("dp", "head"), scatter_dimension=1, tiled=True),
        lax.psum_scatter(down_grad, ("dp", "head"), scatter_dimension=1, tiled=True),
    )
    middle_lower, gain_two, shift_two = normalize_back(
        second_grad, second_plain, second_factor, norm_params[2]
    )
    middle_grad = out_grad.astype(jnp.float32) + middle_lower
    attended_low = middle_grad.astype(jnp.bfloat16)
    rows_grad = lax.dot_general(
        attended_low, out_full, (((1,), (1,)), ((), ())), preferred_element_type=jnp.float32
    ).astype(jnp.bfloat16)
    context_grad = lax.all_to_all(rows_grad, "head", split_axis=1, concat_axis=0, tiled=True)
    whole_out = lax.dot_general(
        context_rows, attended_low, (((0,), (0,)), ((), ())), preferred_element_type=jnp.float32
    )
    out_part = lax.psum_scatter(
        whole_out.astype(jnp.bfloat16), "head", scatter_dimension=0, tiled=True
    )
    context_grad = context_grad.reshape(sequences, SEQ, heads_here, HEAD_DIM)
    mixed_grad = lax.map(attend_backward, (query, keys, values, segment_rows, context_grad, lse))
    mixed_grad = mixed_grad.reshape(group, 3 * narrow)
    qkv_part = lax.dot_general(
        first_all, mixed_grad, (((0,), (0,)), ((), ())), preferred_element_type=jnp.float32
    )
    mixed_rows = lax.all_to_all(mixed_grad, "head", split_axis=0, concat_axis=1, tiled=True)
    qkv_full = lax.all_gather(qkv_low, "head", axis=1, tiled=True)
    first_grad = lax.dot_general(
        mixed_rows, qkv_full, (((1,), (1,)), ((), ())), preferred_element_type=jnp.float32
    )
    input_lower, gain_one, shift_one = normalize_back(
        first_grad, first_plain, first_factor, norm_params[0]
    )
    input_grad = middle_grad + input_lower
    qkv_sum, out_sum = (
        lax.psum(qkv_part.astype(jnp.bfloat16), "dp").astype(jnp.float32),
        lax.psum(out_part, "dp").astype(jnp.float32),
    )
    leading = (lax.axis_index("dp") == 0).astype(jnp.float32)
    moments = [qkv_moment, out_moment, up_moment, down_moment]
    grads = [qkv_sum, out_sum, up_part, down_part]
    stats = jnp.stack(
        [
            squares_of(qkv_moment, qkv_sum, leading),
            squares_of(out_moment, out_sum, leading),
            squares_of(up_moment, up_part, 1.0),
            squares_of(down_moment, down_part, 1.0),
        ]
    )
    vector_part = jnp.stack([gain_one, shift_one, gain_two, shift_two])
    vector_sum, stat_sum = lax.psum((vector_part, stats), ("dp", "head"))
    grad_norm = jnp.sqrt(jnp.sum(stat_sum[:, 2]) + jnp.sum(vector_sum * vector_sum))
    clip = jnp.minimum(1.0, 1.0 / (grad_norm + 1e-06))
    sizes = jnp.sqrt(
        momentum_decay * momentum_decay * stat_sum[:, 0]
        + 2.0 * momentum_decay * clip * stat_sum[:, 1]
        + clip * clip * stat_sum[:, 2]
    )
    new_moments = [momentum_decay * moments[index] + clip * grads[index] for index in range(4)]
    starts = [
        (new_moments[index] / (sizes[index] + 1e-07)).astype(jnp.bfloat16) for index in range(4)
    ]
    up_block, down_block = (
        lax.all_gather(starts[2], "dp", axis=1, tiled=True),
        lax.all_gather(starts[3], "dp", axis=1, tiled=True),
    )
    blocks = [starts[0], starts[1], up_block, down_block]
    for turn in range(NS_STEPS):
        partials = (
            gram_left(blocks[0]),
            gram_right(blocks[1]),
            gram_left(blocks[2]),
            gram_left(blocks[3]),
        )
        grams = (
            lax.psum(partials[0].astype(jnp.bfloat16), "head").astype(jnp.float32),
            lax.psum(partials[1].astype(jnp.bfloat16), "head").astype(jnp.float32),
            lax.psum(partials[2].astype(jnp.bfloat16), "head").astype(jnp.float32),
            lax.psum(partials[3].astype(jnp.bfloat16), "head").astype(jnp.float32),
        )
        updated = []
        for index in range(4):
            gram = grams[index].astype(jnp.bfloat16)
            mix = (
                ns_b * gram.astype(jnp.float32)
                + ns_c * jnp.dot(gram, gram, preferred_element_type=jnp.float32)
            ).astype(jnp.bfloat16)
            if index == 1:
                product = jnp.dot(blocks[index], mix, preferred_element_type=jnp.float32)
            else:
                product = jnp.dot(mix, blocks[index], preferred_element_type=jnp.float32)
            updated.append(
                (ns_a * blocks[index].astype(jnp.float32) + product).astype(jnp.bfloat16)
            )
        blocks = updated
    share = up_weight.shape[1]
    offset = lax.axis_index("dp") * share
    owned = [
        blocks[0],
        blocks[1],
        lax.dynamic_slice_in_dim(blocks[2], offset, share, 1),
        lax.dynamic_slice_in_dim(blocks[3], offset, share, 1),
    ]
    weights = [qkv_weight, out_weight, up_weight, down_weight]
    factors = [
        math.sqrt(3.0),
        math.sqrt(SEQ / 8.0),
        math.sqrt(max(1.0, FF / width)),
        math.sqrt(max(1.0, FF / width)),
    ]
    new_weights = [
        weights[index] * (1.0 - muon_rate * muon_decay)
        - muon_rate * factors[index] * owned[index].astype(jnp.float32)
        for index in range(4)
    ]
    clipped = clip * vector_sum
    first_new = beta_one * norm_first + (1.0 - beta_one) * clipped
    second_new = beta_two * norm_second + (1.0 - beta_two) * clipped * clipped
    return (
        layer_out,
        input_grad,
        grad_norm,
        clipped,
        first_new,
        second_new,
        new_weights[0],
        new_moments[0],
        new_weights[1],
        new_moments[1],
        new_weights[2],
        new_moments[2],
        new_weights[3],
        new_moments[3],
    )


def solution(mesh):
    placed = (
        P(("dp", "head"), None),
        P("dp"),
        P(("dp", "head"), None),
        P(),
        P(),
        P(),
        P(None, "head"),
        P(None, "head"),
        P("head", None),
        P("head", None),
        P(None, ("dp", "head")),
        P(None, ("dp", "head")),
        P(None, ("dp", "head")),
        P(None, ("dp", "head")),
    )
    return jax.shard_map(
        shards,
        mesh=mesh,
        in_specs=placed,
        out_specs=(
            P(("dp", "head"), None),
            P(("dp", "head"), None),
            P(),
            P(),
            P(),
            P(),
            P(None, "head"),
            P(None, "head"),
            P("head", None),
            P("head", None),
            P(None, ("dp", "head")),
            P(None, ("dp", "head")),
            P(None, ("dp", "head")),
            P(None, ("dp", "head")),
        ),
        check_vma=False,
    )
```

profile of v0, /device:TPU:19, one launch (start us, length us, event | category | flops | bytes accessed | tf_op | source)
XLA Modules:
  0.0 1167.2 jit_solution(14758495943311568836)
XLA Ops:
  13.5 32.9 %all-gather.5.cloned.1.call-done = bf16[4096,512]{0,1:T(8,128)(2,1)} async-done(((bf16[1024,512]{0,1:T(8,128)(2,1)}), bf16[4096,512]{0,1:T(8,128)(2,1)}) %all-gather.5.cloned.1.call-update) | async-done | bytes 4194320 | tf_op jit(solution)/shard_map/all_gather | solution.py:126
  62.9 40.0 %while.22 = (s32[]{:T(128)}, bf16[8,512,2,64]{1,3,2,0:T(8,128)(2,1)}, f32[8,2,512,1]{2,1,3,0:T(2,128)}, bf16[8,512,2,64]{1,3,2,0:T(8,128)(2,1)}, s32[8,512]{1,0:...) while((s32[]{:T(128)}, ...), condition=%wide.region_5.6_spmd, body=%wide.region_2.5_spmd.sunk | while | flops 140835840 | bytes 7905881 | solution.py:135
  118.0 16.2 %all_gather.22 = bf16[512,512]{1,0:T(8,128)(2,1)} all-gather(bf16[128,512]{1,0:T(8,128)(2,1)S(1)} %convert_element_type.448), channel_id=1, replica_groups=mesh['dp'=8,'head'=4] {'head'}, dimensions={0}, use_global_device_ids=true | all-gather | bytes 655360 | tf_op jit(solution)/shard_map/all_gather | solution.py:138
  138.0 8.4 multiply_convert_fusion.2
  146.4 18.0 %all-gather.9.cloned.1.call-done = bf16[512,2048]{0,1:T(8,128)(2,1)} async-done(((bf16[512,64]{0,1:T(8,128)(2,1)}), bf16[512,2048]{0,1:T(8,128)(2,1)}) %all-gather.9.cloned.1.call-update) | async-done | bytes 2097168 | tf_op jit(solution)/shard_map/all_gather | solution.py:145
  164.4 8.4 multiply_convert_fusion.1
  195.0 9.4 all-to-all-done.1
  212.2 82.0 %while.23 = (s32[]{:T(128)}, bf16[8,512,2,3,64]{1,4,2,3,0:T(8,128)(2,1)}, bf16[8,512,2,64]{1,3,2,0:T(8,128)(2,1)}, s32[8,512]{1,0:T(8,128)}, bf16[8,512,2,64]{1,...) while((s32[]{:T(128)}, ...), condition=%wide.region_12.13_spmd, body=%wide.region_10.12_spmd.sunk | while | flops 342031360 | bytes 18380900 | solution.py:187
  304.9 7.3 fusion.263
  312.5 6.8 convolution_bitcast_fusion
  329.9 6.7 all-to-all-start.2
  336.6 39.4 %all-reduce.14.cloned.1.call-done = (bf16[128,512]{1,0:T(8,128)(2,1)}, bf16[512,384]{1,0:T(8,128)(2,1)}) async-done(((bf16[128,512]{1,0:T(8,128)(2,1)}, bf16[512,384]{1,0:T(8,128)(2,1)}), (bf16[128,512]{1,0:T(8,128)(2,1)}, bf16[512,384]{1,0:T(8,128)(2,1)})) %all-reduce.14.cloned.1.call-update) | async-done | bytes 524304 | tf_op jit(solution)/shard_map/psum | solution.py:203
  384.7 14.1 %all-gather.11.cloned.1.call-done = bf16[512,1536]{1,0:T(8,128)(2,1)} async-done(((bf16[512,384]{1,0:T(8,128)(2,1)}), bf16[512,1536]{1,0:T(8,128)(2,1)}) %all-gather.11.cloned.1.call-update) | async-done | bytes 1572880 | tf_op jit(solution)/shard_map/all_gather | solution.py:193
  411.4 100.7 %reduce-scatter.6.cloned.1.call-done = f32[512,64]{0,1:T(8,128)} async-done(((f32[512,2048]{0,1:T(8,128)}), f32[512,64]{0,1:T(8,128)}) %reduce-scatter.6.cloned.1.call-update) | async-done | bytes 131088 | tf_op jit(solution)/shard_map/reduce_scatter | solution.py:168
  513.7 137.7 %reduce-scatter.8.cloned.1.call-done = f32[512,64]{0,1:T(8,128)} async-done(((f32[512,2048]{0,1:T(8,128)}), f32[512,64]{0,1:T(8,128)}) %reduce-scatter.8.cloned.1.call-update) | async-done | bytes 131088 | tf_op jit(solution)/shard_map/reduce_scatter | solution.py:169
  658.2 67.2 %all-reduce = (f32[4,3]{1,0:T(4,128)S(1)}, f32[4,512]{1,0:T(4,128)}) all-reduce(f32[4,3]{1,0:T(4,128)} %pad_maximum_fusion.1, f32[4,512]{1,0:T(4,128)} %pad_maximum_fusion), channel_id=1, replica_groups=mesh['dp'=8,'head'=4] {'dp','head'}, use_global_device_ids=true, to_apply=%region_32.33 | all-reduce | flops 2060 | bytes 16480 | tf_op jit(solution)/shard_map/psum | solution.py:217
  735.6 21.2 %all_gather.27 = bf16[512,512]{0,1:T(8,128)(2,1)S(1)} all-gather(bf16[512,64]{0,1:T(8,128)(2,1)S(1)} %get-tuple-element.241), channel_id=1, replica_groups=mesh['dp'=8,'head'=4] {'dp'}, dimensions={1}, use_global_device_ids=true | all-gather | bytes 589824 | tf_op jit(solution)/shard_map/all_gather | solution.py:231
  759.5 25.2 %all_gather.26 = bf16[512,512]{0,1:T(8,128)(2,1)S(1)} all-gather(bf16[512,64]{0,1:T(8,128)(2,1)S(1)} %get-tuple-element.243), channel_id=1, replica_groups=mesh['dp'=8,'head'=4] {'dp'}, dimensions={1}, use_global_device_ids=true | all-gather | bytes 589824 | tf_op jit(solution)/shard_map/all_gather | solution.py:230
  790.0 67.9 %all-reduce.24.cloned.1.call-done = (bf16[512,512]{1,0:T(8,128)(2,1)}, bf16[512,512]{1,0:T(8,128)(2,1)}, bf16[512,512]{1,0:T(8,128)(2,1)}, bf16[512,512]{1,0:T(8,128)(2,1)}) async-done(((bf16[512,512]{1,0:T(8,128)(2,1)}, bf16[512,512]{1,0:T(8,128)(2,1)}, bf16[512,512]{1,0:T(8,128)(2,1)}, bf16[512,512]{1,0:T(8,128)(2,1)}), (bf16[512,512]{1,0:T(8,128)(2,1)}, bf16[512,512]{1,0:T(8,128)(2,1)}, ...) | async-done | bytes 2097168 | tf_op jit(solution)/shard_map/psum | solution.py:242
  877.1 52.1 %all-reduce.22.cloned.1.call-done = (bf16[512,512]{1,0:T(8,128)(2,1)}, bf16[512,512]{1,0:T(8,128)(2,1)}, bf16[512,512]{1,0:T(8,128)(2,1)}, bf16[512,512]{1,0:T(8,128)(2,1)}) async-done(((bf16[512,512]{1,0:T(8,128)(2,1)}, bf16[512,512]{1,0:T(8,128)(2,1)}, bf16[512,512]{1,0:T(8,128)(2,1)}, bf16[512,512]{1,0:T(8,128)(2,1)}), (bf16[512,512]{1,0:T(8,128)(2,1)}, bf16[512,512]{1,0:T(8,128)(2,1)}, ...) | async-done | bytes 2097168 | tf_op jit(solution)/shard_map/psum | solution.py:242
  951.4 52.1 %all-reduce.20.cloned.1.call-done = (bf16[512,512]{1,0:T(8,128)(2,1)}, bf16[512,512]{1,0:T(8,128)(2,1)}, bf16[512,512]{1,0:T(8,128)(2,1)}, bf16[512,512]{1,0:T(8,128)(2,1)}) async-done(((bf16[512,512]{1,0:T(8,128)(2,1)}, bf16[512,512]{1,0:T(8,128)(2,1)}, bf16[512,512]{1,0:T(8,128)(2,1)}, bf16[512,512]{1,0:T(8,128)(2,1)}), (bf16[512,512]{1,0:T(8,128)(2,1)}, bf16[512,512]{1,0:T(8,128)(2,1)}, ...) | async-done | bytes 2097168 | tf_op jit(solution)/shard_map/psum | solution.py:242
  1022.7 6.8 add_convert_fusion
  1032.4 42.2 %all-reduce.18.cloned.1.call-done = (bf16[512,512]{1,0:T(8,128)(2,1)}, bf16[512,512]{1,0:T(8,128)(2,1)}, bf16[512,512]{1,0:T(8,128)(2,1)}, bf16[512,512]{1,0:T(8,128)(2,1)}) async-done(((bf16[512,512]{1,0:T(8,128)(2,1)}, bf16[512,512]{1,0:T(8,128)(2,1)}, bf16[512,512]{1,0:T(8,128)(2,1)}, bf16[512,512]{1,0:T(8,128)(2,1)}), (bf16[512,512]{1,0:T(8,128)(2,1)}, bf16[512,512]{1,0:T(8,128)(2,1)}, ...) | async-done | bytes 2097168 | tf_op jit(solution)/shard_map/psum | solution.py:242
  1101.4 44.4 %all-reduce.16.cloned.1.call-done = (bf16[512,512]{1,0:T(8,128)(2,1)}, bf16[512,512]{1,0:T(8,128)(2,1)}, bf16[512,512]{1,0:T(8,128)(2,1)}, bf16[512,512]{1,0:T(8,128)(2,1)}) async-done(((bf16[512,512]{1,0:T(8,128)(2,1)}, bf16[512,512]{1,0:T(8,128)(2,1)}, bf16[512,512]{1,0:T(8,128)(2,1)}, bf16[512,512]{1,0:T(8,128)(2,1)}), (bf16[512,512]{1,0:T(8,128)(2,1)}, bf16[512,512]{1,0:T(8,128)(2,1)}, ...) | async-done | bytes 2097168 | tf_op jit(solution)/shard_map/psum | solution.py:242
  (378 shorter events, 361.6 us)
Async XLA Ops:
  7.2 39.3 %all-gather.5.cloned.1.call-start = ((), (), s32[]{:S(2)}) async-start(), calls=%async_computation.6 | async-start | bytes 5242880 | tf_op jit(solution)/shard_map/all_gather | solution.py:126
  11.3 126.3 %all-gather.7.cloned.1.call-start = ((), (), s32[]{:S(2)}) async-start(), calls=%async_computation.7 | async-start | bytes 2162688 | tf_op jit(solution)/shard_map/all_gather | solution.py:144
  12.0 152.4 %all-gather.9.cloned.1.call-start = ((), (), s32[]{:S(2)}) async-start(), calls=%async_computation.8 | async-start | bytes 2162688 | tf_op jit(solution)/shard_map/all_gather | solution.py:145
  12.8 39.8 %copy-start.10 = (bf16[512,384]{1,0:T(8,128)(2,1)}, bf16[512,384]{1,0:T(8,128)(2,1)S(1)}, u32[]{:S(2)}) copy-start(bf16[512,384]{1,0:T(8,128)(2,1)S(1)} %convert_element_type.446) | copy-start | bytes 1179652
  111.6 22.6 %all-to-all-start = ((bf16[4,1024,128]{1,2,0:T(8,128)(2,1)}), bf16[4,1024,128]{1,2,0:T(8,128)(2,1)S(1)}, u32[]{:S(2)}, u32[]{:S(2)}) async-start(bf16[4,1024,128]{1,2,0:T(8,128)(2,1)} %copy.81), calls=%async_computation | async-start | bytes 2097152 | tf_op jit(solution)/shard_map/all_to_all | solution.py:137
  137.3 42.7 %copy-start = (f32[1024,512]{0,1:T(8,128)}, f32[1024,512]{0,1:T(8,128)S(1)}, u32[]{:S(2)}) copy-start(f32[1024,512]{0,1:T(8,128)S(1)} %get-tuple-element.263) | copy-start | bytes 6291460
  187.1 17.3 %all-to-all-start.1 = ((bf16[1024,4,128]{0,2,1:T(8,128)(2,1)}), bf16[1024,4,128]{0,2,1:T(8,128)(2,1)}, u32[]{:S(2)}, u32[]{:S(2)}) async-start(bf16[1024,4,128]{0,2,1:T(8,128)(2,1)} %bitcast.284), calls=%async_computation.1 | async-start | bytes 2097152 | tf_op jit(solution)/shard_map/all_to_all | solution.py:179
  191.8 112.5 %reduce-scatter.4.cloned.1.call-start = ((), (), s32[]{:S(2)}) async-start(), calls=%async_computation.10 | async-start | bytes 655360 | tf_op jit(solution)/shard_map/reduce_scatter | solution.py:183
  194.6 181.5 %all-reduce.14.cloned.1.call-start = ((), (), s32[]{:S(2)}) async-start(), calls=%async_computation.13 | async-start | bytes 1048576 | tf_op jit(solution)/shard_map/psum | solution.py:203
  304.3 94.5 %all-gather.11.cloned.1.call-start = ((), (), s32[]{:S(2)}) async-start(), calls=%async_computation.9 | async-start | bytes 1966080 | tf_op jit(solution)/shard_map/all_gather | solution.py:193
  304.9 207.2 %reduce-scatter.6.cloned.1.call-start = ((), (), s32[]{:S(2)}) async-start(), calls=%async_computation.11 | async-start | bytes 4325376 | tf_op jit(solution)/shard_map/reduce_scatter | solution.py:168
  312.3 339.1 %reduce-scatter.8.cloned.1.call-start = ((), (), s32[]{:S(2)}) async-start(), calls=%async_computation.12 | async-start | bytes 4325376 | tf_op jit(solution)/shard_map/reduce_scatter | solution.py:169
  329.9 50.7 %copy-start.12 = (f32[128,512]{1,0:T(8,128)S(1)}, f32[128,512]{1,0:T(8,128)}, u32[]{:S(2)}) copy-start(f32[128,512]{1,0:T(8,128)} %param.27) | copy-start | bytes 786436
  329.9 68.9 %all-to-all-start.2 = ((bf16[4,1024,384]{1,2,0:T(8,128)(2,1)}), bf16[4,1024,384]{1,2,0:T(8,128)(2,1)}, u32[]{:S(2)}, u32[]{:S(2)}) async-start(bf16[4,1024,384]{1,2,0:T(8,128)(2,1)} %copy.91), calls=%async_computation.2 | async-start | bytes 6291456 | tf_op jit(solution)/shard_map/all_to_all | solution.py:192
  336.6 521.3 %all-reduce.24.cloned.1.call-start = ((), (), s32[]{:S(2)}) async-start(), calls=%async_computation.18 | async-start | bytes 4194304 | tf_op jit(solution)/shard_map/psum | solution.py:242
  407.8 322.7 %copy-start.8 = (bf16[512,384]{1,0:T(8,128)(2,1)S(1)}, bf16[512,384]{1,0:T(8,128)(2,1)}, u32[]{:S(2)}) copy-start(bf16[512,384]{1,0:T(8,128)(2,1)} %get-tuple-element.220) | copy-start | bytes 1179652
  756.8 30.5 %copy-start.32 = (f32[128,512]{1,0:T(8,128)S(1)}, f32[128,512]{1,0:T(8,128)}, u32[]{:S(2)}) copy-start(f32[128,512]{1,0:T(8,128)} %fusion.219) | copy-start | bytes 786436
  789.7 139.5 %all-reduce.22.cloned.1.call-start = ((), (), s32[]{:S(2)}) async-start(), calls=%async_computation.17 | async-start | bytes 4194304 | tf_op jit(solution)/shard_map/psum | solution.py:242
  877.0 126.5 %all-reduce.20.cloned.1.call-start = ((), (), s32[]{:S(2)}) async-start(), calls=%async_computation.16 | async-start | bytes 4194304 | tf_op jit(solution)/shard_map/psum | solution.py:242
  951.4 123.2 %all-reduce.18.cloned.1.call-start = ((), (), s32[]{:S(2)}) async-start(), calls=%async_computation.15 | async-start | bytes 4194304 | tf_op jit(solution)/shard_map/psum | solution.py:242
  1022.4 123.3 %all-reduce.16.cloned.1.call-start = ((), (), s32[]{:S(2)}) async-start(), calls=%async_computation.14 | async-start | bytes 4194304 | tf_op jit(solution)/shard_map/psum | solution.py:242
  1097.2 48.6 %copy-start.42 = (bf16[512,512]{0,1:T(8,128)(2,1)S(1)}, bf16[512,512]{0,1:T(8,128)(2,1)}, u32[]{:S(2)}) copy-start(bf16[512,512]{0,1:T(8,128)(2,1)} %fusion.103) | copy-start | bytes 1572868
  1100.1 48.8 %copy-start.43 = (bf16[512,512]{0,1:T(8,128)(2,1)S(1)}, bf16[512,512]{0,1:T(8,128)(2,1)}, u32[]{:S(2)}) copy-start(bf16[512,512]{0,1:T(8,128)(2,1)} %fusion.99) | copy-start | bytes 1572868
  1100.8 50.5 %copy-start.34 = (f32[4,512]{1,0:T(4,128)}, f32[4,512]{1,0:T(4,128)S(1)}, u32[]{:S(2)}) copy-start(f32[4,512]{1,0:T(4,128)S(1)} %get-tuple-element.246) | copy-start | bytes 24580
  (44 other events, 260.0 us)
Sparse Core Ops, SparseCore 0:
  11.4 35.0 all-gather.4
  49.9 55.6 all-gather.6
  109.0 55.2 all-gather.8
  195.4 21.7 reduce-scatter.3
  304.4 71.5 all-reduce.13
  378.1 20.7 all-gather.10
  401.1 110.9 reduce-scatter.5
  514.4 136.9 reduce-scatter.7
  789.9 67.9 all-reduce.23
  877.2 52.0 all-reduce.21
  951.5 52.0 all-reduce.19
  1022.5 52.0 all-reduce.17
  1093.7 52.0 all-reduce.15
where the time goes:
time: 1180 us; the launch traced here: 1170 us
  waiting for transfers between devices  612 us (52%)
  matrix products  239 us (20%)
  blocking collectives  130 us (11%)
  local copies, waits for them, and re-layouts  78.6 us (7%)
  other arithmetic  69.6 us (6%)
  between operations  20.1 us (2%)
  starting transfers between devices  17.9 us (2%)
    psum x5, waiting for transfers between devices, shards(): lax.psum(partials[0].astype(jnp.bfloat16), 'head').astype(jnp.float32)  259 us
    reduce_scatter x1, waiting for transfers between devices, shards(): lax.psum_scatter(down_grad, ('dp', 'head'), scatter_dimension=1, tiled=True)  138 us
    reduce_scatter x1, waiting for transfers between devices, shards(): lax.psum_scatter(up_grad, ('dp', 'head'), scatter_dimension=1, tiled=True)  101 us
    psum x1, blocking collectives, shards(): vector_sum, stat_sum = lax.psum((vector_part, stats), ('dp', 'head'))  67.2 us
    dot_general x15, matrix products, shards(): product = jnp.dot(mix, blocks[index], preferred_element_type=jnp.float32)  45.7 us
    psum x1, waiting for transfers between devices, shards(): lax.psum(out_part, 'dp').astype(jnp.float32)  39.4 us
    all_gather x1, waiting for transfers between devices, shards(): lax.all_gather(first.astype(jnp.bfloat16), 'head', axis=0, tiled=True)  32.9 us
    dot_general x15, matrix products, gram_left(): lax.dot_general(block, block, (((1,), (1,)), ((), ())), preferred_element...  29.8 us
  transfers between devices with their start and end apart: 16, of which 12 were waited for; matrix products, arithmetic and copies ran while one was open for 20% of the time, Pallas kernels for 0%

commit v1 on v0

v1 whole, which is shorter than its diff:
```python
import math

import jax
import jax.numpy as jnp
from jax import lax
from jax.experimental import pallas as pl
from jax.experimental.pallas import tpu as pltpu
from jax.sharding import PartitionSpec as P

HEAD_DIM = 64
FF = 2048
SEQ = 512
NS_STEPS = 5


neg_fill = -1000000000.0
norm_eps = 1e-05
ns_a = 3.4445
ns_b = -4.775
ns_c = 2.0315
momentum_decay = 0.95
muon_rate = 0.5
muon_decay = 0.01
beta_one = 0.9
beta_two = 0.95


def normalize(values, gain, shift):
    mean = jnp.mean(values, axis=-1, keepdims=True)
    centered = values - mean
    factor = lax.rsqrt(jnp.mean(centered * centered, axis=-1, keepdims=True) + norm_eps)
    plain = centered * factor
    return (plain * gain + shift, plain, factor)


def normalize_back(upper, plain, factor, gain):
    inner = upper * gain
    lower = factor * (
        inner
        - jnp.mean(inner, axis=-1, keepdims=True)
        - plain * jnp.mean(inner * plain, axis=-1, keepdims=True)
    )
    return (lower, jnp.sum(upper * plain, axis=0), jnp.sum(upper, axis=0))


def masked_scores(query, keys, segment):
    scores = jnp.einsum(
        "qhd,khd->hqk", query, keys, preferred_element_type=jnp.float32
    ) * HEAD_DIM ** (-0.5)
    same = segment[:, None] == segment[None, :]
    return jnp.where(same[None], scores, neg_fill)


def attend_forward(block):
    query, keys, values, segment = block
    scores = masked_scores(query, keys, segment)
    top = jnp.max(scores, axis=-1, keepdims=True)
    weights = jnp.exp(scores - top)
    total = jnp.sum(weights, axis=-1, keepdims=True)
    probs = (weights / total).astype(jnp.bfloat16)
    context = jnp.einsum("hqk,khd->qhd", probs, values, preferred_element_type=jnp.float32)
    return (context.astype(jnp.bfloat16), top + jnp.log(total))


def attend_backward(block):
    query, keys, values, segment, context_grad, lse = block
    scores = masked_scores(query, keys, segment)
    probs = jnp.exp(scores - lse)
    probs_low = probs.astype(jnp.bfloat16)
    probs_grad = jnp.einsum(
        "qhd,khd->hqk", context_grad, values, preferred_element_type=jnp.float32
    )
    inner = jnp.sum(probs * probs_grad, axis=-1, keepdims=True)
    score_grad = (probs * (probs_grad - inner)).astype(jnp.bfloat16)
    query_grad = jnp.einsum(
        "hqk,khd->qhd", score_grad, keys, preferred_element_type=jnp.float32
    ) * HEAD_DIM ** (-0.5)
    key_grad = jnp.einsum(
        "hqk,qhd->khd", score_grad, query, preferred_element_type=jnp.float32
    ) * HEAD_DIM ** (-0.5)
    value_grad = jnp.einsum(
        "hqk,qhd->khd", probs_low, context_grad, preferred_element_type=jnp.float32
    )
    return jnp.stack([query_grad, key_grad, value_grad], axis=2).astype(jnp.bfloat16)


def gram_left(block):
    return lax.dot_general(
        block, block, (((1,), (1,)), ((), ())), preferred_element_type=jnp.float32
    )


def gram_right(block):
    return lax.dot_general(
        block, block, (((0,), (0,)), ((), ())), preferred_element_type=jnp.float32
    )


def squares_of(moment, grad, weight):
    return (
        jnp.stack([jnp.sum(moment * moment), jnp.sum(moment * grad), jnp.sum(grad * grad)]) * weight
    )


COMM_ORDERS = ("cxylg", "cylgx", "clgxy")
WIDE = 2048


def coordinates():
    dp = lax.axis_index("dp")
    head = lax.axis_index("head")
    bits = {
        "c": head % 2,
        "x": head // 2,
        "y": dp % 2,
        "l": (dp // 2) % 2,
        "g": dp // 4,
    }
    steps = {"c": (0, 1), "x": (0, 2), "y": (1, 0), "l": (2, 0), "g": (4, 0)}
    peers = {}
    for name, (along_dp, along_head) in steps.items():
        turn = 1 - 2 * bits[name]
        peers[name] = (dp + along_dp * turn, head + along_head * turn)
    return dp, head, bits, peers


def remote(src, dst, send_sem, recv_sem, peer):
    return pltpu.make_async_remote_copy(
        src_ref=src,
        dst_ref=dst,
        send_sem=send_sem,
        recv_sem=recv_sem,
        device_id=peer,
        device_id_type=pl.DeviceIdType.MESH,
    )


def greet(head, dp, peers):
    barrier = pltpu.get_barrier_semaphore()
    across = (dp, 3 - head)
    everyone = list(peers.values()) + [across]
    for peer in everyone:
        pl.semaphore_signal(
            barrier, inc=1, device_id=peer, device_id_type=pl.DeviceIdType.MESH
        )
    pl.semaphore_wait(barrier, len(everyone))
    return across


def add_rows(dst, dst_at, one, one_at, two, two_at, count):
    def body(i, carry):
        here = pl.multiple_of(i * 16, 16)
        total = one[pl.ds(one_at + here, 16), :].astype(jnp.float32) + two[
            pl.ds(two_at + here, 16), :
        ].astype(jnp.float32)
        dst[pl.ds(dst_at + here, 16), :] = total.astype(jnp.bfloat16)
        return carry

    lax.fori_loop(0, count // 16, body, 0)


def update_kernel(
    a_ref, u_ref, d_ref, vec_ref, mom_ref,
    oq_ref, oo_ref, ou_ref, od_ref, gq_ref, go_ref, gu_ref, gd_ref, vsum_ref, scal_ref,
    got, acc, full, vgot, vnow, block, work, gram_ref, mix_ref,
    ssem, rsem, asem, bsem, vssem, vrsem, dssem, drsem,
):
    dp, head, bits, peers = coordinates()
    across = greet(head, dp, peers)
    sources = (a_ref, u_ref, d_ref)
    vnow[0] = vec_ref[...]
    spans = []
    for m in range(3):
        low = 0
        size = 512
        span = []
        for name in COMM_ORDERS[m]:
            size = size // 2
            keep = low + bits[name] * size
            give = low + (1 - bits[name]) * size
            span.append((name, size, keep, give))
            low = keep
        spans.append(span)
    for k in range(5):
        copies = []
        for m in range(3):
            name, size, keep, give = spans[m][k]
            place = 512 - 2 * size
            if k == 0:
                src = sources[m].at[pl.ds(pl.multiple_of(give, 16), size)]
            else:
                before = 512 - 4 * size
                src = acc.at[m, pl.ds(pl.multiple_of(before + (1 - bits[name]) * size, 16), size)]
            cp = remote(
                src, got.at[m, pl.ds(place, size)], ssem.at[m, k], rsem.at[m, k], peers[name]
            )
            cp.start()
            copies.append(cp)
        vcp = remote(vnow.at[k], vgot.at[k], vssem.at[k], vrsem.at[k], peers[COMM_ORDERS[0][k]])
        vcp.start()
        for m in range(3):
            name, size, keep, give = spans[m][k]
            place = 512 - 2 * size
            copies[m].wait()
            if k == 0:
                add_rows(acc.at[m], place, sources[m], pl.multiple_of(keep, 16), got.at[m], place, size)
            elif k < 4:
                before = 512 - 4 * size
                add_rows(
                    acc.at[m], place, acc.at[m],
                    pl.multiple_of(before + bits[name] * size, 16), got.at[m], place, size,
                )
            else:
                before = 512 - 4 * size
                add_rows(
                    full.at[m], pl.multiple_of(keep, 16), acc.at[m],
                    pl.multiple_of(before + bits[name] * size, 16), got.at[m], place, size,
                )
        vcp.wait()
        vnow[k + 1] = vnow[k] + vgot[k]
    for k in reversed(range(5)):
        copies = []
        for m in range(3):
            name, size, keep, give = spans[m][k]
            mine = full.at[m, pl.ds(pl.multiple_of(keep, 16), size)]
            cp = remote(mine, mine, asem.at[m, k], bsem.at[m, k], peers[name])
            cp.start()
            copies.append(cp)
        for cp in copies:
            cp.wait()
    vsum_ref[...] = vnow[5]
    chunk = 16

    def square_body(i, sums):
        here = pl.multiple_of(i * chunk, chunk)
        out = sums
        for m in range(3):
            part = full[m, pl.ds(here, chunk), :].astype(jnp.float32)
            out = out + jnp.sum(part * part, axis=0, keepdims=True)
        return out

    sums = lax.fori_loop(0, 512 // chunk, square_body, jnp.zeros((1, WIDE), jnp.float32))
    total = jnp.sum(sums, axis=1, keepdims=True)
    vector = vnow[5]
    total = total + jnp.sum(
        jnp.sum(vector * vector, axis=0, keepdims=True), axis=1, keepdims=True
    )
    norm = jnp.sqrt(total)
    clip = jnp.minimum(1.0, 1.0 / (norm + 1e-06))
    lane = lax.broadcasted_iota(jnp.int32, (8, 128), 1)
    scal_ref[...] = jnp.where(lane == 0, norm, clip)
    which = jnp.maximum(head - 1, 0)
    columns = lax.broadcasted_iota(jnp.int32, (chunk, WIDE), 1)
    first_column = jnp.where(head == 1, 1536, 0)
    past_column = jnp.where(head == 0, 1536, WIDE)
    inside = (columns >= first_column) & (columns < past_column)

    def moment_body(i, sums):
        here = pl.multiple_of(i * chunk, chunk)
        grad = full[which, pl.ds(here, chunk), :].astype(jnp.float32)
        grad = jnp.where(inside, grad, 0.0)
        moment = momentum_decay * mom_ref[pl.ds(here, chunk), :].astype(jnp.float32) + clip * grad
        work[pl.ds(here, chunk), :] = moment
        return sums + jnp.sum(moment * moment, axis=0, keepdims=True)

    sums = lax.fori_loop(0, 512 // chunk, moment_body, jnp.zeros((1, WIDE), jnp.float32))
    scale = 1.0 / (jnp.sqrt(jnp.sum(sums, axis=1, keepdims=True)) + 1e-07)

    def start_body(i, carry):
        here = pl.multiple_of(i * chunk, chunk)
        block[0, pl.ds(here, chunk), :] = (work[pl.ds(here, chunk), :] * scale).astype(jnp.bfloat16)
        return carry

    lax.fori_loop(0, 512 // chunk, start_body, 0)
    own = (gq_ref, go_ref, gu_ref, gd_ref)
    gq_ref[...] = full[0, :, pl.ds(pl.multiple_of(head * 384, 128), 384)]
    go_ref[...] = full[0, :, pl.ds(pl.multiple_of(1536 + head * 128, 128), 128)]
    pair = pl.multiple_of((dp * 2 + bits["x"]) * 128, 128)
    gu_ref[...] = full[1, :, pl.ds(pair, 128)]
    gd_ref[...] = full[2, :, pl.ds(pair, 128)]
    tile = 256

    def turn_body(turn, carry):
        now = turn % 2
        later = 1 - now

        def gram_body(i, c):
            rows = pl.ds(pl.multiple_of(i * tile, tile), tile)
            gram_ref[rows, :] = lax.dot_general(
                block[now, rows, :], block[now], (((1,), (1,)), ((), ())),
                preferred_element_type=jnp.float32,
            ).astype(jnp.bfloat16)
            return c

        lax.fori_loop(0, 512 // tile, gram_body, 0)

        def mix_body(i, c):
            rows = pl.ds(pl.multiple_of(i * tile, tile), tile)
            mine = gram_ref[rows, :]
            mix_ref[rows, :] = (
                ns_b * mine.astype(jnp.float32)
                + ns_c * jnp.dot(mine, gram_ref[...], preferred_element_type=jnp.float32)
            ).astype(jnp.bfloat16)
            return c

        lax.fori_loop(0, 512 // tile, mix_body, 0)

        def next_body(i, c):
            cols = pl.ds(pl.multiple_of(i * 512, 512), 512)
            block[later, :, cols] = (
                ns_a * block[now, :, cols].astype(jnp.float32)
                + jnp.dot(mix_ref[...], block[now, :, cols], preferred_element_type=jnp.float32)
            ).astype(jnp.bfloat16)
            return c

        lax.fori_loop(0, WIDE // 512, next_body, 0)
        return carry

    lax.fori_loop(0, NS_STEPS, turn_body, 0)
    last = NS_STEPS % 2
    outs = (oq_ref, oo_ref, ou_ref, od_ref)

    def piece(kind, who):
        if kind == 0:
            return block.at[last, :, pl.ds(pl.multiple_of(who * 384, 128), 384)]
        if kind == 1:
            return block.at[last, :, pl.ds(pl.multiple_of(1536 + who * 128, 128), 128)]
        return block.at[last, :, pl.ds(pl.multiple_of((dp * 2 + who // 2) * 128, 128), 128)]

    partners = (peers["c"], peers["x"], across)
    for kind in range(4):
        @pl.when(head == kind)
        def _(kind=kind):
            copies = []
            for j, partner in enumerate(partners):
                cp = remote(
                    piece(kind, partner[1]), outs[kind], dssem.at[j], drsem.at[kind], partner
                )
                cp.start()
                copies.append(cp)
            outs[kind][...] = piece(kind, head)[...]
            for cp in copies:
                cp.wait_send()

    for kind in range(4):
        @pl.when(head != kind)
        def _(kind=kind):
            remote(
                piece(kind, head), outs[kind], dssem.at[0], drsem.at[kind], partners[0]
            ).wait_recv()


def update_call(a, u, d, vec, mom):
    low = jnp.bfloat16
    shape = jax.ShapeDtypeStruct
    vmem = pl.BlockSpec(memory_space=pltpu.VMEM)
    return pl.pallas_call(
        update_kernel,
        out_shape=(
            shape((512, 384), low), shape((512, 128), low), shape((512, 128), low), shape((512, 128), low),
            shape((512, 384), low), shape((512, 128), low), shape((512, 128), low), shape((512, 128), low),
            shape((4, 512), jnp.float32), shape((8, 128), jnp.float32),
        ),
        in_specs=[vmem] * 5,
        out_specs=(vmem,) * 10,
        scratch_shapes=[
            pltpu.VMEM((3, 512, WIDE), low),
            pltpu.VMEM((3, 512, WIDE), low),
            pltpu.VMEM((3, 512, WIDE), low),
            pltpu.VMEM((5, 4, 512), jnp.float32),
            pltpu.VMEM((6, 4, 512), jnp.float32),
            pltpu.VMEM((2, 512, WIDE), low),
            pltpu.VMEM((512, WIDE), jnp.float32),
            pltpu.VMEM((512, 512), low),
            pltpu.VMEM((512, 512), low),
            pltpu.SemaphoreType.DMA((3, 5)),
            pltpu.SemaphoreType.DMA((3, 5)),
            pltpu.SemaphoreType.DMA((3, 5)),
            pltpu.SemaphoreType.DMA((3, 5)),
            pltpu.SemaphoreType.DMA((5,)),
            pltpu.SemaphoreType.DMA((5,)),
            pltpu.SemaphoreType.DMA((3,)),
            pltpu.SemaphoreType.DMA((4,)),
        ],
        compiler_params=pltpu.CompilerParams(
            collective_id=1, has_side_effects=True, vmem_limit_bytes=60 << 20
        ),
        name="update",
    )(a, u, d, vec, mom)


def general_update(
    whole_qkv, whole_out, up_grad, down_grad, vector_part,
    qkv_moment, out_moment, up_moment, down_moment,
):
    everywhere = ("dp", "head")
    narrow = out_moment.shape[0]
    up_part, down_part = (
        lax.psum_scatter(
            up_grad.astype(jnp.bfloat16), everywhere, scatter_dimension=1, tiled=True
        ).astype(jnp.float32),
        lax.psum_scatter(
            down_grad.astype(jnp.bfloat16), everywhere, scatter_dimension=1, tiled=True
        ).astype(jnp.float32),
    )
    qkv_part = lax.psum_scatter(
        whole_qkv.astype(jnp.bfloat16), "head", scatter_dimension=1, tiled=True
    )
    out_part = lax.psum_scatter(
        whole_out.astype(jnp.bfloat16), "head", scatter_dimension=0, tiled=True
    )
    qkv_sum, out_sum = (
        lax.psum(qkv_part, "dp").astype(jnp.float32),
        lax.psum(out_part, "dp").astype(jnp.float32),
    )
    leading = (lax.axis_index("dp") == 0).astype(jnp.float32)
    moments = [qkv_moment, out_moment, up_moment, down_moment]
    grads = [qkv_sum, out_sum, up_part, down_part]
    stats = jnp.stack(
        [
            squares_of(qkv_moment, qkv_sum, leading),
            squares_of(out_moment, out_sum, leading),
            squares_of(up_moment, up_part, 1.0),
            squares_of(down_moment, down_part, 1.0),
        ]
    )
    vector_sum, stat_sum = lax.psum((vector_part, stats), everywhere)
    grad_norm = jnp.sqrt(jnp.sum(stat_sum[:, 2]) + jnp.sum(vector_sum * vector_sum))
    clip = jnp.minimum(1.0, 1.0 / (grad_norm + 1e-06))
    sizes = jnp.sqrt(
        momentum_decay * momentum_decay * stat_sum[:, 0]
        + 2.0 * momentum_decay * clip * stat_sum[:, 1]
        + clip * clip * stat_sum[:, 2]
    )
    new_moments = [momentum_decay * moments[index] + clip * grads[index] for index in range(4)]
    starts = [
        (new_moments[index] / (sizes[index] + 1e-07)).astype(jnp.bfloat16) for index in range(4)
    ]
    blocks = [
        lax.all_gather(starts[0], "head", axis=1, tiled=True),
        lax.all_gather(starts[1], "head", axis=0, tiled=True),
        lax.all_gather(starts[2], everywhere, axis=1, tiled=True),
        lax.all_gather(starts[3], everywhere, axis=1, tiled=True),
    ]
    for turn in range(NS_STEPS):
        updated = []
        for index in range(4):
            form = gram_right if index == 1 else gram_left
            gram = form(blocks[index]).astype(jnp.bfloat16)
            mix = (
                ns_b * gram.astype(jnp.float32)
                + ns_c * jnp.dot(gram, gram, preferred_element_type=jnp.float32)
            ).astype(jnp.bfloat16)
            if index == 1:
                product = jnp.dot(blocks[index], mix, preferred_element_type=jnp.float32)
            else:
                product = jnp.dot(mix, blocks[index], preferred_element_type=jnp.float32)
            updated.append(
                (ns_a * blocks[index].astype(jnp.float32) + product).astype(jnp.bfloat16)
            )
        blocks = updated
    share = up_moment.shape[1]
    along = lax.axis_index("head")
    offset = (lax.axis_index("dp") * lax.axis_size("head") + along) * share
    owned = [
        lax.dynamic_slice_in_dim(blocks[0], along * qkv_moment.shape[1], qkv_moment.shape[1], 1),
        lax.dynamic_slice_in_dim(blocks[1], along * narrow, narrow, 0),
        lax.dynamic_slice_in_dim(blocks[2], offset, share, 1),
        lax.dynamic_slice_in_dim(blocks[3], offset, share, 1),
    ]
    return (owned, new_moments, vector_sum, grad_norm, clip)


def shards(
    tokens,
    segments,
    out_grad,
    norm_params,
    norm_first,
    norm_second,
    qkv_weight,
    qkv_moment,
    out_weight,
    out_moment,
    up_weight,
    up_moment,
    down_weight,
    down_moment,
):
    width = tokens.shape[1]
    rows = tokens.shape[0]
    narrow = out_weight.shape[0]
    sequences = rows // SEQ
    heads = width // HEAD_DIM
    everywhere = ("dp", "head")
    inputs = tokens.astype(jnp.float32)
    first, first_plain, first_factor = normalize(inputs, norm_params[0], norm_params[1])
    first_low = first.astype(jnp.bfloat16)
    qkv_full = lax.all_gather(qkv_weight.astype(jnp.bfloat16), "head", axis=1, tiled=True)
    out_full = lax.all_gather(out_weight.astype(jnp.bfloat16), "head", axis=0, tiled=True)
    up_all = lax.all_gather(up_weight.astype(jnp.bfloat16), everywhere, axis=1, tiled=True)
    down_all = lax.all_gather(down_weight.astype(jnp.bfloat16), everywhere, axis=1, tiled=True)
    mixed = jnp.dot(first_low, qkv_full, preferred_element_type=jnp.float32).astype(jnp.bfloat16)
    mixed = mixed.reshape(sequences, SEQ, heads, 3, HEAD_DIM)
    segment_rows = lax.dynamic_slice_in_dim(segments, lax.axis_index("head") * rows, rows, 0)
    segment_rows = segment_rows.reshape(sequences, SEQ)
    query = mixed[:, :, :, 0]
    keys = mixed[:, :, :, 1]
    values = mixed[:, :, :, 2]
    context, lse = lax.map(attend_forward, (query, keys, values, segment_rows))
    context = context.reshape(rows, width)
    attended = jnp.dot(context, out_full, preferred_element_type=jnp.float32)
    middle = inputs + attended
    second, second_plain, second_factor = normalize(middle, norm_params[2], norm_params[3])
    second_low = second.astype(jnp.bfloat16)
    hidden = jnp.dot(second_low, up_all, preferred_element_type=jnp.float32)
    switch = jax.nn.sigmoid(1.702 * hidden)
    active = (hidden * switch).astype(jnp.bfloat16)
    result = middle + lax.dot_general(
        active, down_all, (((1,), (1,)), ((), ())), preferred_element_type=jnp.float32
    )
    layer_out = result.astype(jnp.bfloat16)
    down_grad = lax.dot_general(
        out_grad, active, (((0,), (0,)), ((), ())), preferred_element_type=jnp.float32
    )
    active_grad = jnp.dot(out_grad, down_all, preferred_element_type=jnp.float32)
    hidden_grad = (active_grad * (switch + 1.702 * hidden * switch * (1.0 - switch))).astype(
        jnp.bfloat16
    )
    up_grad = lax.dot_general(
        second_low, hidden_grad, (((0,), (0,)), ((), ())), preferred_element_type=jnp.float32
    )
    second_grad = lax.dot_general(
        hidden_grad, up_all, (((1,), (1,)), ((), ())), preferred_element_type=jnp.float32
    )
    middle_lower, gain_two, shift_two = normalize_back(
        second_grad, second_plain, second_factor, norm_params[2]
    )
    middle_grad = out_grad.astype(jnp.float32) + middle_lower
    attended_low = middle_grad.astype(jnp.bfloat16)
    context_grad = lax.dot_general(
        attended_low, out_full, (((1,), (1,)), ((), ())), preferred_element_type=jnp.float32
    ).astype(jnp.bfloat16)
    whole_out = lax.dot_general(
        context, attended_low, (((0,), (0,)), ((), ())), preferred_element_type=jnp.float32
    )
    context_grad = context_grad.reshape(sequences, SEQ, heads, HEAD_DIM)
    mixed_grad = lax.map(attend_backward, (query, keys, values, segment_rows, context_grad, lse))
    mixed_grad = mixed_grad.reshape(rows, 3 * width)
    whole_qkv = lax.dot_general(
        first_low, mixed_grad, (((0,), (0,)), ((), ())), preferred_element_type=jnp.float32
    )
    first_grad = lax.dot_general(
        mixed_grad, qkv_full, (((1,), (1,)), ((), ())), preferred_element_type=jnp.float32
    )
    input_lower, gain_one, shift_one = normalize_back(
        first_grad, first_plain, first_factor, norm_params[0]
    )
    input_grad = middle_grad + input_lower
    vector_part = jnp.stack([gain_one, shift_one, gain_two, shift_two])
    fast = lax.axis_size("dp") == 8 and lax.axis_size("head") == 4
    if fast:
        out_t = lax.dot_general(
            attended_low, context, (((0,), (0,)), ((), ())), preferred_element_type=jnp.float32
        )
        both = jnp.concatenate([whole_qkv, out_t], axis=1).astype(jnp.bfloat16)
        along = lax.axis_index("head")
        low_m = [m.astype(jnp.bfloat16) for m in (qkv_moment, out_moment.T, up_moment, down_moment)]
        mq = lax.all_gather(low_m[0], "head", axis=1, tiled=True)
        mo = lax.all_gather(low_m[1], "head", axis=1, tiled=True)
        mu = lax.all_gather(low_m[2], everywhere, axis=1, tiled=True)
        md = lax.all_gather(low_m[3], everywhere, axis=1, tiled=True)
        mom = lax.select_n(
            along,
            jnp.pad(mq, ((0, 0), (0, 512))),
            jnp.pad(mo, ((0, 0), (1536, 0))),
            mu,
            md,
        )
        (oq, oo, ou, od, gq, go, gu, gd, vector_sum, scalars) = update_call(
            both, up_grad.astype(jnp.bfloat16), down_grad.astype(jnp.bfloat16), vector_part, mom
        )
        grad_norm = scalars[0, 0]
        clip = scalars[0, 1]
        half = (along % 2) * 64
        cut = lambda v: lax.dynamic_slice_in_dim(v, half, 64, 1)
        owned = [oq, oo.T, cut(ou), cut(od)]
        grads = [gq, go.T, cut(gu), cut(gd)]
        moments = [qkv_moment, out_moment, up_moment, down_moment]
        new_moments = [
            momentum_decay * moments[index] + clip * grads[index].astype(jnp.float32)
            for index in range(4)
        ]
    else:
        (owned, new_moments, vector_sum, grad_norm, clip) = general_update(
            whole_qkv, whole_out, up_grad, down_grad, vector_part,
            qkv_moment, out_moment, up_moment, down_moment,
        )
    weights = [qkv_weight, out_weight, up_weight, down_weight]
    factors = [
        math.sqrt(3.0),
        math.sqrt(SEQ / 8.0),
        math.sqrt(max(1.0, FF / width)),
        math.sqrt(max(1.0, FF / width)),
    ]
    new_weights = [
        weights[index] * (1.0 - muon_rate * muon_decay)
        - muon_rate * factors[index] * owned[index].astype(jnp.float32)
        for index in range(4)
    ]
    clipped = clip * vector_sum
    first_new = beta_one * norm_first + (1.0 - beta_one) * clipped
    second_new = beta_two * norm_second + (1.0 - beta_two) * clipped * clipped
    return (
        layer_out,
        input_grad,
        grad_norm,
        clipped,
        first_new,
        second_new,
        new_weights[0],
        new_moments[0],
        new_weights[1],
        new_moments[1],
        new_weights[2],
        new_moments[2],
        new_weights[3],
        new_moments[3],
    )


def solution(mesh):
    placed = (
        P(("dp", "head"), None),
        P("dp"),
        P(("dp", "head"), None),
        P(),
        P(),
        P(),
        P(None, "head"),
        P(None, "head"),
        P("head", None),
        P("head", None),
        P(None, ("dp", "head")),
        P(None, ("dp", "head")),
        P(None, ("dp", "head")),
        P(None, ("dp", "head")),
    )
    return jax.shard_map(
        shards,
        mesh=mesh,
        in_specs=placed,
        out_specs=(
            P(("dp", "head"), None),
            P(("dp", "head"), None),
            P(),
            P(),
            P(),
            P(),
            P(None, "head"),
            P(None, "head"),
            P("head", None),
            P("head", None),
            P(None, ("dp", "head")),
            P(None, ("dp", "head")),
            P(None, ("dp", "head")),
            P(None, ("dp", "head")),
        ),
        check_vma=False,
    )
```

time: 1180 us -> 477 us (0.40)
  waiting for transfers between devices: 612 us -> 97.6 us
  matrix products: 239 us -> 75.4 us
  Pallas kernels: 0 us -> 131 us
  blocking collectives: 130 us -> 19 us
  other arithmetic: 69.6 us -> 50.7 us
  starting transfers between devices: 17.9 us -> 0.25 us
    psum x6 -> x0, waiting for transfers between devices: 298 us -> none  [the longest x5 259 us: shards(): lax.psum(partials[0].astype(jnp.bfloat16), 'head').astype(jnp.float32)]
    reduce_scatter x3 -> x0, waiting for transfers between devices: 238 us -> none  [the longest x1 138 us: shards(): lax.psum_scatter(down_grad, ('dp', 'head'), scatter_dimension=1, tiled=True)]
    pallas_call x0 -> x1, Pallas kernels: none -> 131 us  [update_call(): pl.pallas_call(update_kernel, out_shape=(shape((512, 384), low), shape((5...]
    dot_general x45 -> x5, matrix products: 114 us -> 13 us  [the longest x1 5.08 us: shards(): jnp.dot(first_low, qkv_full, preferred_element_type=jnp.float32)]
    psum x1 -> x0, blocking collectives: 67.2 us -> none  [shards(): vector_sum, stat_sum = lax.psum((vector_part, stats), ('dp', 'head'))]
    all_gather x3 -> x2, blocking collectives: 62.7 us -> 19 us  [the longest x1 11.3 us: shards(): lax.all_gather(out_weight.astype(jnp.bfloat16), 'head', axis=0, tiled=True)]
    all_gather x4 -> x6, waiting for transfers between devices: 65 us -> 97.5 us  [the longest x1 47.9 us: shards(): lax.all_gather(down_weight.astype(jnp.bfloat16), everywhere, axis=1, tile...]
    all_to_all x5 -> x0, local copies, waits for them, and re-layouts: 18.7 us -> none  [the longest x2 10.6 us: shards(): lax.all_to_all(mixed_grad, 'head', split_axis=0, concat_axis=1, tiled=True)]
  transfers between devices with their start and end apart: 16 -> 6, of which waited for: 12 -> 4; matrix products, arithmetic and copies ran while one was open for 20% -> 32% of each run, Pallas kernels for 0% -> 0%
where the time goes in v1:
time: 477 us; the launch traced here: 467 us
  Pallas kernels  131 us (27%)
  waiting for transfers between devices  97.6 us (20%)
  local copies, waits for them, and re-layouts  77 us (16%)
  matrix products  75.4 us (16%)
  other arithmetic  50.7 us (11%)
  blocking collectives  19 us (4%)
  between operations  15.2 us (3%)
    pallas_call x1, Pallas kernels, update_call(): pl.pallas_call(update_kernel, out_shape=(shape((512, 384), low), shape((5...  131 us
    all_gather x1, waiting for transfers between devices, shards(): lax.all_gather(down_weight.astype(jnp.bfloat16), everywhere, axis=1, tile...  47.9 us
    all_gather x1, waiting for transfers between devices, shards(): md = lax.all_gather(low_m[3], everywhere, axis=1, tiled=True)  37 us
    unnamed x126, local copies, waits for them, and re-layouts  27.2 us
    all_gather x1, blocking collectives, shards(): lax.all_gather(out_weight.astype(jnp.bfloat16), 'head', axis=0, tiled=True)  11.3 us
    dot_general x1, matrix products, shards(): hidden = jnp.dot(second_low, up_all, preferred_element_type=jnp.float32)  10.8 us
  transfers between devices with their start and end apart: 6, of which 4 were waited for; matrix products, arithmetic and copies ran while one was open for 32% of the time, Pallas kernels for 0%

profile of v1, /device:TPU:19, one launch (start us, length us, event | category | flops | bytes accessed | tf_op | source)
XLA Modules:
  0.0 467.4 jit_solution(16079631048003858624)
XLA Ops:
  20.1 11.3 %all_gather.25 = bf16[512,512]{1,0:T(8,128)(2,1)} all-gather(bf16[128,512]{1,0:T(8,128)(2,1)S(1)} %convert_element_type.123), channel_id=1, replica_groups=mesh['dp'=8,'head'=4] {'head'}, dimensions={0}, use_global_device_ids=true | all-gather | bytes 655360 | tf_op jit(solution)/shard_map/all_gather | solution.py:500
  31.3 7.7 %all_gather.29 = bf16[512,512]{1,0:T(8,128)(2,1)} all-gather(bf16[512,128]{1,0:T(8,128)(2,1)S(1)} %convert_bitcast_fusion), channel_id=1, replica_groups=mesh['dp'=8,'head'=4] {'head'}, dimensions={1}, use_global_device_ids=true | all-gather | bytes 655360 | tf_op jit(solution)/shard_map/all_gather | solution.py:570
  42.6 5.1 %convolution_convert_fusion = bf16[1024,1536]{1,0:T(8,128)(2,1)} fusion(bf16[512,1536]{1,0:T(8,128)(2,1)} %all-gather.7.cloned.1.call-done, bf16[1024,512]{0,1:T(8,128)(2,1)S(1)} %copy.107, f32[512]{0:T(512)S(1)} %bitcast.175, f32[512]{0:T(512)S(1)} %bitcast.167, f32[1024]{0:T(1024)S(1)} %add_rsqrt_fusion.1, f32[1024]{0:T(1024)S(1)} %broadcast_multiply_fusion.6), kind=kOutput, calls=%fused_computation.67 | convolution fusion | flops 1615331328 | bytes 5779456 | tf_op jit(solution)/shard_map/dot_general | solution.py:503
  47.6 4.6 copy.108
  52.3 6.2 %reshape.217 = bf16[2,512,8,3,64]{1,0,4,3,2:T(2,128)(2,1)} reshape(bf16[1024,1536]{0,1:T(8,128)(2,1)} %copy.108) | data formatting | bytes 6291456 | tf_op jit(solution)/shard_map/reshape | solution.py:504
  58.4 3.6 slice_bitcast_fusion
  63.6 14.4 %while.22 = (s32[]{:T(128)}, bf16[2,512,8,64]{1,3,2,0:T(8,128)(2,1)}, f32[2,8,512,1]{2,1,3,0:T(8,128)S(1)}, bf16[2,512,8,64]{1,3,2,0:T(8,128)(2,1)}, s32[2,512]{...) while((s32[]{:T(128)}, ...), condition=%wide.region_5.6_spmd, body=%wide.region_2.5_spmd.sunk | while | flops 562556928 | bytes 41033912 | solution.py:510
  83.3 9.1 %all-gather.9.cloned.1.call-done = bf16[512,2048]{0,1:T(8,128)(2,1)} async-done(((bf16[512,64]{0,1:T(8,128)(2,1)}), bf16[512,2048]{0,1:T(8,128)(2,1)}) %all-gather.9.cloned.1.call-update) | async-done | bytes 2097168 | tf_op jit(solution)/shard_map/all_gather | solution.py:501
  92.4 10.8 %multiply_convert_fusion.2 = (bf16[1024,2048]{1,0:T(8,128)(2,1)}, f32[1024,2048]{1,0:T(8,128)}) fusion(bf16[512,2048]{0,1:T(8,128)(2,1)} %all-gather.9.cloned.1.call-done, f32[1024,512]{0,1:T(8,128)} %copy-done.4, f32[512]{0:T(512)S(1)} %bitcast.173, f32[512]{0:T(512)S(1)} %bitcast.163, f32[1024]{0:T(1024)S(1)} %add_rsqrt_fusion, ...), kind=kOutput, calls=%fused_computation.65 | convolution fusion | flops 2162688000 | bytes 16789504 | tf_op jit(solution)/shard_map/dot_general | solution.py:516
  103.1 47.9 %all-gather.11.cloned.1.call-done = bf16[512,2048]{0,1:T(8,128)(2,1)} async-done(((bf16[512,64]{0,1:T(8,128)(2,1)}), bf16[512,2048]{0,1:T(8,128)(2,1)}) %all-gather.11.cloned.1.call-update) | async-done | bytes 2097168 | tf_op jit(solution)/shard_map/all_gather | solution.py:502
  151.1 6.8 %add_convert_fusion = bf16[1024,512]{0,1:T(8,128)(2,1)} fusion(f32[1024,512]{0,1:T(8,128)} %copy-done.4, bf16[1024,2048]{1,0:T(8,128)(2,1)} %get-tuple-element.250, bf16[512,2048]{0,1:T(8,128)(2,1)} %all-gather.11.cloned.1.call-done), kind=kOutput, calls=%fused_computation.94 | convolution fusion | flops 2148532224 | bytes 9437184 | tf_op jit(solution)/shard_map/dot_general | solution.py:519
  160.3 7.2 %multiply_convert_fusion.1 = bf16[1024,2048]{1,0:T(8,128)(2,1)S(1)} fusion(f32[1024,2048]{1,0:T(8,128)} %get-tuple-element.251, bf16[1024,512]{1,0:T(8,128)(2,1)S(1)} %copy-done.26, bf16[512,2048]{0,1:T(8,128)(2,1)} %all-gather.11.cloned.1.call-done), kind=kOutput, calls=%fused_computation.64 | convolution fusion | flops 2168455168 | bytes 15728640 | tf_op jit(solution)/shard_map/dot_general | solution.py:526
  167.5 3.7 fusion.78
  185.1 28.5 %while.23 = (s32[]{:T(128)}, bf16[2,512,8,3,64]{1,4,2,3,0:T(8,128)(2,1)}, bf16[2,512,8,64]{1,3,2,0:T(8,128)(2,1)S(1)}, s32[2,512]{1,0:T(2,128)S(1)}, bf16[2,512,...) while((s32[]{:T(128)}, ...), condition=%wide.region_12.13_spmd, body=%wide.region_10.12_spmd.sunk | while | flops 1379921920 | bytes 101834952 | solution.py:548
  213.6 5.1 %copy.121 = bf16[2,512,8,3,64]{1,0,4,3,2:T(2,128)(2,1)S(1)} copy(bf16[2,512,8,3,64]{1,4,2,3,0:T(8,128)(2,1)} %get-tuple-element.106) | data formatting | bytes 6291456 | tf_op jit(solution)/shard_map/while | solution.py:548
  227.3 4.0 copy.128
  231.2 37.0 %all-gather.17.cloned.1.call-done = bf16[512,2048]{0,1:T(8,128)(2,1)} async-done(((bf16[512,64]{0,1:T(8,128)(2,1)}), bf16[512,2048]{0,1:T(8,128)(2,1)}) %all-gather.17.cloned.1.call-update) | async-done | bytes 2097168 | tf_op jit(solution)/shard_map/all_gather | solution.py:572
  268.2 4.2 copy.129
  278.2 3.8 fusion.54.d_ref
  282.1 3.8 convolution_convert_fusion.2.u_ref
  285.9 3.5 all-gather.13.cloned.1.call-done
  289.4 4.8 %select_select_fusion.mom_ref = bf16[512,2048]{1,0:T(8,128)(2,1)} fusion(bf16[512,2048]{1,0:T(8,128)(2,1)} %copy.128, bf16[512,2048]{1,0:T(8,128)(2,1)} %copy.129, bf16[512,512]{1,0:T(8,128)(2,1)} %all_gather.29, bf16[512,1536]{1,0:T(8,128)(2,1)} %all-gather.13.cloned.1.call-done, pred[]{:T(512)S(6)} %select_n.56, pred[]{:T(512)S(6)} %select_n.53, ...), kind=kLoop, calls=%fused_computation.90 | loop fusion | flops 3145728 | bytes 8388611 | tf_op jit(solution)/shard_map/select_n | solution.py:573
  294.2 131.4 %update.1 = (bf16[512,384]{1,0:T(8,128)(2,1)}, bf16[512,128]{1,0:T(8,128)(2,1)}, bf16[512,128]{1,0:T(8,128)(2,1)}, bf16[512,128]{1,0:T(8,128)(2,1)}, bf16[512,38...) custom-call(bf16[512,2048]{1,0:T(8,128)(2,1)} %pad_maximum_fusion.a_, ...), custom_call_target="tpu_custom_call" | custom-call | tf_op jit(solution)/shard_map/update/pallas_call | solution.py:357
  448.9 3.6 fusion.66
  (249 shorter events, 126.2 us)
Async XLA Ops:
  7.2 6.1 %copy-start.35 = (f32[512,64]{0,1:T(8,128)S(1)}, f32[512,64]{0,1:T(8,128)}, u32[]{:S(2)}) copy-start(f32[512,64]{0,1:T(8,128)} %param.31) | copy-start | bytes 393220
  7.2 6.9 %copy-start.19 = (f32[512,384]{1,0:T(8,128)S(1)}, f32[512,384]{1,0:T(8,128)}, u32[]{:S(2)}) copy-start(f32[512,384]{1,0:T(8,128)} %param.25) | copy-start | bytes 2359300
  7.2 7.7 %copy-start.30 = (f32[128,512]{1,0:T(8,128)S(1)}, f32[128,512]{1,0:T(8,128)}, u32[]{:S(2)}) copy-start(f32[128,512]{1,0:T(8,128)} %param.26) | copy-start | bytes 786436
  7.2 35.3 %all-gather.7.cloned.1.call-start = ((), (), s32[]{:S(2)}) async-start(), calls=%async_computation | async-start | bytes 1966080 | tf_op jit(solution)/shard_map/all_gather | solution.py:499
  9.3 6.5 %copy-start.32 = (f32[512,64]{0,1:T(8,128)S(1)}, f32[512,64]{0,1:T(8,128)}, u32[]{:S(2)}) copy-start(f32[512,64]{0,1:T(8,128)} %param.28) | copy-start | bytes 393220
  9.3 83.1 %all-gather.9.cloned.1.call-start = ((), (), s32[]{:S(2)}) async-start(), calls=%async_computation.1 | async-start | bytes 2162688 | tf_op jit(solution)/shard_map/all_gather | solution.py:501
  10.9 6.5 %copy-start.34 = (f32[512,64]{0,1:T(8,128)S(1)}, f32[512,64]{0,1:T(8,128)}, u32[]{:S(2)}) copy-start(f32[512,64]{0,1:T(8,128)} %param.30) | copy-start | bytes 393220
  10.9 140.1 %all-gather.11.cloned.1.call-start = ((), (), s32[]{:S(2)}) async-start(), calls=%async_computation.2 | async-start | bytes 2162688 | tf_op jit(solution)/shard_map/all_gather | solution.py:502
  12.6 214.7 %all-gather.15.cloned.1.call-start = ((), (), s32[]{:S(2)}) async-start(), calls=%async_computation.4 | async-start | bytes 2162688 | tf_op jit(solution)/shard_map/all_gather | solution.py:571
  13.3 254.9 %all-gather.17.cloned.1.call-start = ((), (), s32[]{:S(2)}) async-start(), calls=%async_computation.5 | async-start | bytes 2162688 | tf_op jit(solution)/shard_map/all_gather | solution.py:572
  14.0 275.4 %all-gather.13.cloned.1.call-start = ((), (), s32[]{:S(2)}) async-start(), calls=%async_computation.3 | async-start | bytes 1966080 | tf_op jit(solution)/shard_map/all_gather | solution.py:569
  14.9 24.1 %copy-start.24 = (bf16[1024,512]{1,0:T(8,128)(2,1)S(1)}, bf16[1024,512]{1,0:T(8,128)(2,1)}, u32[]{:S(2)}) copy-start(bf16[1024,512]{1,0:T(8,128)(2,1)} %param.18) | copy-start | bytes 3145732
  19.9 22.7 %copy-start.45 = (f32[1,512]{1,0:T(1,128)}, f32[1,512]{1,0:T(1,128)S(1)}, u32[]{:S(2)}) copy-start(f32[1,512]{1,0:T(1,128)S(1)} %get-tuple-element.244) | copy-start | bytes 6148
  19.9 22.7 %copy-start.53 = (f32[1,512]{1,0:T(1,128)}, f32[1,512]{1,0:T(1,128)S(1)}, u32[]{:S(2)}) copy-start(f32[1,512]{1,0:T(1,128)S(1)} %get-tuple-element.243) | copy-start | bytes 6148
  19.9 72.5 %copy-start.51 = (f32[1,512]{1,0:T(1,128)}, f32[1,512]{1,0:T(1,128)S(1)}, u32[]{:S(2)}) copy-start(f32[1,512]{1,0:T(1,128)S(1)} %get-tuple-element.245) | copy-start | bytes 6148
  20.0 19.8 %copy-start.22 = (f32[128,512]{0,1:T(8,128)}, f32[128,512]{0,1:T(8,128)S(1)}, u32[]{:S(2)}) copy-start(f32[128,512]{0,1:T(8,128)S(1)} %copy.127) | copy-start | bytes 786436
  39.6 41.1 %copy-start = (bf16[1024,512]{0,1:T(8,128)(2,1)}, bf16[1024,512]{0,1:T(8,128)(2,1)S(1)}, u32[]{:S(2)}) copy-start(bf16[1024,512]{0,1:T(8,128)(2,1)S(1)} %copy.107) | copy-start | bytes 3145732
  39.8 7.8 %copy-start.40 = (f32[1024]{0:T(1024)}, f32[1024]{0:T(1024)S(1)}, u32[]{:S(2)}) copy-start(f32[1024]{0:T(1024)S(1)} %broadcast_multiply_fusion.6) | copy-start | bytes 12292
  41.2 6.4 %copy-start.42 = (f32[1024]{0:T(1024)}, f32[1024]{0:T(1024)S(1)}, u32[]{:S(2)}) copy-start(f32[1024]{0:T(1024)S(1)} %add_rsqrt_fusion.1) | copy-start | bytes 12292
  160.3 7.2 %copy-start.55 = (bf16[512,2048]{0,1:T(8,128)(2,1)S(1)}, bf16[512,2048]{0,1:T(8,128)(2,1)}, u32[]{:S(2)}) copy-start(bf16[512,2048]{0,1:T(8,128)(2,1)} %all-gather.9.cloned.1.call-done) | copy-start | bytes 6291460
  231.2 41.1 %copy-start.3 = (f32[1024,512]{0,1:T(8,128)S(1)}, f32[1024,512]{0,1:T(8,128)}, u32[]{:S(2)}) copy-start(f32[1024,512]{0,1:T(8,128)} %copy-done.2) | copy-start | bytes 6291460
  294.2 131.4 %copy-start.31 = (f32[512,64]{1,0:T(8,128)S(1)}, f32[512,64]{1,0:T(8,128)}, u32[]{:S(2)}) copy-start(f32[512,64]{1,0:T(8,128)} %copy.134) | copy-start | bytes 393220
  425.6 14.4 %copy-start.39 = (bf16[512,128]{1,0:T(8,128)(2,1)S(1)}, bf16[512,128]{1,0:T(8,128)(2,1)}, u32[]{:S(2)}) copy-start(bf16[512,128]{1,0:T(8,128)(2,1)} %get-tuple-element.116) | copy-start | bytes 393220
  427.4 16.7 %copy-start.23 = (f32[128,512]{0,1:T(8,128)S(1)}, f32[128,512]{0,1:T(8,128)}, u32[]{:S(2)}) copy-start(f32[128,512]{0,1:T(8,128)} %copy-done.22) | copy-start | bytes 786436
  (48 other events, 128.9 us)
Sparse Core Ops, SparseCore 0:
  10.2 22.9 all-gather.6
  36.6 55.6 all-gather.8
  95.8 55.2 all-gather.10
  154.4 55.2 all-gather.14
  212.9 55.2 all-gather.16
  270.2 19.1 all-gather.12

commit v2 on v1

--- a/solution.py
+++ b/solution.py
@@ -102,8 +102,274 @@
     )
 
 
-COMM_ORDERS = ("cxylg", "cylgx", "clgxy")
+ROWS = 1024
+TILE = 256
+PAIRS = 4
 WIDE = 2048
+CHUNK = 512
+VMEM_BYTES = 62 << 20
+LOW = jnp.bfloat16
+F32 = jnp.float32
+
+
+def dot(one, two):
+    return jnp.dot(one, two, preferred_element_type=F32)
+
+
+def dot_back(one, two):
+    return lax.dot_general(one, two, (((1,), (1,)), ((), ())), preferred_element_type=F32)
+
+
+def dot_rows(one, two):
+    return lax.dot_general(one, two, (((0,), (0,)), ((), ())), preferred_element_type=F32)
+
+
+def each(count, body):
+    def step(i, carry):
+        body(i)
+        return carry
+
+    lax.fori_loop(0, count, step, 0)
+
+
+def rows_at(i, size):
+    return pl.ds(pl.multiple_of(i * size, size), size)
+
+
+def first_phase(tokens, params, first):
+    gain = params[0:1, :]
+    shift = params[1:2, :]
+
+    def body(i):
+        here = rows_at(i, 128)
+        plain_gain, _, _ = normalize(tokens[here, :].astype(F32), gain, shift)
+        first[here, :] = plain_gain.astype(LOW)
+
+    each(ROWS // 128, body)
+
+
+def mixed_phase(pair, first, wqkv, mixed):
+    def body(i):
+        here = rows_at(i, TILE)
+        mixed[pair, here, :] = dot(first[here, :], wqkv[pair]).astype(LOW)
+
+    each(ROWS // TILE, body)
+
+
+def bias_phase(seg_col, seg_row, bias):
+    def body(i):
+        here = rows_at(i, 128)
+        row = seg_row[pl.ds(i // 4, 1), :]
+        bias[here, :] = jnp.where(seg_col[here, :] == row, 0.0, neg_fill).astype(LOW)
+
+    each(ROWS // 128, body)
+
+
+def attend_phase(pair, mixed, bias, probs, context):
+    tile = 256
+    lane = lax.broadcasted_iota(jnp.int32, (1, 128), 1)
+    left = (lane < HEAD_DIM).astype(LOW)
+
+    def body(i):
+        seq = i // (SEQ // tile)
+        here = rows_at(i, tile)
+        keys_at = rows_at(seq, SEQ)
+        inside = rows_at(i % (SEQ // tile), tile)
+        query = mixed[pair, here, 0:128] * LOW(HEAD_DIM ** (-0.5))
+        keys = mixed[pair, keys_at, 128:256]
+        values = mixed[pair, keys_at, 256:384]
+        allowed = bias[here, :].astype(F32)
+        outs = []
+        for half in range(2):
+            mask = left if half == 0 else LOW(1.0) - left
+            scores = dot_back(query * mask, keys) + allowed
+            top = jnp.max(scores, axis=-1, keepdims=True)
+            weights = jnp.exp(scores - top)
+            total = jnp.sum(weights, axis=-1, keepdims=True)
+            prob = (weights * (1.0 / total)).astype(LOW)
+            probs[pair * 4 + half * 2 + seq, inside, :] = prob
+            outs.append(dot(prob, values))
+        context[here, pl.ds(pl.multiple_of(pair * 128, 128), 128)] = jnp.where(
+            lane < HEAD_DIM, outs[0], outs[1]
+        ).astype(LOW)
+
+    each(ROWS // tile, body)
+
+
+def second_phase(tokens, context, wout, params, middle, second):
+    gain = params[2:3, :]
+    shift = params[3:4, :]
+
+    def body(i):
+        here = rows_at(i, TILE)
+        value = tokens[here, :].astype(F32) + dot(context[here, :], wout[...])
+        middle[here, :] = value
+        normal, _, _ = normalize(value, gain, shift)
+        second[here, :] = normal.astype(LOW)
+
+    each(ROWS // TILE, body)
+
+
+def turn_phase(src, dst):
+    def body(i):
+        here = rows_at(i, 256)
+        dst[:, here] = src[here, :].T
+
+    each(ROWS // 256, body)
+
+
+def feed_phase(
+    chunk, second, second_t, out_grad, out_grad_t, up, down, active, hidden_grad,
+    result, second_grad, g_up, g_down,
+):
+    units = rows_at(chunk, CHUNK)
+
+    def body(i):
+        here = rows_at(i, TILE)
+        hidden = dot_back(second[here, :], up[units, :])
+        switch = 0.5 * jnp.tanh(0.851 * hidden) + 0.5
+        act = (hidden * switch).astype(LOW)
+        active[here, :] = act
+        grad = dot_back(out_grad[here, :], down[units, :])
+        back = (grad * (switch + 1.702 * hidden * switch * (1.0 - switch))).astype(LOW)
+        hidden_grad[here, :] = back
+        result[here, :] += dot(act, down[units, :])
+        second_grad[here, :] += dot(back, up[units, :])
+
+    each(ROWS // TILE, body)
+
+    def grads(c):
+        here = rows_at(c, 256)
+        for turned, wide, out in ((out_grad_t, active, g_down), (second_t, hidden_grad, g_up)):
+            grad = dot(turned[here, :], wide[...]).astype(LOW)
+            for j in range(CHUNK // 128):
+                out[chunk * 8 + j * 2 + c] = grad[:, j * 128 : j * 128 + 128]
+
+    each(2, grads)
+
+
+def middle_phase(
+    params, middle, result, second_grad, out_grad, wout,
+    layer_out, middle_grad, attended_low, context_grad, norms,
+):
+    gain = params[2:3, :]
+
+    def body(i, sums):
+        here = rows_at(i, TILE)
+        value = middle[here, :]
+        layer_out[here, :] = (value + result[here, :]).astype(LOW)
+        _, plain, factor = normalize(value, gain, gain)
+        upper = second_grad[here, :]
+        lower, gains, shifts = normalize_back(upper, plain, factor, gain)
+        total = out_grad[here, :].astype(F32) + lower
+        middle_grad[here, :] = total
+        low = total.astype(LOW)
+        attended_low[here, :] = low
+        context_grad[here, :] = dot_back(low, wout[...]).astype(LOW)
+        return (sums[0] + gains[None], sums[1] + shifts[None])
+
+    zero = jnp.zeros((1, 512), F32)
+    sums = lax.fori_loop(0, ROWS // TILE, body, (zero, zero))
+    norms[2:3, :] = sums[0]
+    norms[3:4, :] = sums[1]
+
+
+def out_phase(attended_t, context, g_attend):
+    def body(i):
+        grad = dot(attended_t[rows_at(i, 256), :], context[...]).astype(LOW)
+        for j in range(4):
+            for p in range(PAIRS):
+                g_attend[i * 16 + j * 4 + p, :, 384:512] = grad[
+                    j * 64 : j * 64 + 64, p * 128 : p * 128 + 128
+                ]
+
+    each(2, body)
+
+
+def attend_back_phase(pair, mixed, probs, context_grad, pair_grad):
+    lane = lax.broadcasted_iota(jnp.int32, (1, 128), 1)
+    left = (lane < HEAD_DIM).astype(LOW)
+    scale = HEAD_DIM ** (-0.5)
+
+    def body(seq):
+        here = rows_at(seq, SEQ)
+        query = mixed[pair, here, 0:128]
+        keys = mixed[pair, here, 128:256]
+        values = mixed[pair, here, 256:384]
+        upper = context_grad[here, pl.ds(pl.multiple_of(pair * 128, 128), 128)]
+        outs = []
+        for half in range(2):
+            mask = left if half == 0 else LOW(1.0) - left
+            above = upper * mask
+            prob_low = probs[pair * 4 + half * 2 + seq]
+            prob = prob_low.astype(F32)
+            prob_grad = dot_back(above, values)
+            inner = jnp.sum(prob * prob_grad, axis=-1, keepdims=True)
+            score_grad = (prob * (prob_grad - inner)).astype(LOW)
+            outs.append(
+                (
+                    dot(score_grad, keys),
+                    dot_rows(score_grad, query),
+                    dot_rows(prob_low, above),
+                )
+            )
+        pick = lane < HEAD_DIM
+        pair_grad[here, 0:128] = (jnp.where(pick, outs[0][0], outs[1][0]) * scale).astype(LOW)
+        pair_grad[here, 128:256] = (jnp.where(pick, outs[0][1], outs[1][1]) * scale).astype(LOW)
+        pair_grad[here, 256:384] = (outs[0][2] + outs[1][2]).astype(LOW)
+
+    each(ROWS // SEQ, body)
+
+
+def qkv_phase(pair, pair_grad, first_t, wqkv, g_attend, first_grad):
+    def body(i):
+        here = rows_at(i, TILE)
+        first_grad[here, :] += dot_back(pair_grad[here, :], wqkv[pair])
+
+    each(ROWS // TILE, body)
+
+    def grads(i):
+        grad = dot(first_t[rows_at(i, 256), :], pair_grad[...]).astype(LOW)
+        for j in range(4):
+            g_attend[i * 16 + j * 4 + pair, :, 0:384] = grad[j * 64 : j * 64 + 64, :]
+
+    each(2, grads)
+
+
+def input_phase(params, tokens, first_grad, input_grad, norms):
+    gain = params[0:1, :]
+
+    def body(i, sums):
+        here = rows_at(i, TILE)
+        _, plain, factor = normalize(tokens[here, :].astype(F32), gain, gain)
+        lower, gains, shifts = normalize_back(first_grad[here, :], plain, factor, gain)
+        input_grad[here, :] += lower
+        return (sums[0] + gains[None], sums[1] + shifts[None])
+
+    zero = jnp.zeros((1, 512), F32)
+    sums = lax.fori_loop(0, ROWS // TILE, body, (zero, zero))
+    norms[0:1, :] = sums[0]
+    norms[1:2, :] = sums[1]
+
+
+def local_call(kernel, outs, scratch, args, name):
+    vmem = pl.BlockSpec(memory_space=pltpu.VMEM)
+    return pl.pallas_call(
+        kernel,
+        out_shape=tuple(jax.ShapeDtypeStruct(*o) for o in outs),
+        in_specs=[vmem] * len(args),
+        out_specs=(vmem,) * len(outs),
+        scratch_shapes=[pltpu.VMEM(*v) for v in scratch],
+        compiler_params=pltpu.CompilerParams(vmem_limit_bytes=60 << 20),
+        name=name,
+    )(*args)
+
+
+STEP_DIMS = {"c": 1, "x": 2, "y": 4, "l": 8, "g": 16}
+GATHER_UP = ("g", "l", "y", "x", "c")
+GATHER_DOWN = ("l", "g", "x", "y", "c")
+STARTS = (("g", "l", "y", "x", "c"), ("g", "x", "l", "y", "c"), ("g", "y", "x", "l", "c"))
+ATTEND_ORDER = ("c", "x", "y", "l", "g")
 
 
 def coordinates():
@@ -135,258 +401,578 @@
     )
 
 
-def greet(head, dp, peers):
-    barrier = pltpu.get_barrier_semaphore()
-    across = (dp, 3 - head)
-    everyone = list(peers.values()) + [across]
-    for peer in everyone:
-        pl.semaphore_signal(
-            barrier, inc=1, device_id=peer, device_id_type=pl.DeviceIdType.MESH
-        )
-    pl.semaphore_wait(barrier, len(everyone))
-    return across
-
-
-def add_rows(dst, dst_at, one, one_at, two, two_at, count):
-    def body(i, carry):
-        here = pl.multiple_of(i * 16, 16)
-        total = one[pl.ds(one_at + here, 16), :].astype(jnp.float32) + two[
-            pl.ds(two_at + here, 16), :
-        ].astype(jnp.float32)
-        dst[pl.ds(dst_at + here, 16), :] = total.astype(jnp.bfloat16)
-        return carry
-
-    lax.fori_loop(0, count // 16, body, 0)
-
-
-def update_kernel(
-    a_ref, u_ref, d_ref, vec_ref, mom_ref,
-    oq_ref, oo_ref, ou_ref, od_ref, gq_ref, go_ref, gu_ref, gd_ref, vsum_ref, scal_ref,
-    got, acc, full, vgot, vnow, block, work, gram_ref, mix_ref,
-    ssem, rsem, asem, bsem, vssem, vrsem, dssem, drsem,
+def tile_of(fixed, free, place):
+    total = 0
+    for name, bit in fixed.items():
+        total = total + STEP_DIMS[name] * bit
+    for i, name in enumerate(free):
+        total = total + STEP_DIMS[name] * ((place // 2**i) % 2)
+    return total
+
+
+def scatter_start(acc, got, base, fixed, name, free, bits, peer, sems, slot):
+    for place in range(2 ** len(free)):
+        away = tile_of({**fixed, name: 1 - bits[name]}, free, place)
+        remote(
+            acc.at[away], got.at[base + place], sems[0].at[slot], sems[1].at[slot], peer
+        ).start()
+
+
+def scatter_end(acc, got, base, fixed, name, free, bits, peer, sems, slot):
+    count = 2 ** len(free)
+    span = got.at[pl.ds(base, count)]
+    remote(span, span, sems[0].at[slot], sems[1].at[slot], peer).wait()
+    rows = acc.shape[1]
+
+    def body(i):
+        here = tile_of({**fixed, name: bits[name]}, free, i)
+        acc[here] = (acc[here].astype(F32) + got[base + i].astype(F32)).astype(LOW)
+
+    each(count, body)
+
+
+def gather_start(ref, rows, done, name, bits, peer, sems, slot):
+    fixed = {d: bits[d] for d in STEP_DIMS if d not in done}
+    for place in range(2 ** len(done)):
+        tile = tile_of(fixed, done, place)
+        if rows:
+            part = ref.at[pl.ds(pl.multiple_of(tile * rows, rows), rows)]
+        else:
+            part = ref.at[tile]
+        remote(part, part, sems[0].at[slot], sems[1].at[slot], peer).start()
+
+
+def gather_end(ref, rows, done, peer, sems, slot):
+    span = ref.at[pl.ds(0, 2 ** len(done) * (rows or 1))]
+    remote(span, span, sems[0].at[slot], sems[1].at[slot], peer).wait()
+
+
+def paired(block):
+    parts = [block[:, i * 64 : i * 64 + 64] for i in (0, 3, 1, 4, 2, 5)]
+    return jnp.concatenate(parts, axis=1)
+
+
+def unpaired(block):
+    parts = [block[:, i * 64 : i * 64 + 64] for i in (0, 2, 4, 1, 3, 5)]
+    return jnp.concatenate(parts, axis=1)
+
+
+def layer_kernel(
+    tokens, seg_col, seg_row, out_grad, params, w_qkv, m_qkv, w_out, m_out, w_up, m_up, w_down, m_down,
+    layer_out, input_grad, start_a, start_u, start_d, ortho_q, ortho_o, ortho_u, ortho_d, norm_sum, scal,
+    first, mixed, context, bias, wqkv, wout, wup, wdown, pool, middle, second, second_t, out_grad_t,
+    active, hidden_grad, result, second_grad, pair_grad, acc_a, acc_u, acc_d, got_a, got_u, got_d,
+    mom_t, mom_x, mom_u, mom_d, mom_a, norm_now, norm_got, stat_got, gram, mix, send, recv,
 ):
     dp, head, bits, peers = coordinates()
-    across = greet(head, dp, peers)
-    sources = (a_ref, u_ref, d_ref)
-    vnow[0] = vec_ref[...]
-    spans = []
-    for m in range(3):
-        low = 0
-        size = 512
-        span = []
-        for name in COMM_ORDERS[m]:
-            size = size // 2
-            keep = low + bits[name] * size
-            give = low + (1 - bits[name]) * size
-            span.append((name, size, keep, give))
-            low = keep
-        spans.append(span)
+    me = dp * 4 + head
+    sems = (send, recv)
+    across = (dp, 3 - head)
+    S_Q, S_O, S_M, S_UP, S_DOWN, S_CHUNK, S_LG, S_A, S_NORM, S_STAT, S_START, S_ORTHO = (
+        0, 4, 8, 10, 15, 20, 44, 48, 53, 58, 59, 74
+    )
+    barrier = pltpu.get_barrier_semaphore()
+
+    def greet(i):
+        other = (me + 1 + i) % 32
+        pl.semaphore_signal(
+            barrier, inc=1, device_id=(other // 4, other % 4), device_id_type=pl.DeviceIdType.MESH
+        )
+
+    each(31, greet)
+    wqkv[head] = paired(w_qkv[...].astype(LOW))
+    wout[pl.ds(pl.multiple_of(head * 128, 128), 128), :] = w_out[...].astype(LOW)
+    mine = pl.ds(pl.multiple_of(me * 64, 64), 64)
+    wup[mine, :] = w_up[...].astype(LOW)
+    wdown[mine, :] = w_down[...].astype(LOW)
+    pl.semaphore_wait(barrier, 31)
+
+    def block_q(who):
+        return wqkv.at[who]
+
+    def block_o(who):
+        return wout.at[pl.ds(pl.multiple_of(who * 128, 128), 128)]
+
+    def weight_copy(block, who, slot, peer):
+        return remote(block(who), block(who), send.at[slot], recv.at[slot], peer)
+
+    sibling = peers["c"]
+    weight_copy(block_q, head, S_Q + 1, sibling).start()
+    weight_copy(block_q, head, S_Q + 2, peers["x"]).start()
+    gather_start(wup, 64, (), GATHER_UP[0], bits, peers[GATHER_UP[0]], sems, S_UP)
+    gather_start(wdown, 64, (), GATHER_DOWN[0], bits, peers[GATHER_DOWN[0]], sems, S_DOWN)
+    weight_copy(block_o, head, S_O + 1, sibling).start()
+    weight_copy(block_o, head, S_O + 2, peers["x"]).start()
+    other_half = pl.ds(pl.multiple_of((1 - bits["c"]) * 256, 256), 256)
+
+    def moment_copy(i, ref):
+        return remote(ref.at[:, other_half], mom_x.at[i], send.at[S_M + i], recv.at[S_M + i], sibling)
+
+    moment_copy(0, m_up).start()
+    moment_copy(1, m_down).start()
+
+    def weight_step(k):
+        for ref, order, slot in ((wup, GATHER_UP, S_UP), (wdown, GATHER_DOWN, S_DOWN)):
+            gather_end(ref, 64, order[:k], peers[order[k]], sems, slot + k)
+            if k < 4:
+                gather_start(
+                    ref, 64, order[: k + 1], order[k + 1], bits, peers[order[k + 1]], sems, slot + k + 1
+                )
+
+    first_phase(tokens, params, first)
+    bias_phase(seg_col, seg_row, bias)
+    weight_step(0)
+    turn_phase(out_grad, out_grad_t)
+
+    def pair_body(j):
+        pair = (bits["c"] + j % 2) % 2 + 2 * ((bits["x"] + j // 2) % 2)
+        mixed_phase(pair, first, wqkv, mixed)
+        attend_phase(pair, mixed, bias, pool, context)
+
+        @pl.when(j == 0)
+        def _():
+            weight_step(1)
+            weight_copy(block_q, head, S_Q + 1, sibling).wait()
+            weight_copy(block_o, head, S_O + 1, sibling).wait()
+            weight_copy(block_q, head, S_Q + 2, peers["x"]).wait()
+            weight_copy(block_q, peers["x"][1], S_Q + 3, sibling).start()
+            weight_copy(block_o, head, S_O + 2, peers["x"]).wait()
+            weight_copy(block_o, peers["x"][1], S_O + 3, sibling).start()
+
+        @pl.when(j == 1)
+        def _():
+            weight_step(2)
+
+        @pl.when(j == 2)
+        def _():
+            weight_copy(block_q, head, S_Q + 3, sibling).wait()
+            weight_copy(block_o, head, S_O + 3, sibling).wait()
+
+    each(PAIRS, pair_body)
+    second_phase(tokens, context, wout, params, middle, second)
+    weight_step(3)
+    turn_phase(second, second_t)
+    result[...] = jnp.zeros_like(result)
+    second_grad[...] = jnp.zeros_like(second_grad)
+    weight_step(4)
+
+    chunk_orders = ((acc_u, got_u, ("c", "x", "y")), (acc_d, got_d, ("c", "y", "x")))
+
+    def chunk_args(q, k, order):
+        fixed = {"g": q // 2, "l": q % 2}
+        for name in order[:k]:
+            fixed[name] = bits[name]
+        return fixed, order[k], order[k + 1 :]
+
+    def chunk_start(q, k):
+        for i, (acc, got, order) in enumerate(chunk_orders):
+            fixed, name, free = chunk_args(q, k, order)
+            scatter_start(
+                acc, got, q * 7 + (0, 4, 6)[k], fixed, name, free, bits, peers[name], sems,
+                S_CHUNK + q * 6 + i * 3 + k,
+            )
+
+    def chunk_end(q, k):
+        for i, (acc, got, order) in enumerate(chunk_orders):
+            fixed, name, free = chunk_args(q, k, order)
+            scatter_end(
+                acc, got, q * 7 + (0, 4, 6)[k], fixed, name, free, bits, peers[name], sems,
+                S_CHUNK + q * 6 + i * 3 + k,
+            )
+
+    def feed_body(q):
+        feed_phase(
+            q, second, second_t, out_grad, out_grad_t, wup, wdown, active, hidden_grad,
+            result, second_grad, acc_u, acc_d,
+        )
+        chunk_start(q, 0)
+
+        @pl.when(q >= 1)
+        def _():
+            chunk_end(q - 1, 0)
+            chunk_start(q - 1, 1)
+
+        @pl.when(q >= 2)
+        def _():
+            chunk_end(q - 2, 1)
+            chunk_start(q - 2, 2)
+
+        @pl.when(q >= 3)
+        def _():
+            chunk_end(q - 3, 2)
+
+    each(WIDE // CHUNK, feed_body)
+    chunk_end(3, 0)
+    chunk_start(3, 1)
+    middle_phase(
+        params, middle, result, second_grad, out_grad, wout,
+        layer_out, input_grad, second, active, norm_now.at[0],
+    )
+    chunk_end(2, 1)
+    chunk_start(2, 2)
+    turn_phase(second, second_t)
+    out_phase(second_t, context, acc_a)
+    chunk_end(1, 2)
+    chunk_end(3, 1)
+    chunk_start(3, 2)
+    turn_phase(first, second_t)
+    result[...] = jnp.zeros_like(result)
+
+    def last_args(k):
+        fixed = {"c": bits["c"], "x": bits["x"], "y": bits["y"]}
+        if k == 1:
+            fixed["l"] = bits["l"]
+            return fixed, "g", ()
+        return fixed, "l", ("g",)
+
+    def last_step(k, ending):
+        for i, (acc, got, _) in enumerate(chunk_orders):
+            fixed, name, free = last_args(k)
+            (scatter_end if ending else scatter_start)(
+                acc, got, 28 + 2 * k, fixed, name, free, bits, peers[name], sems, S_LG + 2 * k + i
+            )
+
+    def back_body(pair):
+        attend_back_phase(pair, mixed, pool, active, pair_grad)
+        qkv_phase(pair, pair_grad, second_t, wqkv, acc_a, result)
+
+        @pl.when(pair == 0)
+        def _():
+            chunk_end(2, 2)
+            chunk_end(3, 2)
+            last_step(0, False)
+
+        @pl.when(pair == 1)
+        def _():
+            last_step(0, True)
+            last_step(1, False)
+
+        @pl.when(pair == 2)
+        def _():
+            last_step(1, True)
+
+    each(PAIRS, back_body)
+
+    def attend_args(k):
+        order = ATTEND_ORDER
+        return {d: bits[d] for d in order[:k]}, order[k], order[k + 1 :]
+
+    def norm_copy(k):
+        return remote(
+            norm_now.at[k], norm_got.at[k], send.at[S_NORM + k], recv.at[S_NORM + k],
+            peers[ATTEND_ORDER[k]],
+        )
+
     for k in range(5):
-        copies = []
+        fixed, name, free = attend_args(k)
+        base = 32 - 2 ** (5 - k)
+        scatter_start(acc_a, got_a, base, fixed, name, free, bits, peers[name], sems, S_A + k)
+        if k == 0:
+            input_phase(params, tokens, result, input_grad, norm_now.at[0])
+            moment_copy(0, m_up).wait()
+            moment_copy(1, m_down).wait()
+            keep = pl.ds(pl.multiple_of(bits["c"] * 256, 256), 256)
+            for i, (ref, out) in enumerate(((m_up, mom_u), (m_down, mom_d))):
+                own = ref[:, keep]
+                far = mom_x[i]
+                low_half = jnp.where(bits["c"] == 0, own, far)
+                high_half = jnp.where(bits["c"] == 0, far, own)
+                out[...] = jnp.concatenate([low_half, high_half], axis=0).T
+            mom_t[...] = m_out[...].T
+            here = pl.ds(pl.multiple_of(dp * 64, 64), 64)
+            mom_a[:, 0:384] = paired(m_qkv[here, :])
+            mom_a[:, 384:512] = mom_t[here, :]
+        norm_copy(k).start()
+        scatter_end(acc_a, got_a, base, fixed, name, free, bits, peers[name], sems, S_A + k)
+        norm_copy(k).wait()
+        norm_now[k + 1] = norm_now[k] + norm_got[k]
+
+    def total_of(value):
+        return jnp.sum(jnp.sum(value, axis=0, keepdims=True), axis=1, keepdims=True)
+
+    lane = lax.broadcasted_iota(jnp.int32, (8, 128), 1)
+    column = lax.broadcasted_iota(jnp.int32, (1, 512), 1)
+    grad_a = acc_a[me].astype(F32)
+    grad_u = acc_u[me].astype(F32)
+    grad_d = acc_d[me].astype(F32)
+    stats = jnp.zeros((8, 128), F32)
+    products = []
+    for moment, grad in ((mom_a[...], grad_a), (mom_u[...], grad_u), (mom_d[...], grad_d)):
+        products.append((moment * moment, moment * grad, grad * grad))
+    for i in range(3):
+        inside = column < 384
+        stats = jnp.where(lane == i, total_of(jnp.where(inside, products[0][i], 0.0)), stats)
+        stats = jnp.where(lane == 3 + i, total_of(jnp.where(inside, 0.0, products[0][i])), stats)
+        stats = jnp.where(lane == 6 + i, total_of(products[1][i]), stats)
+        stats = jnp.where(lane == 9 + i, total_of(products[2][i]), stats)
+    stat_got[me] = stats
+
+    def tell(i):
+        other = (me + 1 + i) % 32
+        remote(
+            stat_got.at[me], stat_got.at[me], send.at[S_STAT], recv.at[S_STAT], (other // 4, other % 4)
+        ).start()
+
+    each(31, tell)
+    span = stat_got.at[pl.ds(0, 31)]
+    remote(span, span, send.at[S_STAT], recv.at[S_STAT], sibling).wait()
+    stats = jnp.sum(stat_got[...], axis=0)
+
+    def stat(i):
+        return jnp.sum(jnp.where(lane == i, stats, 0.0), axis=1, keepdims=True)[0:1]
+
+    vector = norm_now[5]
+    norm_sum[...] = vector
+    norm = jnp.sqrt(stat(2) + stat(5) + stat(8) + stat(11) + total_of(vector * vector))
+    clip = jnp.minimum(1.0, 1.0 / (norm + 1e-06))
+    sizes = []
+    for m in range(4):
+        square = (
+            momentum_decay * momentum_decay * stat(3 * m)
+            + 2.0 * momentum_decay * clip * stat(3 * m + 1)
+            + clip * clip * stat(3 * m + 2)
+        )
+        sizes.append(jnp.sqrt(jnp.maximum(square, 0.0)) + 1e-07)
+    told = jnp.where(lane == 0, norm, clip)
+    for m in range(4):
+        told = jnp.where(lane == 2 + m, sizes[m], told)
+    scal[...] = told
+    scale_a = jnp.where(column < 384, 1.0 / sizes[0], 1.0 / sizes[1])
+    got_a[me] = ((momentum_decay * mom_a[...] + clip * grad_a) * scale_a).astype(LOW)
+    got_u[me] = ((momentum_decay * mom_u[...] + clip * grad_u) * (1.0 / sizes[2])).astype(LOW)
+    got_d[me] = ((momentum_decay * mom_d[...] + clip * grad_d) * (1.0 / sizes[3])).astype(LOW)
+
+    starts = (got_a, got_u, got_d)
+    for k in range(5):
         for m in range(3):
-            name, size, keep, give = spans[m][k]
-            place = 512 - 2 * size
-            if k == 0:
-                src = sources[m].at[pl.ds(pl.multiple_of(give, 16), size)]
-            else:
-                before = 512 - 4 * size
-                src = acc.at[m, pl.ds(pl.multiple_of(before + (1 - bits[name]) * size, 16), size)]
-            cp = remote(
-                src, got.at[m, pl.ds(place, size)], ssem.at[m, k], rsem.at[m, k], peers[name]
+            order = STARTS[m]
+            gather_start(
+                starts[m], 0, order[:k], order[k], bits, peers[order[k]], sems, S_START + 3 * k + m
             )
-            cp.start()
-            copies.append(cp)
-        vcp = remote(vnow.at[k], vgot.at[k], vssem.at[k], vrsem.at[k], peers[COMM_ORDERS[0][k]])
-        vcp.start()
         for m in range(3):
-            name, size, keep, give = spans[m][k]
-            place = 512 - 2 * size
-            copies[m].wait()
-            if k == 0:
-                add_rows(acc.at[m], place, sources[m], pl.multiple_of(keep, 16), got.at[m], place, size)
-            elif k < 4:
-                before = 512 - 4 * size
-                add_rows(
-                    acc.at[m], place, acc.at[m],
-                    pl.multiple_of(before + bits[name] * size, 16), got.at[m], place, size,
-                )
-            else:
-                before = 512 - 4 * size
-                add_rows(
-                    full.at[m], pl.multiple_of(keep, 16), acc.at[m],
-                    pl.multiple_of(before + bits[name] * size, 16), got.at[m], place, size,
-                )
-        vcp.wait()
-        vnow[k + 1] = vnow[k] + vgot[k]
-    for k in reversed(range(5)):
-        copies = []
-        for m in range(3):
-            name, size, keep, give = spans[m][k]
-            mine = full.at[m, pl.ds(pl.multiple_of(keep, 16), size)]
-            cp = remote(mine, mine, asem.at[m, k], bsem.at[m, k], peers[name])
-            cp.start()
-            copies.append(cp)
-        for cp in copies:
-            cp.wait()
-    vsum_ref[...] = vnow[5]
-    chunk = 16
-
-    def square_body(i, sums):
-        here = pl.multiple_of(i * chunk, chunk)
-        out = sums
-        for m in range(3):
-            part = full[m, pl.ds(here, chunk), :].astype(jnp.float32)
-            out = out + jnp.sum(part * part, axis=0, keepdims=True)
-        return out
-
-    sums = lax.fori_loop(0, 512 // chunk, square_body, jnp.zeros((1, WIDE), jnp.float32))
-    total = jnp.sum(sums, axis=1, keepdims=True)
-    vector = vnow[5]
-    total = total + jnp.sum(
-        jnp.sum(vector * vector, axis=0, keepdims=True), axis=1, keepdims=True
-    )
-    norm = jnp.sqrt(total)
-    clip = jnp.minimum(1.0, 1.0 / (norm + 1e-06))
-    lane = lax.broadcasted_iota(jnp.int32, (8, 128), 1)
-    scal_ref[...] = jnp.where(lane == 0, norm, clip)
-    which = jnp.maximum(head - 1, 0)
-    columns = lax.broadcasted_iota(jnp.int32, (chunk, WIDE), 1)
-    first_column = jnp.where(head == 1, 1536, 0)
-    past_column = jnp.where(head == 0, 1536, WIDE)
-    inside = (columns >= first_column) & (columns < past_column)
-
-    def moment_body(i, sums):
-        here = pl.multiple_of(i * chunk, chunk)
-        grad = full[which, pl.ds(here, chunk), :].astype(jnp.float32)
-        grad = jnp.where(inside, grad, 0.0)
-        moment = momentum_decay * mom_ref[pl.ds(here, chunk), :].astype(jnp.float32) + clip * grad
-        work[pl.ds(here, chunk), :] = moment
-        return sums + jnp.sum(moment * moment, axis=0, keepdims=True)
-
-    sums = lax.fori_loop(0, 512 // chunk, moment_body, jnp.zeros((1, WIDE), jnp.float32))
-    scale = 1.0 / (jnp.sqrt(jnp.sum(sums, axis=1, keepdims=True)) + 1e-07)
-
-    def start_body(i, carry):
-        here = pl.multiple_of(i * chunk, chunk)
-        block[0, pl.ds(here, chunk), :] = (work[pl.ds(here, chunk), :] * scale).astype(jnp.bfloat16)
-        return carry
-
-    lax.fori_loop(0, 512 // chunk, start_body, 0)
-    own = (gq_ref, go_ref, gu_ref, gd_ref)
-    gq_ref[...] = full[0, :, pl.ds(pl.multiple_of(head * 384, 128), 384)]
-    go_ref[...] = full[0, :, pl.ds(pl.multiple_of(1536 + head * 128, 128), 128)]
-    pair = pl.multiple_of((dp * 2 + bits["x"]) * 128, 128)
-    gu_ref[...] = full[1, :, pl.ds(pair, 128)]
-    gd_ref[...] = full[2, :, pl.ds(pair, 128)]
-    tile = 256
-
-    def turn_body(turn, carry):
-        now = turn % 2
-        later = 1 - now
-
-        def gram_body(i, c):
-            rows = pl.ds(pl.multiple_of(i * tile, tile), tile)
-            gram_ref[rows, :] = lax.dot_general(
-                block[now, rows, :], block[now], (((1,), (1,)), ((), ())),
-                preferred_element_type=jnp.float32,
-            ).astype(jnp.bfloat16)
-            return c
-
-        lax.fori_loop(0, 512 // tile, gram_body, 0)
-
-        def mix_body(i, c):
-            rows = pl.ds(pl.multiple_of(i * tile, tile), tile)
-            mine = gram_ref[rows, :]
-            mix_ref[rows, :] = (
-                ns_b * mine.astype(jnp.float32)
-                + ns_c * jnp.dot(mine, gram_ref[...], preferred_element_type=jnp.float32)
-            ).astype(jnp.bfloat16)
-            return c
-
-        lax.fori_loop(0, 512 // tile, mix_body, 0)
-
-        def next_body(i, c):
-            cols = pl.ds(pl.multiple_of(i * 512, 512), 512)
-            block[later, :, cols] = (
-                ns_a * block[now, :, cols].astype(jnp.float32)
-                + jnp.dot(mix_ref[...], block[now, :, cols], preferred_element_type=jnp.float32)
-            ).astype(jnp.bfloat16)
-            return c
-
-        lax.fori_loop(0, WIDE // 512, next_body, 0)
-        return carry
-
-    lax.fori_loop(0, NS_STEPS, turn_body, 0)
-    last = NS_STEPS % 2
-    outs = (oq_ref, oo_ref, ou_ref, od_ref)
+            order = STARTS[m]
+            gather_end(starts[m], 0, order[:k], peers[order[k]], sems, S_START + 3 * k + m)
+
+    @pl.when(head < 2)
+    def _():
+        wanted = jnp.where(head == 0, 1.0, 0.0)
+        here_only = jnp.where(column < 384, wanted, 1.0 - wanted).astype(LOW)
+
+        def body(i):
+            rows = pl.ds(pl.multiple_of((i // 4) * 64, 64), 64)
+            pool[i % 4, rows, :] = got_a[i] * here_only
+
+        each(32, body)
+
+    for kind, got in ((2, got_u), (3, got_d)):
+        @pl.when(head == kind)
+        def _(got=got):
+            def body(i):
+                for j in range(4):
+                    for c in range(2):
+                        pool[i, c * 256 : c * 256 + 256, j * 128 : j * 128 + 128] = got[i * 8 + j * 2 + c]
+
+            each(4, body)
+
+    def slice_body(i):
+        rows = pl.ds(pl.multiple_of(i * 64, 64), 64)
+        start_a[rows, :] = got_a[i * 4 + head]
+
+    each(8, slice_body)
+    left = me - bits["c"]
+    for c in range(2):
+        start_u[c * 256 : c * 256 + 256, :] = got_u[left + c]
+        start_d[c * 256 : c * 256 + 256, :] = got_d[left + c]
+
+    def turn_body(turn):
+        now = (turn % 2) * 4
+        later = 4 - now
+
+        def gram_body(i):
+            rows = rows_at(i, TILE)
+            total = dot_back(pool[now, rows, :], pool[now])
+            for b in range(1, 4):
+                total = total + dot_back(pool[now + b, rows, :], pool[now + b])
+            gram[rows, :] = total.astype(LOW)
+
+        each(512 // TILE, gram_body)
+
+        def mix_body(i):
+            rows = rows_at(i, TILE)
+            own = gram[rows, :]
+            mix[rows, :] = (ns_b * own.astype(F32) + ns_c * dot(own, gram[...])).astype(LOW)
+
+        each(512 // TILE, mix_body)
+
+        def next_body(b):
+            value = pool[now + b]
+            pool[later + b] = (ns_a * value.astype(F32) + dot(mix[...], value)).astype(LOW)
+
+        each(4, next_body)
+
+    each(NS_STEPS, turn_body)
+    last = (NS_STEPS % 2) * 4
+    outs = (ortho_q, ortho_o, ortho_u, ortho_d)
 
     def piece(kind, who):
         if kind == 0:
-            return block.at[last, :, pl.ds(pl.multiple_of(who * 384, 128), 384)]
+            return pool.at[last + who, :, pl.ds(0, 384)]
         if kind == 1:
-            return block.at[last, :, pl.ds(pl.multiple_of(1536 + who * 128, 128), 128)]
-        return block.at[last, :, pl.ds(pl.multiple_of((dp * 2 + who // 2) * 128, 128), 128)]
+            return pool.at[last + who, :, pl.ds(384, 128)]
+        block = dp * 2 + who // 2
+        return pool.at[last + block // 4, :, pl.ds(pl.multiple_of((block % 4) * 128, 128), 128)]
 
     partners = (peers["c"], peers["x"], across)
     for kind in range(4):
         @pl.when(head == kind)
         def _(kind=kind):
-            copies = []
             for j, partner in enumerate(partners):
-                cp = remote(
-                    piece(kind, partner[1]), outs[kind], dssem.at[j], drsem.at[kind], partner
-                )
-                cp.start()
-                copies.append(cp)
+                remote(
+                    piece(kind, partner[1]), outs[kind], send.at[S_ORTHO + j], recv.at[S_ORTHO + kind], partner
+                ).start()
             outs[kind][...] = piece(kind, head)[...]
-            for cp in copies:
-                cp.wait_send()
+            for j, partner in enumerate(partners):
+                remote(
+                    piece(kind, partner[1]), outs[kind], send.at[S_ORTHO + j], recv.at[S_ORTHO + kind], partner
+                ).wait_send()
 
     for kind in range(4):
         @pl.when(head != kind)
         def _(kind=kind):
             remote(
-                piece(kind, head), outs[kind], dssem.at[0], drsem.at[kind], partners[0]
+                piece(kind, head), outs[kind], send.at[S_ORTHO], recv.at[S_ORTHO + kind], sibling
             ).wait_recv()
 
 
-def update_call(a, u, d, vec, mom):
-    low = jnp.bfloat16
+def layer_call(*args):
     shape = jax.ShapeDtypeStruct
     vmem = pl.BlockSpec(memory_space=pltpu.VMEM)
+    outs = (
+        shape((ROWS, 512), LOW), shape((ROWS, 512), F32),
+        shape((512, 512), LOW), shape((512, 128), LOW), shape((512, 128), LOW),
+        shape((512, 384), LOW), shape((512, 128), LOW), shape((512, 128), LOW), shape((512, 128), LOW),
+        shape((4, 512), F32), shape((8, 128), F32),
+    )
+    scratch = [
+        ((ROWS, 512), LOW),
+        ((PAIRS, ROWS, 384), LOW),
+        ((ROWS, 512), LOW),
+        ((ROWS, SEQ), LOW),
+        ((PAIRS, 512, 384), LOW),
+        ((512, 512), LOW),
+        ((WIDE, 512), LOW),
+        ((WIDE, 512), LOW),
+        ((16, 512, 512), LOW),
+        ((ROWS, 512), F32),
+        ((ROWS, 512), LOW),
+        ((512, ROWS), LOW),
+        ((512, ROWS), LOW),
+        ((ROWS, CHUNK), LOW),
+        ((ROWS, CHUNK), LOW),
+        ((ROWS, 512), F32),
+        ((ROWS, 512), F32),
+        ((ROWS, 384), LOW),
+        ((32, 64, 512), LOW),
+        ((32, 256, 128), LOW),
+        ((32, 256, 128), LOW),
+        ((32, 64, 512), LOW),
+        ((32, 256, 128), LOW),
+        ((32, 256, 128), LOW),
+        ((512, 128), F32),
+        ((2, 64, 256), F32),
+        ((256, 128), F32),
+        ((256, 128), F32),
+        ((64, 512), F32),
+        ((6, 4, 512), F32),
+        ((5, 4, 512), F32),
+        ((32, 8, 128), F32),
+        ((512, 512), LOW),
+        ((512, 512), LOW),
+    ]
     return pl.pallas_call(
+        layer_kernel,
+        out_shape=outs,
+        in_specs=[vmem] * len(args),
+        out_specs=(vmem,) * len(outs),
+        scratch_shapes=[pltpu.VMEM(*v) for v in scratch]
+        + [pltpu.SemaphoreType.DMA((80,)), pltpu.SemaphoreType.DMA((80,))],
+        compiler_params=pltpu.CompilerParams(
+            collective_id=1, has_side_effects=True, vmem_limit_bytes=VMEM_BYTES
+        ),
+        name="layer",
+    )(*args)
+
+
+def update_kernel(
+    start_a, start_u, start_d, ortho_q, ortho_o, ortho_u, ortho_d, norm_sum, scal,
+    w_qkv, w_out, w_up, w_down, norm_first, norm_second,
+    new_q, mom_q, new_o, mom_o, new_u, mom_u, new_d, mom_d, clipped, first_new, second_new,
+):
+    core = lax.axis_index("head") % 2
+    clip = scal[0:1, 1:2]
+    keep = 1.0 - muon_rate * muon_decay
+
+    def fresh(weight, factor, ortho):
+        return weight * keep - muon_rate * factor * ortho
+
+    new_q[...] = fresh(w_qkv[...], math.sqrt(3.0), unpaired(ortho_q[...].astype(F32)))
+    mom_q[...] = unpaired(start_a[:, 0:384].astype(F32)) * scal[0:1, 2:3]
+    new_o[...] = fresh(w_out[...], math.sqrt(SEQ / 8.0), ortho_o[...].astype(F32).T)
+    mom_o[...] = start_a[:, 384:512].astype(F32).T * scal[0:1, 3:4]
+    for weight, ortho, start, new, mom, i in (
+        (w_up, ortho_u, start_u, new_u, mom_u, 4),
+        (w_down, ortho_d, start_d, new_d, mom_d, 5),
+    ):
+        turned = ortho[...].astype(F32).T
+        turned = jnp.where(core == 0, turned[0:64], turned[64:128])
+        new[...] = fresh(weight[...], math.sqrt(max(1.0, FF / 512)), turned)
+        turned = start[...].astype(F32).T
+        mom[...] = jnp.where(core == 0, turned[0:64], turned[64:128]) * scal[0:1, i : i + 1]
+    clip_grad = clip * norm_sum[...]
+    clipped[...] = clip_grad
+    first_new[...] = beta_one * norm_first[...] + (1.0 - beta_one) * clip_grad
+    second_new[...] = beta_two * norm_second[...] + (1.0 - beta_two) * clip_grad * clip_grad
+
+
+def fast_shards(
+    tokens,
+    segments,
+    out_grad,
+    norm_params,
+    norm_first,
+    norm_second,
+    qkv_weight,
+    qkv_moment,
+    out_weight,
+    out_moment,
+    up_weight,
+    up_moment,
+    down_weight,
+    down_moment,
+):
+    seg = lax.dynamic_slice_in_dim(segments, lax.axis_index("head") * ROWS, ROWS, 0)
+    (
+        layer_out, input_grad, start_a, start_u, start_d, ortho_q, ortho_o, ortho_u, ortho_d, norm_sum, scal
+    ) = layer_call(
+        tokens, seg[:, None], seg.reshape(ROWS // SEQ, SEQ), out_grad, norm_params,
+        qkv_weight, qkv_moment, out_weight, out_moment,
+        up_weight.T, up_moment.T, down_weight.T, down_moment.T,
+    )
+    tall = ((64, 512), F32)
+    new_q, mom_q, new_o, mom_o, new_u, mom_u, new_d, mom_d, clipped, first_new, second_new = local_call(
         update_kernel,
-        out_shape=(
-            shape((512, 384), low), shape((512, 128), low), shape((512, 128), low), shape((512, 128), low),
-            shape((512, 384), low), shape((512, 128), low), shape((512, 128), low), shape((512, 128), low),
-            shape((4, 512), jnp.float32), shape((8, 128), jnp.float32),
+        [((512, 384), F32)] * 2 + [((128, 512), F32)] * 2 + [tall] * 4 + [((4, 512), F32)] * 3,
+        [],
+        (
+            start_a, start_u, start_d, ortho_q, ortho_o, ortho_u, ortho_d, norm_sum, scal,
+            qkv_weight, out_weight, up_weight.T, down_weight.T, norm_first, norm_second,
         ),
-        in_specs=[vmem] * 5,
-        out_specs=(vmem,) * 10,
-        scratch_shapes=[
-            pltpu.VMEM((3, 512, WIDE), low),
-            pltpu.VMEM((3, 512, WIDE), low),
-            pltpu.VMEM((3, 512, WIDE), low),
-            pltpu.VMEM((5, 4, 512), jnp.float32),
-            pltpu.VMEM((6, 4, 512), jnp.float32),
-            pltpu.VMEM((2, 512, WIDE), low),
-            pltpu.VMEM((512, WIDE), jnp.float32),
-            pltpu.VMEM((512, 512), low),
-            pltpu.VMEM((512, 512), low),
-            pltpu.SemaphoreType.DMA((3, 5)),
-            pltpu.SemaphoreType.DMA((3, 5)),
-            pltpu.SemaphoreType.DMA((3, 5)),
-            pltpu.SemaphoreType.DMA((3, 5)),
-            pltpu.SemaphoreType.DMA((5,)),
-            pltpu.SemaphoreType.DMA((5,)),
-            pltpu.SemaphoreType.DMA((3,)),
-            pltpu.SemaphoreType.DMA((4,)),
-        ],
-        compiler_params=pltpu.CompilerParams(
-            collective_id=1, has_side_effects=True, vmem_limit_bytes=60 << 20
-        ),
-        name="update",
-    )(a, u, d, vec, mom)
+        "update",
+    )
+    return (
+        layer_out, input_grad, scal[0, 0], clipped, first_new, second_new,
+        new_q, mom_q, new_o, mom_o, new_u.T, mom_u.T, new_d.T, mom_d.T,
+    )
 
 
 def general_update(
@@ -471,7 +1057,7 @@
     return (owned, new_moments, vector_sum, grad_norm, clip)
 
 
-def shards(
+def general_shards(
     tokens,
     segments,
     out_grad,
@@ -558,44 +1144,10 @@
     )
     input_grad = middle_grad + input_lower
     vector_part = jnp.stack([gain_one, shift_one, gain_two, shift_two])
-    fast = lax.axis_size("dp") == 8 and lax.axis_size("head") == 4
-    if fast:
-        out_t = lax.dot_general(
-            attended_low, context, (((0,), (0,)), ((), ())), preferred_element_type=jnp.float32
-        )
-        both = jnp.concatenate([whole_qkv, out_t], axis=1).astype(jnp.bfloat16)
-        along = lax.axis_index("head")
-        low_m = [m.astype(jnp.bfloat16) for m in (qkv_moment, out_moment.T, up_moment, down_moment)]
-        mq = lax.all_gather(low_m[0], "head", axis=1, tiled=True)
-        mo = lax.all_gather(low_m[1], "head", axis=1, tiled=True)
-        mu = lax.all_gather(low_m[2], everywhere, axis=1, tiled=True)
-        md = lax.all_gather(low_m[3], everywhere, axis=1, tiled=True)
-        mom = lax.select_n(
-            along,
-            jnp.pad(mq, ((0, 0), (0, 512))),
-            jnp.pad(mo, ((0, 0), (1536, 0))),
-            mu,
-            md,
-        )
-        (oq, oo, ou, od, gq, go, gu, gd, vector_sum, scalars) = update_call(
-            both, up_grad.astype(jnp.bfloat16), down_grad.astype(jnp.bfloat16), vector_part, mom
-        )
-        grad_norm = scalars[0, 0]
-        clip = scalars[0, 1]
-        half = (along % 2) * 64
-        cut = lambda v: lax.dynamic_slice_in_dim(v, half, 64, 1)
-        owned = [oq, oo.T, cut(ou), cut(od)]
-        grads = [gq, go.T, cut(gu), cut(gd)]
-        moments = [qkv_moment, out_moment, up_moment, down_moment]
-        new_moments = [
-            momentum_decay * moments[index] + clip * grads[index].astype(jnp.float32)
-            for index in range(4)
-        ]
-    else:
-        (owned, new_moments, vector_sum, grad_norm, clip) = general_update(
-            whole_qkv, whole_out, up_grad, down_grad, vector_part,
-            qkv_moment, out_moment, up_moment, down_moment,
-        )
+    (owned, new_moments, vector_sum, grad_norm, clip) = general_update(
+        whole_qkv, whole_out, up_grad, down_grad, vector_part,
+        qkv_moment, out_moment, up_moment, down_moment,
+    )
     weights = [qkv_weight, out_weight, up_weight, down_weight]
     factors = [
         math.sqrt(3.0),
@@ -646,8 +1198,9 @@
         P(None, ("dp", "head")),
         P(None, ("dp", "head")),
     )
+    fast = mesh.shape["dp"] == 8 and mesh.shape["head"] == 4
     return jax.shard_map(
-        shards,
+        fast_shards if fast else general_shards,
         mesh=mesh,
         in_specs=placed,
         out_specs=(

time: 477 us -> 224 us (0.47); the launches traced: 467 us -> 222 us
  waiting for transfers between devices: 97.6 us -> 0 us
  Pallas kernels: 131 us -> 216 us
  matrix products: 75.4 us -> 0 us
  local copies, waits for them, and re-layouts: 77 us -> 5.9 us
  other arithmetic: 50.7 us -> 0 us
  blocking collectives: 19 us -> 0 us
  between operations: 15.2 us -> 0.67 us
    all_gather x6 -> x0, waiting for transfers between devices: 97.5 us -> none  [the longest x1 47.9 us: shards(): lax.all_gather(down_weight.astype(jnp.bfloat16), everywhere, axis=1, tile...]
    pallas_call x1 -> x2, Pallas kernels: 131 us -> 216 us  [the longest x1 212 us: layer_call(): pl.pallas_call(layer_kernel, out_shape=outs, in_specs=[vmem] * len(args),...]
    dot_general x26 -> x0, matrix products: 75.4 us -> none  [the longest x1 10.8 us: shards(): hidden = jnp.dot(second_low, up_all, preferred_element_type=jnp.float32)]
    unnamed x126 -> x6, local copies, waits for them, and re-layouts: 27.2 us -> 2.3 us
    all_gather x2 -> x0, blocking collectives: 19 us -> none  [the longest x1 11.3 us: shards(): lax.all_gather(out_weight.astype(jnp.bfloat16), 'head', axis=0, tiled=True)]
    while x30 -> x0, local copies, waits for them, and re-layouts: 18.1 us -> none  [the longest x2 7.66 us: shards(): lax.map(attend_backward, (query, keys, values, segment_rows, context_grad...]
    add x8 -> x0, other arithmetic: 14.9 us -> none  [the longest x4 8.79 us: shards(): momentum_decay * moments[index] + clip * grads[index].astype(jnp.float32)]
    convert_element_type x10 -> x0, other arithmetic: 12.5 us -> none  [the longest x2 5.3 us: attend_backward(): score_grad = (probs * (probs_grad - inner)).astype(jnp.bfloat16)]
  transfers between devices with their start and end apart: 6 -> 0, of which waited for: 4 -> 0; matrix products, arithmetic and copies ran while one was open for 32% -> 0% of each run, Pallas kernels for 0% -> 0%
where the time goes in v2:
time: 224 us; the launch traced here: 222 us
  Pallas kernels  216 us (96%)
  local copies, waits for them, and re-layouts  5.9 us (3%)
    pallas_call x1, Pallas kernels, layer_call(): pl.pallas_call(layer_kernel, out_shape=outs, in_specs=[vmem] * len(args),...  212 us

profile of v2, /device:TPU:19, one launch (start us, length us, event | category | flops | bytes accessed | tf_op | source)
XLA Modules:
  0.0 222.5 jit_solution(7267414986416364561)
XLA Ops:
  0.6 0.7 dynamic_slice.3
  1.3 0.6 reshape.31.seg_row
  1.9 1.0 copy.28.seg_col
  3.0 212.1 %layer.1 = (bf16[1024,512]{1,0:T(8,128)(2,1)}, f32[1024,512]{1,0:T(8,128)}, bf16[512,512]{1,0:T(8,128)(2,1)}, bf16[512,128]{1,0:T(8,128)(2,1)}, bf16[512,128]{1,...) custom-call(bf16[1024,512]{1,0:T(8,128)(2,1)} %tokens.1, ...), custom_call_target="tpu_custom_call" | custom-call | tf_op jit(solution)/shard_map/layer/pallas_call | solution.py:892
  215.1 0.0 copy-start.1
  215.1 1.3 slice.3
  216.4 0.0 copy-start
  216.4 3.8 %update.1 = (f32[512,384]{1,0:T(8,128)}, f32[512,384]{1,0:T(8,128)}, f32[128,512]{1,0:T(8,128)}, f32[128,512]{1,0:T(8,128)}, f32[64,512]{1,0:T(8,128)}, /*index=...) custom-call(bf16[512,512]{1,0:T(8,128)(2,1)} %get-tuple-element.39.s, ...), custom_call_target="tpu_custom_call" | custom-call | tf_op jit(solution)/shard_map/update/pallas_call | solution.py:357
  220.2 0.0 copy-done.1
  220.2 1.0 copy.31
  221.2 0.0 copy-done
  221.2 1.3 copy.32
Async XLA Ops:
  215.1 5.1 %copy-start.1 = (bf16[1024,512]{1,0:T(8,128)(2,1)S(1)}, bf16[1024,512]{1,0:T(8,128)(2,1)}, u32[]{:S(2)}) copy-start(bf16[1024,512]{1,0:T(8,128)(2,1)} %get-tuple-element.72) | copy-start | bytes 3145732
  216.4 4.8 %copy-start = (f32[1024,512]{1,0:T(8,128)S(1)}, f32[1024,512]{1,0:T(8,128)}, u32[]{:S(2)}) copy-start(f32[1024,512]{1,0:T(8,128)} %get-tuple-element.73) | copy-start | bytes 6291460

commit v3 on v2

--- a/solution.py
+++ b/solution.py
@@ -156,13 +156,15 @@
     each(ROWS // TILE, body)
 
 
-def bias_phase(seg_col, seg_row, bias):
-    def body(i):
-        here = rows_at(i, 128)
-        row = seg_row[pl.ds(i // 4, 1), :]
-        bias[here, :] = jnp.where(seg_col[here, :] == row, 0.0, neg_fill).astype(LOW)
-
-    each(ROWS // 128, body)
+def bias_phase(segments, head, bias):
+    turned = segments[...].astype(F32).T
+    lane = lax.broadcasted_iota(jnp.int32, (1, segments.shape[0]), 1)
+
+    for seq in range(ROWS // SEQ):
+        which = head * (ROWS // SEQ) + seq
+        row = segments[pl.ds(which, 1), :].astype(F32)
+        column = jnp.sum(jnp.where(lane == which, turned, 0.0), axis=1, keepdims=True)
+        bias[seq * SEQ : seq * SEQ + SEQ, :] = jnp.where(column == row, 0.0, neg_fill).astype(LOW)
 
 
 def attend_phase(pair, mixed, bias, probs, context):
@@ -276,64 +278,60 @@
 
 def out_phase(attended_t, context, g_attend):
     def body(i):
-        grad = dot(attended_t[rows_at(i, 256), :], context[...]).astype(LOW)
-        for j in range(4):
-            for p in range(PAIRS):
-                g_attend[i * 16 + j * 4 + p, :, 384:512] = grad[
-                    j * 64 : j * 64 + 64, p * 128 : p * 128 + 128
-                ]
+        here = rows_at(i, 256)
+        grad = dot(attended_t[here, :], context[...]).astype(LOW)
+        for p in range(PAIRS):
+            g_attend[p, here, 384:512] = grad[:, p * 128 : p * 128 + 128]
 
     each(2, body)
 
 
-def attend_back_phase(pair, mixed, probs, context_grad, pair_grad):
+def attend_back_phase(pair, seq, mixed, probs, context_grad, pair_grad):
     lane = lax.broadcasted_iota(jnp.int32, (1, 128), 1)
     left = (lane < HEAD_DIM).astype(LOW)
     scale = HEAD_DIM ** (-0.5)
 
-    def body(seq):
-        here = rows_at(seq, SEQ)
-        query = mixed[pair, here, 0:128]
-        keys = mixed[pair, here, 128:256]
-        values = mixed[pair, here, 256:384]
-        upper = context_grad[here, pl.ds(pl.multiple_of(pair * 128, 128), 128)]
-        outs = []
-        for half in range(2):
-            mask = left if half == 0 else LOW(1.0) - left
-            above = upper * mask
-            prob_low = probs[pair * 4 + half * 2 + seq]
-            prob = prob_low.astype(F32)
-            prob_grad = dot_back(above, values)
-            inner = jnp.sum(prob * prob_grad, axis=-1, keepdims=True)
-            score_grad = (prob * (prob_grad - inner)).astype(LOW)
-            outs.append(
-                (
-                    dot(score_grad, keys),
-                    dot_rows(score_grad, query),
-                    dot_rows(prob_low, above),
-                )
+    here = rows_at(seq, SEQ)
+    query = mixed[pair, here, 0:128]
+    keys = mixed[pair, here, 128:256]
+    values = mixed[pair, here, 256:384]
+    upper = context_grad[here, pl.ds(pl.multiple_of(pair * 128, 128), 128)]
+    outs = []
+    for half in range(2):
+        mask = left if half == 0 else LOW(1.0) - left
+        above = upper * mask
+        prob_low = probs[pair * 4 + half * 2 + seq]
+        prob = prob_low.astype(F32)
+        prob_grad = dot_back(above, values)
+        inner = jnp.sum(prob * prob_grad, axis=-1, keepdims=True)
+        score_grad = (prob * (prob_grad - inner)).astype(LOW)
+        outs.append(
+            (
+                dot(score_grad, keys),
+                dot_rows(score_grad, query),
+                dot_rows(prob_low, above),
             )
-        pick = lane < HEAD_DIM
-        pair_grad[here, 0:128] = (jnp.where(pick, outs[0][0], outs[1][0]) * scale).astype(LOW)
-        pair_grad[here, 128:256] = (jnp.where(pick, outs[0][1], outs[1][1]) * scale).astype(LOW)
-        pair_grad[here, 256:384] = (outs[0][2] + outs[1][2]).astype(LOW)
-
-    each(ROWS // SEQ, body)
-
-
-def qkv_phase(pair, pair_grad, first_t, wqkv, g_attend, first_grad):
+        )
+    pick = lane < HEAD_DIM
+    pair_grad[here, 0:128] = (jnp.where(pick, outs[0][0], outs[1][0]) * scale).astype(LOW)
+    pair_grad[here, 128:256] = (jnp.where(pick, outs[0][1], outs[1][1]) * scale).astype(LOW)
+    pair_grad[here, 256:384] = (outs[0][2] + outs[1][2]).astype(LOW)
+
+
+def qkv_phase(pair, pair_grad, first_t, g_attend):
+    def body(i):
+        here = rows_at(i, 256)
+        g_attend[pair, here, 0:384] = dot(first_t[here, :], pair_grad[...]).astype(LOW)
+
+    each(2, body)
+
+
+def first_grad_phase(pair, pair_grad, wqkv, first_grad):
     def body(i):
         here = rows_at(i, TILE)
         first_grad[here, :] += dot_back(pair_grad[here, :], wqkv[pair])
 
     each(ROWS // TILE, body)
-
-    def grads(i):
-        grad = dot(first_t[rows_at(i, 256), :], pair_grad[...]).astype(LOW)
-        for j in range(4):
-            g_attend[i * 16 + j * 4 + pair, :, 0:384] = grad[j * 64 : j * 64 + 64, :]
-
-    each(2, grads)
 
 
 def input_phase(params, tokens, first_grad, input_grad, norms):
@@ -457,19 +455,58 @@
     return jnp.concatenate(parts, axis=1)
 
 
+class Slots:
+    def __init__(self):
+        self.used = 0
+
+    def __call__(self, count):
+        start = self.used
+        self.used += count
+        return start
+
+
+def update_step(pool, now, later, count, blocks, lanes, gram, mix):
+    def gram_body(i):
+        rows = rows_at(i, TILE)
+        total = dot_back(pool[now, rows, :], pool[now])
+        for b in range(1, count):
+            total = total + dot_back(pool[now + b, rows, :], pool[now + b])
+        gram[rows, :] = total.astype(LOW)
+
+    each(512 // TILE, gram_body)
+
+    def mix_body(i):
+        rows = rows_at(i, TILE)
+        own = gram[rows, :]
+        mix[rows, :] = (ns_b * own.astype(F32) + ns_c * dot(own, gram[...])).astype(LOW)
+
+    each(512 // TILE, mix_body)
+
+    def next_body(i):
+        b = blocks[0] + i
+        value = pool[now + b, :, lanes]
+        pool[later + b, :, lanes] = (ns_a * value.astype(F32) + dot(mix[...], value)).astype(LOW)
+
+    each(blocks[1], next_body)
+
+
 def layer_kernel(
-    tokens, seg_col, seg_row, out_grad, params, w_qkv, m_qkv, w_out, m_out, w_up, m_up, w_down, m_down,
+    tokens, segments, out_grad, params, w_qkv, m_qkv, w_out, m_out, w_up, m_up, w_down, m_down,
     layer_out, input_grad, start_a, start_u, start_d, ortho_q, ortho_o, ortho_u, ortho_d, norm_sum, scal,
     first, mixed, context, bias, wqkv, wout, wup, wdown, pool, middle, second, second_t, out_grad_t,
     active, hidden_grad, result, second_grad, pair_grad, acc_a, acc_u, acc_d, got_a, got_u, got_d,
-    mom_t, mom_x, mom_u, mom_d, mom_a, norm_now, norm_got, stat_got, gram, mix, send, recv,
+    mom_full, mom_x, mom_u, mom_d, mom_a, norm_got, stat_got, gram, mix, send, recv,
 ):
     dp, head, bits, peers = coordinates()
     me = dp * 4 + head
+    sibling = peers["c"]
+    across = (dp, 3 - head)
     sems = (send, recv)
-    across = (dp, 3 - head)
-    S_Q, S_O, S_M, S_UP, S_DOWN, S_CHUNK, S_LG, S_A, S_NORM, S_STAT, S_START, S_ORTHO = (
-        0, 4, 8, 10, 15, 20, 44, 48, 53, 58, 59, 74
+    slots = Slots()
+    S_Q, S_O, S_M, S_MA = slots(4), slots(4), slots(2), slots(4)
+    S_UP, S_DOWN, S_CHUNK, S_LG = slots(5), slots(5), slots(24), slots(4)
+    S_A, S_NORM, S_STAT, S_START, S_SIDE, S_ORTHO = (
+        slots(20), slots(1), slots(1), slots(15), slots(2), slots(8)
     )
     barrier = pltpu.get_barrier_semaphore()
 
@@ -496,7 +533,6 @@
     def weight_copy(block, who, slot, peer):
         return remote(block(who), block(who), send.at[slot], recv.at[slot], peer)
 
-    sibling = peers["c"]
     weight_copy(block_q, head, S_Q + 1, sibling).start()
     weight_copy(block_q, head, S_Q + 2, peers["x"]).start()
     gather_start(wup, 64, (), GATHER_UP[0], bits, peers[GATHER_UP[0]], sems, S_UP)
@@ -520,9 +556,29 @@
                 )
 
     first_phase(tokens, params, first)
-    bias_phase(seg_col, seg_row, bias)
+    bias_phase(segments, head, bias)
     weight_step(0)
     turn_phase(out_grad, out_grad_t)
+    mom_full[:, 0:384] = paired(m_qkv[...])
+    mom_full[:, 384:512] = m_out[...].T
+
+    def rank_of(c, x):
+        return c * 16 + x * 8 + bits["y"] * 4 + bits["l"] * 2 + bits["g"]
+
+    def rank_rows(who):
+        return pl.ds(pl.multiple_of(rank_of(who % 2, who // 2) * 16, 16), 16)
+
+    partners = (sibling, peers["x"], across)
+
+    def rows_copy(j):
+        who = partners[j][1]
+        return remote(
+            mom_full.at[rank_rows(who)], mom_a.at[head], send.at[S_MA + j], recv.at[S_MA + j], partners[j]
+        )
+
+    for j in range(3):
+        rows_copy(j).start()
+    mom_a[head] = mom_full[rank_rows(head), :]
 
     def pair_body(j):
         pair = (bits["c"] + j % 2) % 2 + 2 * ((bits["x"] + j // 2) % 2)
@@ -602,19 +658,17 @@
             chunk_end(q - 3, 2)
 
     each(WIDE // CHUNK, feed_body)
+    middle_phase(
+        params, middle, result, second_grad, out_grad, wout,
+        layer_out, input_grad, second, active, norm_got.at[me],
+    )
     chunk_end(3, 0)
     chunk_start(3, 1)
-    middle_phase(
-        params, middle, result, second_grad, out_grad, wout,
-        layer_out, input_grad, second, active, norm_now.at[0],
-    )
     chunk_end(2, 1)
     chunk_start(2, 2)
+    chunk_end(1, 2)
     turn_phase(second, second_t)
     out_phase(second_t, context, acc_a)
-    chunk_end(1, 2)
-    chunk_end(3, 1)
-    chunk_start(3, 2)
     turn_phase(first, second_t)
     result[...] = jnp.zeros_like(result)
 
@@ -632,79 +686,153 @@
                 acc, got, 28 + 2 * k, fixed, name, free, bits, peers[name], sems, S_LG + 2 * k + i
             )
 
+    spans = []
+    low_row = 0
+    for k, name in enumerate(ATTEND_ORDER):
+        size = 256 >> k
+        spans.append((name, size, low_row + bits[name] * size, low_row + (1 - bits[name]) * size))
+        low_row = low_row + bits[name] * size
+
+    def aligned(row, size):
+        return pl.ds(pl.multiple_of(row, 16), size)
+
+    def attend_copy(pair, k):
+        name, size, _, give = spans[k]
+        return remote(
+            acc_a.at[pair, aligned(give, size)], got_a.at[pair, pl.ds(512 - 2 * size, size)],
+            send.at[S_A + pair * 5 + k], recv.at[S_A + pair * 5 + k], peers[name],
+        )
+
+    def attend_start(pair, k):
+        attend_copy(pair, k).start()
+
+    def attend_next(pair, k, more=True):
+        attend_copy(pair, k).wait()
+        _, size, keep, _ = spans[k]
+        step = min(size, 64)
+
+        def body(i):
+            here = aligned(keep + i * step, step)
+            come = aligned(512 - 2 * size + i * step, step)
+            acc_a[pair, here, :] = (
+                acc_a[pair, here, :].astype(F32) + got_a[pair, come, :].astype(F32)
+            ).astype(LOW)
+
+        each(size // step, body)
+        if k < 4:
+            attend_start(pair, k + 1)
+
+    def at(wanted, pair):
+        return pl.when(pair == wanted)
+
     def back_body(pair):
-        attend_back_phase(pair, mixed, pool, active, pair_grad)
-        qkv_phase(pair, pair_grad, second_t, wqkv, acc_a, result)
-
-        @pl.when(pair == 0)
+        attend_back_phase(pair, 0, mixed, pool, active, pair_grad)
+
+        @at(0, pair)
         def _():
+            chunk_end(3, 1)
+            chunk_start(3, 2)
             chunk_end(2, 2)
+
+        @at(1, pair)
+        def _():
+            attend_next(0, 0)
+
+        @at(2, pair)
+        def _():
+            attend_next(1, 0)
+            attend_next(0, 1)
+
+        @at(3, pair)
+        def _():
+            attend_next(2, 0)
+            attend_next(1, 1)
+            attend_next(0, 3)
+
+        attend_back_phase(pair, 1, mixed, pool, active, pair_grad)
+        qkv_phase(pair, pair_grad, second_t, acc_a)
+        attend_start(pair, 0)
+
+        @at(0, pair)
+        def _():
             chunk_end(3, 2)
             last_step(0, False)
 
-        @pl.when(pair == 1)
+        @at(1, pair)
         def _():
             last_step(0, True)
             last_step(1, False)
 
-        @pl.when(pair == 2)
+        @at(2, pair)
         def _():
             last_step(1, True)
+            attend_next(0, 2)
+
+        first_grad_phase(pair, pair_grad, wqkv, result)
 
     each(PAIRS, back_body)
-
-    def attend_args(k):
-        order = ATTEND_ORDER
-        return {d: bits[d] for d in order[:k]}, order[k], order[k + 1 :]
-
-    def norm_copy(k):
-        return remote(
-            norm_now.at[k], norm_got.at[k], send.at[S_NORM + k], recv.at[S_NORM + k],
-            peers[ATTEND_ORDER[k]],
-        )
-
-    for k in range(5):
-        fixed, name, free = attend_args(k)
-        base = 32 - 2 ** (5 - k)
-        scatter_start(acc_a, got_a, base, fixed, name, free, bits, peers[name], sems, S_A + k)
-        if k == 0:
-            input_phase(params, tokens, result, input_grad, norm_now.at[0])
-            moment_copy(0, m_up).wait()
-            moment_copy(1, m_down).wait()
-            keep = pl.ds(pl.multiple_of(bits["c"] * 256, 256), 256)
-            for i, (ref, out) in enumerate(((m_up, mom_u), (m_down, mom_d))):
-                own = ref[:, keep]
-                far = mom_x[i]
-                low_half = jnp.where(bits["c"] == 0, own, far)
-                high_half = jnp.where(bits["c"] == 0, far, own)
-                out[...] = jnp.concatenate([low_half, high_half], axis=0).T
-            mom_t[...] = m_out[...].T
-            here = pl.ds(pl.multiple_of(dp * 64, 64), 64)
-            mom_a[:, 0:384] = paired(m_qkv[here, :])
-            mom_a[:, 384:512] = mom_t[here, :]
-        norm_copy(k).start()
-        scatter_end(acc_a, got_a, base, fixed, name, free, bits, peers[name], sems, S_A + k)
-        norm_copy(k).wait()
-        norm_now[k + 1] = norm_now[k] + norm_got[k]
+    attend_next(3, 0)
+    attend_next(2, 1)
+    attend_next(1, 2)
+    attend_next(0, 4)
+    input_phase(params, tokens, result, input_grad, norm_got.at[me])
+
+    def tell_norm(i):
+        other = (me + 1 + i) % 32
+        remote(
+            norm_got.at[me], norm_got.at[me], send.at[S_NORM], recv.at[S_NORM], (other // 4, other % 4)
+        ).start()
+
+    attend_next(3, 1)
+    each(31, tell_norm)
+    attend_next(2, 2)
+    attend_next(1, 3)
+    moment_copy(0, m_up).wait()
+    moment_copy(1, m_down).wait()
+    keep_half = pl.ds(pl.multiple_of(bits["c"] * 256, 256), 256)
+    for i, (ref, out) in enumerate(((m_up, mom_u), (m_down, mom_d))):
+        own = ref[:, keep_half]
+        far = mom_x[i]
+        low_half = jnp.where(bits["c"] == 0, own, far)
+        high_half = jnp.where(bits["c"] == 0, far, own)
+        out[...] = jnp.concatenate([low_half, high_half], axis=0).T
+    for j in range(3):
+        rows_copy(j).wait()
 
     def total_of(value):
         return jnp.sum(jnp.sum(value, axis=0, keepdims=True), axis=1, keepdims=True)
 
     lane = lax.broadcasted_iota(jnp.int32, (8, 128), 1)
     column = lax.broadcasted_iota(jnp.int32, (1, 512), 1)
-    grad_a = acc_a[me].astype(F32)
     grad_u = acc_u[me].astype(F32)
     grad_d = acc_d[me].astype(F32)
     stats = jnp.zeros((8, 128), F32)
-    products = []
-    for moment, grad in ((mom_a[...], grad_a), (mom_u[...], grad_u), (mom_d[...], grad_d)):
-        products.append((moment * moment, moment * grad, grad * grad))
+    for m, (moment, grad) in enumerate(((mom_u[...], grad_u), (mom_d[...], grad_d))):
+        for i, product in enumerate((moment * moment, moment * grad, grad * grad)):
+            stats = jnp.where(lane == 6 + 3 * m + i, total_of(product), stats)
+    attend_next(3, 2)
+    attend_next(2, 3)
+    attend_next(1, 4)
+    attend_next(3, 3)
+    attend_next(2, 4)
+    span = norm_got.at[pl.ds(0, 31)]
+    remote(span, span, send.at[S_NORM], recv.at[S_NORM], sibling).wait()
+    vector = norm_got[0]
+    for i in range(1, 32):
+        vector = vector + norm_got[i]
+    norm_sum[...] = vector
+    vector_total = total_of(vector * vector)
+    attend_next(3, 4)
+    my_rows = aligned(low_row, 16)
     for i in range(3):
-        inside = column < 384
-        stats = jnp.where(lane == i, total_of(jnp.where(inside, products[0][i], 0.0)), stats)
-        stats = jnp.where(lane == 3 + i, total_of(jnp.where(inside, 0.0, products[0][i])), stats)
-        stats = jnp.where(lane == 6 + i, total_of(products[1][i]), stats)
-        stats = jnp.where(lane == 9 + i, total_of(products[2][i]), stats)
+        inside = jnp.zeros((1, 512), F32)
+        for pair in range(PAIRS):
+            moment = mom_a[pair]
+            grad = acc_a[pair, my_rows, :].astype(F32)
+            product = (moment * moment, moment * grad, grad * grad)[i]
+            inside = inside + jnp.sum(product, axis=0, keepdims=True)
+        stats = jnp.where(lane == i, total_of(jnp.where(column < 384, inside, 0.0)), stats)
+        stats = jnp.where(lane == 3 + i, total_of(jnp.where(column < 384, 0.0, inside)), stats)
     stat_got[me] = stats
 
     def tell(i):
@@ -721,9 +849,7 @@
     def stat(i):
         return jnp.sum(jnp.where(lane == i, stats, 0.0), axis=1, keepdims=True)[0:1]
 
-    vector = norm_now[5]
-    norm_sum[...] = vector
-    norm = jnp.sqrt(stat(2) + stat(5) + stat(8) + stat(11) + total_of(vector * vector))
+    norm = jnp.sqrt(stat(2) + stat(5) + stat(8) + stat(11) + vector_total)
     clip = jnp.minimum(1.0, 1.0 / (norm + 1e-06))
     sizes = []
     for m in range(4):
@@ -738,110 +864,172 @@
         told = jnp.where(lane == 2 + m, sizes[m], told)
     scal[...] = told
     scale_a = jnp.where(column < 384, 1.0 / sizes[0], 1.0 / sizes[1])
-    got_a[me] = ((momentum_decay * mom_a[...] + clip * grad_a) * scale_a).astype(LOW)
     got_u[me] = ((momentum_decay * mom_u[...] + clip * grad_u) * (1.0 / sizes[2])).astype(LOW)
     got_d[me] = ((momentum_decay * mom_d[...] + clip * grad_d) * (1.0 / sizes[3])).astype(LOW)
-
-    starts = (got_a, got_u, got_d)
-    for k in range(5):
-        for m in range(3):
-            order = STARTS[m]
+    for pair in range(PAIRS):
+        grad = acc_a[pair, my_rows, :].astype(F32)
+        pool[pair, my_rows, :] = ((momentum_decay * mom_a[pair] + clip * grad) * scale_a).astype(LOW)
+
+    mine_half = pl.ds(pl.multiple_of(bits["c"] * 256, 256), 256)
+
+    def side_copy(i):
+        src, dst = ((got_u, start_u), (got_d, start_d))[i]
+        return remote(
+            src.at[me], dst.at[mine_half], send.at[S_SIDE + i], recv.at[S_SIDE + i], sibling
+        )
+
+    side_copy(0).start()
+    side_copy(1).start()
+    start_u[mine_half, :] = got_u[me]
+    start_d[mine_half, :] = got_d[me]
+
+    def start_copy(k):
+        name, size, keep, _ = spans[4 - k]
+        part = pool.at[pl.ds(0, 4), aligned(keep, size)]
+        return remote(part, part, send.at[S_START + 3 * k], recv.at[S_START + 3 * k], peers[name])
+
+    tiles = ((got_u, STARTS[1]), (got_d, STARTS[2]))
+    for k in range(4):
+        start_copy(k).start()
+        for m, (got, order) in enumerate(tiles):
             gather_start(
-                starts[m], 0, order[:k], order[k], bits, peers[order[k]], sems, S_START + 3 * k + m
+                got, 0, order[:k], order[k], bits, peers[order[k]], sems, S_START + 3 * k + 1 + m
             )
-        for m in range(3):
-            order = STARTS[m]
-            gather_end(starts[m], 0, order[:k], peers[order[k]], sems, S_START + 3 * k + m)
-
-    @pl.when(head < 2)
+        start_copy(k).wait()
+        for m, (got, order) in enumerate(tiles):
+            gather_end(got, 0, order[:k], peers[order[k]], sems, S_START + 3 * k + 1 + m)
+    half_rows = aligned(spans[0][2], 256)
+    pair_part = pool.at[pl.ds(head + 1 - 2 * bits["c"], 1), half_rows]
+    all_part = pool.at[pl.ds(0, 4), half_rows]
+
+    def core_copy(part):
+        return remote(part, part, send.at[S_START + 12], recv.at[S_START + 12], sibling)
+
+    @pl.when(bits["c"] == 1)
     def _():
-        wanted = jnp.where(head == 0, 1.0, 0.0)
-        here_only = jnp.where(column < 384, wanted, 1.0 - wanted).astype(LOW)
+        core_copy(all_part).start()
+
+        def slice_body(i):
+            rows = rows_at(i, 256)
+            start_a[rows, :] = pool[head, rows, :]
+
+        for x, (got, order) in enumerate(tiles):
+            @pl.when(bits["x"] == x)
+            def _(got=got, order=order, x=x):
+                span = got.at[pl.ds(0, 16)]
+                remote(span, span, send.at[S_START + 13], recv.at[S_START + 13], sibling).wait_recv()
+
+                def body(i):
+                    for j in range(4):
+                        for c in range(2):
+                            pool[4 + i, c * 256 : c * 256 + 256, j * 128 : j * 128 + 128] = got[
+                                i * 8 + j * 2 + c
+                            ]
+
+                each(4, body)
+
+        core_copy(pair_part).wait_recv()
+        core_copy(all_part).wait_send()
+        each(2, slice_body)
+
+    @pl.when(bits["c"] == 0)
+    def _():
+        for x, (got, order) in enumerate(tiles):
+            @pl.when(bits["x"] == x)
+            def _(got=got, order=order):
+                gather_start(got, 0, order[:4], "c", bits, sibling, sems, S_START + 13)
+
+        core_copy(pair_part).start()
+        core_copy(all_part).wait_recv()
 
         def body(i):
-            rows = pl.ds(pl.multiple_of((i // 4) * 64, 64), 64)
-            pool[i % 4, rows, :] = got_a[i] * here_only
-
-        each(32, body)
-
-    for kind, got in ((2, got_u), (3, got_d)):
-        @pl.when(head == kind)
-        def _(got=got):
-            def body(i):
-                for j in range(4):
-                    for c in range(2):
-                        pool[i, c * 256 : c * 256 + 256, j * 128 : j * 128 + 128] = got[i * 8 + j * 2 + c]
-
-            each(4, body)
-
-    def slice_body(i):
-        rows = pl.ds(pl.multiple_of(i * 64, 64), 64)
-        start_a[rows, :] = got_a[i * 4 + head]
-
-    each(8, slice_body)
-    left = me - bits["c"]
-    for c in range(2):
-        start_u[c * 256 : c * 256 + 256, :] = got_u[left + c]
-        start_d[c * 256 : c * 256 + 256, :] = got_d[left + c]
-
-    def turn_body(turn):
-        now = (turn % 2) * 4
-        later = 4 - now
-
-        def gram_body(i):
-            rows = rows_at(i, TILE)
-            total = dot_back(pool[now, rows, :], pool[now])
-            for b in range(1, 4):
-                total = total + dot_back(pool[now + b, rows, :], pool[now + b])
-            gram[rows, :] = total.astype(LOW)
-
-        each(512 // TILE, gram_body)
-
-        def mix_body(i):
-            rows = rows_at(i, TILE)
-            own = gram[rows, :]
-            mix[rows, :] = (ns_b * own.astype(F32) + ns_c * dot(own, gram[...])).astype(LOW)
-
-        each(512 // TILE, mix_body)
-
-        def next_body(b):
-            value = pool[now + b]
-            pool[later + b] = (ns_a * value.astype(F32) + dot(mix[...], value)).astype(LOW)
-
-        each(4, next_body)
-
-    each(NS_STEPS, turn_body)
-    last = (NS_STEPS % 2) * 4
-    outs = (ortho_q, ortho_o, ortho_u, ortho_d)
-
-    def piece(kind, who):
-        if kind == 0:
-            return pool.at[last + who, :, pl.ds(0, 384)]
-        if kind == 1:
-            return pool.at[last + who, :, pl.ds(384, 128)]
-        block = dp * 2 + who // 2
-        return pool.at[last + block // 4, :, pl.ds(pl.multiple_of((block % 4) * 128, 128), 128)]
-
-    partners = (peers["c"], peers["x"], across)
-    for kind in range(4):
-        @pl.when(head == kind)
-        def _(kind=kind):
-            for j, partner in enumerate(partners):
-                remote(
-                    piece(kind, partner[1]), outs[kind], send.at[S_ORTHO + j], recv.at[S_ORTHO + kind], partner
-                ).start()
-            outs[kind][...] = piece(kind, head)[...]
-            for j, partner in enumerate(partners):
-                remote(
-                    piece(kind, partner[1]), outs[kind], send.at[S_ORTHO + j], recv.at[S_ORTHO + kind], partner
-                ).wait_send()
-
-    for kind in range(4):
-        @pl.when(head != kind)
-        def _(kind=kind):
-            remote(
-                piece(kind, head), outs[kind], send.at[S_ORTHO], recv.at[S_ORTHO + kind], sibling
-            ).wait_recv()
+            rows = rows_at(i, 256)
+            start_a[rows, :] = pool[head, rows, :]
+            for p in range(PAIRS):
+                for r in range(3):
+                    group = p * 3 + r
+                    pool[4 + group // 4, rows, (group % 4) * 128 : (group % 4) * 128 + 128] = pool[
+                        p, rows, r * 128 : r * 128 + 128
+                    ]
+                pool[7, rows, p * 128 : p * 128 + 128] = pool[p, rows, 384:512]
+
+        each(2, body)
+        core_copy(pair_part).wait_send()
+        span = got_u.at[pl.ds(0, 16)]
+        remote(span, span, send.at[S_START + 13], recv.at[S_START + 13], sibling).wait_send()
+
+    side_copy(0).wait()
+    side_copy(1).wait()
+
+    every = pl.ds(0, 512)
+    outs = (ortho_u, ortho_d)
+
+    def out_copy(src, dst, i, peer):
+        return remote(src, dst, send.at[S_ORTHO + i], recv.at[S_ORTHO + i], peer)
+
+    def group_of(r):
+        group = bits["x"] * 6 + r
+        return pool.at[8 + group // 4, :, pl.ds(pl.multiple_of((group % 4) * 128, 128), 128)]
+
+    def out_of(who):
+        return pool.at[11, :, pl.ds(pl.multiple_of(who * 128, 128), 128)]
+
+    @pl.when(bits["c"] == 0)
+    def _():
+        def turn_body(turn):
+            now = 4 + (turn % 2) * 4
+            later = 12 - now
+            update_step(pool, now, later, 3, (0, 3), every, gram, mix)
+            update_step(pool, now + 3, later + 3, 1, (0, 1), every, gram, mix)
+
+        each(NS_STEPS - 1, turn_body)
+        update_step(pool, 4, 8, 3, (bits["x"], 2), every, gram, mix)
+        for r in range(3):
+            out_copy(group_of(3 + r), ortho_q.at[:, pl.ds(r * 128, 128)], 0, sibling).start()
+        for r in range(3):
+            ortho_q[:, r * 128 : r * 128 + 128] = group_of(r)[...]
+        columns = pl.ds(pl.multiple_of(bits["x"] * 256, 256), 256)
+        update_step(pool, 7, 11, 1, (0, 1), columns, gram, mix)
+        out_copy(out_of(head + 1), ortho_o, 1, sibling).start()
+        ortho_o[...] = out_of(head)[...]
+        out_copy(ortho_q, ortho_q, 0, sibling).wait_send()
+        out_copy(ortho_o, ortho_o, 1, sibling).wait_send()
+
+    @pl.when(bits["c"] == 1)
+    def _():
+        def turn_body(turn):
+            now = 4 + (turn % 2) * 4
+            update_step(pool, now, 12 - now, 4, (0, 4), every, gram, mix)
+
+        each(NS_STEPS - 1, turn_body)
+        wanted = dp // 2
+        update_step(pool, 4, 8, 4, (wanted, 1), every, gram, mix)
+
+        def block_of(x):
+            block = dp * 2 + x
+            return pool.at[8 + wanted, :, pl.ds(pl.multiple_of((block % 4) * 128, 128), 128)]
+
+        for x in range(2):
+            @pl.when(bits["x"] == x)
+            def _(x=x):
+                targets = ((across, 1 - x), (peers["x"], 1 - x), (sibling, x))
+                for j, (peer, side) in enumerate(targets):
+                    remote(
+                        block_of(side), outs[x], send.at[S_ORTHO + 2 + j], recv.at[S_ORTHO + 2 + x], peer
+                    ).start()
+                outs[x][...] = block_of(x)[...]
+                for j, (peer, side) in enumerate(targets):
+                    remote(
+                        block_of(side), outs[x], send.at[S_ORTHO + 2 + j], recv.at[S_ORTHO + 2 + x], peer
+                    ).wait_send()
+
+        out_copy(ortho_q, ortho_q, 0, sibling).wait_recv()
+        out_copy(ortho_o, ortho_o, 1, sibling).wait_recv()
+
+    for x in range(2):
+        @pl.when(head != 2 * x + 1)
+        def _(x=x):
+            out_copy(outs[x], outs[x], 2 + x, sibling).wait_recv()
 
 
 def layer_call(*args):
@@ -872,19 +1060,18 @@
         ((ROWS, 512), F32),
         ((ROWS, 512), F32),
         ((ROWS, 384), LOW),
-        ((32, 64, 512), LOW),
+        ((PAIRS, 512, 512), LOW),
         ((32, 256, 128), LOW),
         ((32, 256, 128), LOW),
-        ((32, 64, 512), LOW),
+        ((PAIRS, 512, 512), LOW),
         ((32, 256, 128), LOW),
         ((32, 256, 128), LOW),
-        ((512, 128), F32),
+        ((512, 512), F32),
         ((2, 64, 256), F32),
         ((256, 128), F32),
         ((256, 128), F32),
-        ((64, 512), F32),
-        ((6, 4, 512), F32),
-        ((5, 4, 512), F32),
+        ((PAIRS, 16, 512), F32),
+        ((32, 4, 512), F32),
         ((32, 8, 128), F32),
         ((512, 512), LOW),
         ((512, 512), LOW),
@@ -895,7 +1082,7 @@
         in_specs=[vmem] * len(args),
         out_specs=(vmem,) * len(outs),
         scratch_shapes=[pltpu.VMEM(*v) for v in scratch]
-        + [pltpu.SemaphoreType.DMA((80,)), pltpu.SemaphoreType.DMA((80,))],
+        + [pltpu.SemaphoreType.DMA((104,)), pltpu.SemaphoreType.DMA((104,))],
         compiler_params=pltpu.CompilerParams(
             collective_id=1, has_side_effects=True, vmem_limit_bytes=VMEM_BYTES
         ),
@@ -906,7 +1093,7 @@
 def update_kernel(
     start_a, start_u, start_d, ortho_q, ortho_o, ortho_u, ortho_d, norm_sum, scal,
     w_qkv, w_out, w_up, w_down, norm_first, norm_second,
-    new_q, mom_q, new_o, mom_o, new_u, mom_u, new_d, mom_d, clipped, first_new, second_new,
+    new_q, mom_q, new_o, mom_o, new_u, mom_u, new_d, mom_d, clipped, first_new, second_new, norm,
 ):
     core = lax.axis_index("head") % 2
     clip = scal[0:1, 1:2]
@@ -928,6 +1115,7 @@
         new[...] = fresh(weight[...], math.sqrt(max(1.0, FF / 512)), turned)
         turned = start[...].astype(F32).T
         mom[...] = jnp.where(core == 0, turned[0:64], turned[64:128]) * scal[0:1, i : i + 1]
+    norm[...] = scal[0:1, 0:1]
     clip_grad = clip * norm_sum[...]
     clipped[...] = clip_grad
     first_new[...] = beta_one * norm_first[...] + (1.0 - beta_one) * clip_grad
@@ -950,18 +1138,17 @@
     down_weight,
     down_moment,
 ):
-    seg = lax.dynamic_slice_in_dim(segments, lax.axis_index("head") * ROWS, ROWS, 0)
     (
         layer_out, input_grad, start_a, start_u, start_d, ortho_q, ortho_o, ortho_u, ortho_d, norm_sum, scal
     ) = layer_call(
-        tokens, seg[:, None], seg.reshape(ROWS // SEQ, SEQ), out_grad, norm_params,
+        tokens, segments.reshape(segments.shape[0] // SEQ, SEQ), out_grad, norm_params,
         qkv_weight, qkv_moment, out_weight, out_moment,
         up_weight.T, up_moment.T, down_weight.T, down_moment.T,
     )
     tall = ((64, 512), F32)
-    new_q, mom_q, new_o, mom_o, new_u, mom_u, new_d, mom_d, clipped, first_new, second_new = local_call(
+    new_q, mom_q, new_o, mom_o, new_u, mom_u, new_d, mom_d, clipped, first_new, second_new, norm = local_call(
         update_kernel,
-        [((512, 384), F32)] * 2 + [((128, 512), F32)] * 2 + [tall] * 4 + [((4, 512), F32)] * 3,
+        [((512, 384), F32)] * 2 + [((128, 512), F32)] * 2 + [tall] * 4 + [((4, 512), F32)] * 3 + [((1, 1), F32)],
         [],
         (
             start_a, start_u, start_d, ortho_q, ortho_o, ortho_u, ortho_d, norm_sum, scal,
@@ -970,7 +1157,7 @@
         "update",
     )
     return (
-        layer_out, input_grad, scal[0, 0], clipped, first_new, second_new,
+        layer_out, input_grad, norm.reshape(()), clipped, first_new, second_new,
         new_q, mom_q, new_o, mom_o, new_u.T, mom_u.T, new_d.T, mom_d.T,
     )
 

time: 224 us -> 196 us (0.88)
  Pallas kernels: 216 us -> 190 us
  local copies, waits for them, and re-layouts: 5.9 us -> 3.63 us
    pallas_call x1, Pallas kernels: 212 us -> 186 us  [layer_call(): pl.pallas_call(layer_kernel, out_shape=outs, in_specs=[vmem] * len(args),...]
where the time goes in v3:
time: 196 us; the launch traced here: 195 us
  Pallas kernels  190 us (97%)
  local copies, waits for them, and re-layouts  3.63 us (2%)
    pallas_call x1, Pallas kernels, layer_call(): pl.pallas_call(layer_kernel, out_shape=outs, in_specs=[vmem] * len(args),...  186 us

profile of v3, /device:TPU:19, one launch (start us, length us, event | category | flops | bytes accessed | tf_op | source)
XLA Modules:
  0.0 194.6 jit_solution(1973442185860500368)
XLA Ops:
  0.6 1.3 reshape.34.segments
  2.0 186.4 %layer.1 = (bf16[1024,512]{1,0:T(8,128)(2,1)}, f32[1024,512]{1,0:T(8,128)}, bf16[512,512]{1,0:T(8,128)(2,1)}, bf16[512,128]{1,0:T(8,128)(2,1)}, bf16[512,128]{1,...) custom-call(bf16[1024,512]{1,0:T(8,128)(2,1)} %tokens.1, ...), custom_call_target="tpu_custom_call" | custom-call | tf_op jit(solution)/shard_map/layer/pallas_call | solution.py:1079
  188.4 0.0 copy-start.1
  188.4 0.0 copy-start
  188.4 3.9 %update.1 = (f32[512,384]{1,0:T(8,128)}, f32[512,384]{1,0:T(8,128)}, f32[128,512]{1,0:T(8,128)}, f32[128,512]{1,0:T(8,128)}, f32[64,512]{1,0:T(8,128)}, /*index=...) custom-call(bf16[512,512]{1,0:T(8,128)(2,1)} %get-tuple-element.39.s, ...), custom_call_target="tpu_custom_call" | custom-call | tf_op jit(solution)/shard_map/update/pallas_call | solution.py:355
  192.3 0.0 copy-done.1
  192.3 1.0 copy.30
  193.3 0.0 copy-done
  193.3 1.3 copy.31
Async XLA Ops:
  188.4 3.9 %copy-start.1 = (bf16[1024,512]{1,0:T(8,128)(2,1)S(1)}, bf16[1024,512]{1,0:T(8,128)(2,1)}, u32[]{:S(2)}) copy-start(bf16[1024,512]{1,0:T(8,128)(2,1)} %get-tuple-element.74) | copy-start | bytes 3145732
  188.4 4.9 %copy-start = (f32[1024,512]{1,0:T(8,128)S(1)}, f32[1024,512]{1,0:T(8,128)}, u32[]{:S(2)}) copy-start(f32[1024,512]{1,0:T(8,128)} %get-tuple-element.75) | copy-start | bytes 6291460

commit v4 on v3

--- a/solution.py
+++ b/solution.py
@@ -103,7 +103,7 @@
 
 
 ROWS = 1024
-TILE = 256
+TILE = 512
 PAIRS = 4
 WIDE = 2048
 CHUNK = 512
@@ -150,10 +150,9 @@
 
 def mixed_phase(pair, first, wqkv, mixed):
     def body(i):
-        here = rows_at(i, TILE)
-        mixed[pair, here, :] = dot(first[here, :], wqkv[pair]).astype(LOW)
-
-    each(ROWS // TILE, body)
+        mixed[pair] = dot(first[...], wqkv[pair]).astype(LOW)
+
+    body(0)
 
 
 def bias_phase(segments, head, bias):
@@ -168,34 +167,30 @@
 
 
 def attend_phase(pair, mixed, bias, probs, context):
-    tile = 256
     lane = lax.broadcasted_iota(jnp.int32, (1, 128), 1)
     left = (lane < HEAD_DIM).astype(LOW)
 
-    def body(i):
-        seq = i // (SEQ // tile)
-        here = rows_at(i, tile)
-        keys_at = rows_at(seq, SEQ)
-        inside = rows_at(i % (SEQ // tile), tile)
+    def body(seq):
+        here = rows_at(seq, SEQ)
         query = mixed[pair, here, 0:128] * LOW(HEAD_DIM ** (-0.5))
-        keys = mixed[pair, keys_at, 128:256]
-        values = mixed[pair, keys_at, 256:384]
+        keys = mixed[pair, here, 128:256]
+        values = mixed[pair, here, 256:384]
         allowed = bias[here, :].astype(F32)
         outs = []
         for half in range(2):
             mask = left if half == 0 else LOW(1.0) - left
-            scores = dot_back(query * mask, keys) + allowed
-            top = jnp.max(scores, axis=-1, keepdims=True)
+            scores = dot_back(keys, query * mask) + allowed
+            top = jnp.max(scores, axis=0, keepdims=True)
             weights = jnp.exp(scores - top)
-            total = jnp.sum(weights, axis=-1, keepdims=True)
+            total = jnp.sum(weights, axis=0, keepdims=True)
             prob = (weights * (1.0 / total)).astype(LOW)
-            probs[pair * 4 + half * 2 + seq, inside, :] = prob
-            outs.append(dot(prob, values))
+            probs[pair * 4 + half * 2 + seq] = prob
+            outs.append(dot_rows(prob, values))
         context[here, pl.ds(pl.multiple_of(pair * 128, 128), 128)] = jnp.where(
             lane < HEAD_DIM, outs[0], outs[1]
         ).astype(LOW)
 
-    each(ROWS // tile, body)
+    each(ROWS // SEQ, body)
 
 
 def second_phase(tokens, context, wout, params, middle, second):
@@ -240,14 +235,11 @@
 
     each(ROWS // TILE, body)
 
-    def grads(c):
-        here = rows_at(c, 256)
-        for turned, wide, out in ((out_grad_t, active, g_down), (second_t, hidden_grad, g_up)):
-            grad = dot(turned[here, :], wide[...]).astype(LOW)
-            for j in range(CHUNK // 128):
-                out[chunk * 8 + j * 2 + c] = grad[:, j * 128 : j * 128 + 128]
-
-    each(2, grads)
+    for turned, wide, out in ((out_grad_t, active, g_down), (second_t, hidden_grad, g_up)):
+        grad = dot(turned[...], wide[...]).astype(LOW)
+        for j in range(CHUNK // 128):
+            for c in range(2):
+                out[chunk * 8 + j * 2 + c] = grad[c * 256 : c * 256 + 256, j * 128 : j * 128 + 128]
 
 
 def middle_phase(
@@ -278,69 +270,61 @@
 
 def out_phase(attended_t, context, g_attend):
     def body(i):
-        here = rows_at(i, 256)
+        here = rows_at(i, 512)
         grad = dot(attended_t[here, :], context[...]).astype(LOW)
         for p in range(PAIRS):
             g_attend[p, here, 384:512] = grad[:, p * 128 : p * 128 + 128]
 
-    each(2, body)
-
-
-def attend_back_phase(pair, seq, mixed, probs, context_grad, pair_grad):
+    body(0)
+
+
+def attend_back_phase(pair, seq, mixed, probs, context, context_grad):
     lane = lax.broadcasted_iota(jnp.int32, (1, 128), 1)
     left = (lane < HEAD_DIM).astype(LOW)
     scale = HEAD_DIM ** (-0.5)
-
     here = rows_at(seq, SEQ)
     query = mixed[pair, here, 0:128]
     keys = mixed[pair, here, 128:256]
     values = mixed[pair, here, 256:384]
     upper = context_grad[here, pl.ds(pl.multiple_of(pair * 128, 128), 128)]
+    product = upper.astype(F32) * context[
+        here, pl.ds(pl.multiple_of(pair * 128, 128), 128)
+    ].astype(F32)
+    product_high = product.astype(LOW)
+    product_low = (product - product_high.astype(F32)).astype(LOW)
+    marks = lax.broadcasted_iota(jnp.int32, (8, 128), 1) // HEAD_DIM
+    marks = (marks == lax.broadcasted_iota(jnp.int32, (8, 128), 0)).astype(LOW)
+    inners = dot_back(marks, product_high) + dot_back(marks, product_low)
     outs = []
     for half in range(2):
         mask = left if half == 0 else LOW(1.0) - left
         above = upper * mask
         prob_low = probs[pair * 4 + half * 2 + seq]
         prob = prob_low.astype(F32)
-        prob_grad = dot_back(above, values)
-        inner = jnp.sum(prob * prob_grad, axis=-1, keepdims=True)
+        prob_grad = dot_back(values, above)
+        inner = inners[half : half + 1, :]
         score_grad = (prob * (prob_grad - inner)).astype(LOW)
-        outs.append(
-            (
-                dot(score_grad, keys),
-                dot_rows(score_grad, query),
-                dot_rows(prob_low, above),
-            )
-        )
+        outs.append((dot_rows(score_grad, keys), dot(score_grad, query), dot(prob_low, above)))
     pick = lane < HEAD_DIM
-    pair_grad[here, 0:128] = (jnp.where(pick, outs[0][0], outs[1][0]) * scale).astype(LOW)
-    pair_grad[here, 128:256] = (jnp.where(pick, outs[0][1], outs[1][1]) * scale).astype(LOW)
-    pair_grad[here, 256:384] = (outs[0][2] + outs[1][2]).astype(LOW)
-
-
-def qkv_phase(pair, pair_grad, first_t, g_attend):
-    def body(i):
-        here = rows_at(i, 256)
-        g_attend[pair, here, 0:384] = dot(first_t[here, :], pair_grad[...]).astype(LOW)
-
-    each(2, body)
-
-
-def first_grad_phase(pair, pair_grad, wqkv, first_grad):
-    def body(i):
-        here = rows_at(i, TILE)
-        first_grad[here, :] += dot_back(pair_grad[here, :], wqkv[pair])
-
-    each(ROWS // TILE, body)
-
-
-def input_phase(params, tokens, first_grad, input_grad, norms):
+    mixed[pair, here, 0:128] = (jnp.where(pick, outs[0][0], outs[1][0]) * scale).astype(LOW)
+    mixed[pair, here, 128:256] = (jnp.where(pick, outs[0][1], outs[1][1]) * scale).astype(LOW)
+    mixed[pair, here, 256:384] = (outs[0][2] + outs[1][2]).astype(LOW)
+
+
+def qkv_phase(pair, mixed, first_t, g_attend):
+    g_attend[pair, :, 0:384] = dot(first_t[...], mixed[pair]).astype(LOW)
+
+
+def input_phase(params, tokens, mixed, wqkv, input_grad, norms):
     gain = params[0:1, :]
 
     def body(i, sums):
         here = rows_at(i, TILE)
         _, plain, factor = normalize(tokens[here, :].astype(F32), gain, gain)
-        lower, gains, shifts = normalize_back(first_grad[here, :], plain, factor, gain)
+        first_grad = dot_back(mixed[0, here, :], wqkv[0])
+        for pair in range(1, PAIRS):
+            first_grad = first_grad + dot_back(mixed[pair, here, :], wqkv[pair])
+        lower, gains, shifts = normalize_back(first_grad, plain, factor, gain)
         input_grad[here, :] += lower
         return (sums[0] + gains[None], sums[1] + shifts[None])
 
@@ -364,8 +348,12 @@
 
 
 STEP_DIMS = {"c": 1, "x": 2, "y": 4, "l": 8, "g": 16}
-GATHER_UP = ("g", "l", "y", "x", "c")
-GATHER_DOWN = ("l", "g", "x", "y", "c")
+GATHERS = (
+    (0, 0, 256, ("g", "l", "y", "x")),
+    (0, 256, 256, ("g", "x", "l", "y")),
+    (1, 0, 128, ("g", "x", "l", "y")),
+    (1, 128, 384, ("g", "y", "x", "l")),
+)
 STARTS = (("g", "l", "y", "x", "c"), ("g", "x", "l", "y", "c"), ("g", "y", "x", "l", "c"))
 ATTEND_ORDER = ("c", "x", "y", "l", "g")
 
@@ -429,19 +417,15 @@
     each(count, body)
 
 
-def gather_start(ref, rows, done, name, bits, peer, sems, slot):
+def gather_start(ref, done, name, bits, peer, sems, slot):
     fixed = {d: bits[d] for d in STEP_DIMS if d not in done}
     for place in range(2 ** len(done)):
-        tile = tile_of(fixed, done, place)
-        if rows:
-            part = ref.at[pl.ds(pl.multiple_of(tile * rows, rows), rows)]
-        else:
-            part = ref.at[tile]
+        part = ref.at[tile_of(fixed, done, place)]
         remote(part, part, sems[0].at[slot], sems[1].at[slot], peer).start()
 
 
-def gather_end(ref, rows, done, peer, sems, slot):
-    span = ref.at[pl.ds(0, 2 ** len(done) * (rows or 1))]
+def gather_end(ref, done, peer, sems, slot):
+    span = ref.at[pl.ds(0, 2 ** len(done))]
     remote(span, span, sems[0].at[slot], sems[1].at[slot], peer).wait()
 
 
@@ -494,7 +478,7 @@
     tokens, segments, out_grad, params, w_qkv, m_qkv, w_out, m_out, w_up, m_up, w_down, m_down,
     layer_out, input_grad, start_a, start_u, start_d, ortho_q, ortho_o, ortho_u, ortho_d, norm_sum, scal,
     first, mixed, context, bias, wqkv, wout, wup, wdown, pool, middle, second, second_t, out_grad_t,
-    active, hidden_grad, result, second_grad, pair_grad, acc_a, acc_u, acc_d, got_a, got_u, got_d,
+    active, hidden_grad, result, second_grad, acc_a, acc_u, acc_d, got_a, got_u, got_d,
     mom_full, mom_x, mom_u, mom_d, mom_a, norm_got, stat_got, gram, mix, send, recv,
 ):
     dp, head, bits, peers = coordinates()
@@ -504,9 +488,9 @@
     sems = (send, recv)
     slots = Slots()
     S_Q, S_O, S_M, S_MA = slots(4), slots(4), slots(2), slots(4)
-    S_UP, S_DOWN, S_CHUNK, S_LG = slots(5), slots(5), slots(24), slots(4)
+    S_W, S_CORE, S_CHUNK, S_LG = slots(16), slots(20), slots(24), slots(16)
     S_A, S_NORM, S_STAT, S_START, S_SIDE, S_ORTHO = (
-        slots(20), slots(1), slots(1), slots(15), slots(2), slots(8)
+        slots(12), slots(1), slots(1), slots(15), slots(2), slots(8)
     )
     barrier = pltpu.get_barrier_semaphore()
 
@@ -535,30 +519,45 @@
 
     weight_copy(block_q, head, S_Q + 1, sibling).start()
     weight_copy(block_q, head, S_Q + 2, peers["x"]).start()
-    gather_start(wup, 64, (), GATHER_UP[0], bits, peers[GATHER_UP[0]], sems, S_UP)
-    gather_start(wdown, 64, (), GATHER_DOWN[0], bits, peers[GATHER_DOWN[0]], sems, S_DOWN)
+    other_half = pl.ds(pl.multiple_of((1 - bits["c"]) * 256, 256), 256)
+
+    def moment_copy(i, ref):
+        return remote(ref.at[:, other_half], mom_x.at[i], send.at[S_M + i], recv.at[S_M + i], sibling)
+
+    moment_copy(0, m_up).start()
+    moment_copy(1, m_down).start()
+
+    def weight_tiles(k, far):
+        for i, (matrix, start, count, order) in enumerate(GATHERS):
+            done = order[: max(k, 0)]
+            fixed = {d: bits[d] for d in STEP_DIMS if d not in done}
+            if far and k >= 0:
+                fixed[order[k]] = 1 - bits[order[k]]
+            name = "c" if far else order[k]
+            slot = S_CORE + i * 5 + k + 1 if far else S_W + i * 4 + k
+            for place in range(2 ** len(done)):
+                row = pl.multiple_of(tile_of(fixed, done, place) * 64, 64)
+                part = (wup, wdown)[matrix].at[pl.ds(row, 64), pl.ds(start, count)]
+                remote(part, part, send.at[slot], recv.at[slot], peers[name]).start()
+
+    def weight_wait(k, far):
+        for i, (matrix, start, count, order) in enumerate(GATHERS):
+            slot = S_CORE + i * 5 + k + 1 if far else S_W + i * 4 + k
+            span = (wup, wdown)[matrix].at[pl.ds(0, 64 * 2 ** max(k, 0)), pl.ds(start, count)]
+            remote(span, span, send.at[slot], recv.at[slot], sibling).wait()
+
+    def weight_step(k):
+        weight_wait(k, False)
+        if k < 3:
+            weight_tiles(k + 1, False)
+        weight_tiles(k, True)
+
+    weight_tiles(0, False)
+    weight_tiles(-1, True)
     weight_copy(block_o, head, S_O + 1, sibling).start()
     weight_copy(block_o, head, S_O + 2, peers["x"]).start()
-    other_half = pl.ds(pl.multiple_of((1 - bits["c"]) * 256, 256), 256)
-
-    def moment_copy(i, ref):
-        return remote(ref.at[:, other_half], mom_x.at[i], send.at[S_M + i], recv.at[S_M + i], sibling)
-
-    moment_copy(0, m_up).start()
-    moment_copy(1, m_down).start()
-
-    def weight_step(k):
-        for ref, order, slot in ((wup, GATHER_UP, S_UP), (wdown, GATHER_DOWN, S_DOWN)):
-            gather_end(ref, 64, order[:k], peers[order[k]], sems, slot + k)
-            if k < 4:
-                gather_start(
-                    ref, 64, order[: k + 1], order[k + 1], bits, peers[order[k + 1]], sems, slot + k + 1
-                )
-
     first_phase(tokens, params, first)
     bias_phase(segments, head, bias)
-    weight_step(0)
-    turn_phase(out_grad, out_grad_t)
     mom_full[:, 0:384] = paired(m_qkv[...])
     mom_full[:, 384:512] = m_out[...].T
 
@@ -587,17 +586,18 @@
 
         @pl.when(j == 0)
         def _():
-            weight_step(1)
+            weight_step(0)
+            turn_phase(out_grad, out_grad_t)
             weight_copy(block_q, head, S_Q + 1, sibling).wait()
             weight_copy(block_o, head, S_O + 1, sibling).wait()
+
+        @pl.when(j == 1)
+        def _():
             weight_copy(block_q, head, S_Q + 2, peers["x"]).wait()
             weight_copy(block_q, peers["x"][1], S_Q + 3, sibling).start()
+            weight_step(1)
             weight_copy(block_o, head, S_O + 2, peers["x"]).wait()
             weight_copy(block_o, peers["x"][1], S_O + 3, sibling).start()
-
-        @pl.when(j == 1)
-        def _():
-            weight_step(2)
 
         @pl.when(j == 2)
         def _():
@@ -605,12 +605,14 @@
             weight_copy(block_o, head, S_O + 3, sibling).wait()
 
     each(PAIRS, pair_body)
+    weight_step(2)
     second_phase(tokens, context, wout, params, middle, second)
-    weight_step(3)
     turn_phase(second, second_t)
     result[...] = jnp.zeros_like(result)
     second_grad[...] = jnp.zeros_like(second_grad)
-    weight_step(4)
+    weight_step(3)
+    for k in range(-1, 4):
+        weight_wait(k, True)
 
     chunk_orders = ((acc_u, got_u, ("c", "x", "y")), (acc_d, got_d, ("c", "y", "x")))
 
@@ -648,14 +650,10 @@
             chunk_end(q - 1, 0)
             chunk_start(q - 1, 1)
 
-        @pl.when(q >= 2)
-        def _():
-            chunk_end(q - 2, 1)
-            chunk_start(q - 2, 2)
-
         @pl.when(q >= 3)
         def _():
-            chunk_end(q - 3, 2)
+            chunk_end(q - 3, 1)
+            chunk_start(q - 3, 2)
 
     each(WIDE // CHUNK, feed_body)
     middle_phase(
@@ -664,27 +662,44 @@
     )
     chunk_end(3, 0)
     chunk_start(3, 1)
-    chunk_end(2, 1)
-    chunk_start(2, 2)
-    chunk_end(1, 2)
+    chunk_end(1, 1)
+    chunk_start(1, 2)
     turn_phase(second, second_t)
     out_phase(second_t, context, acc_a)
     turn_phase(first, second_t)
-    result[...] = jnp.zeros_like(result)
-
-    def last_args(k):
-        fixed = {"c": bits["c"], "x": bits["x"], "y": bits["y"]}
-        if k == 1:
-            fixed["l"] = bits["l"]
-            return fixed, "g", ()
-        return fixed, "l", ("g",)
-
-    def last_step(k, ending):
+
+    depth = dp // 2
+
+    def owner_copy(i, acc, got, q):
+        tile = tile_of({"g": q // 2, "l": q % 2, "c": bits["c"], "x": bits["x"], "y": bits["y"]}, (), 0)
+        other = (2 * q + bits["y"], head)
+        return remote(
+            acc.at[tile], got.at[28 + (depth - q + 3) % 4], send.at[S_LG + 2 * q + i],
+            recv.at[S_LG + 8 + 3 * i + (depth - q + 3) % 4], other,
+        )
+
+    def owner_start(q):
+        @pl.when(depth != q)
+        def _():
+            for i, (acc, got, _) in enumerate(chunk_orders):
+                owner_copy(i, acc, got, q).start()
+
+    def owner_sent(q):
+        @pl.when(depth != q)
+        def _():
+            for i, (acc, got, _) in enumerate(chunk_orders):
+                owner_copy(i, acc, got, q).wait_send()
+
+    def owner_end():
         for i, (acc, got, _) in enumerate(chunk_orders):
-            fixed, name, free = last_args(k)
-            (scatter_end if ending else scatter_start)(
-                acc, got, 28 + 2 * k, fixed, name, free, bits, peers[name], sems, S_LG + 2 * k + i
-            )
+            for way in range(3):
+                remote(
+                    got.at[28 + way], got.at[28 + way], send.at[S_LG], recv.at[S_LG + 8 + 3 * i + way], sibling
+                ).wait_recv()
+            total = acc[me].astype(F32)
+            for way in range(3):
+                total = total + got[28 + way].astype(F32)
+            acc[me] = total.astype(LOW)
 
     spans = []
     low_row = 0
@@ -700,43 +715,70 @@
         name, size, _, give = spans[k]
         return remote(
             acc_a.at[pair, aligned(give, size)], got_a.at[pair, pl.ds(512 - 2 * size, size)],
-            send.at[S_A + pair * 5 + k], recv.at[S_A + pair * 5 + k], peers[name],
+            send.at[S_A + pair * 3 + k], recv.at[S_A + pair * 3 + k], peers[name],
         )
 
+    quarter = spans[1][2]
+
+    def place_of(group):
+        return (group % 2) * 4 + ((group // 2) % 2) * 2 + group // 4
+
     def attend_start(pair, k):
-        attend_copy(pair, k).start()
-
-    def attend_next(pair, k, more=True):
+        if k < 2:
+            attend_copy(pair, k).start()
+            return
+
+        def body(i):
+            other = (dp + 1 + i) % 8
+            remote(
+                acc_a.at[pair, aligned(quarter + place_of(other) * 16, 16)],
+                got_a.at[pair, aligned(384 + (6 - i) * 16, 16)],
+                send.at[S_A + pair * 3 + 2], recv.at[S_A + pair * 3 + 2], (other, head),
+            ).start()
+
+        each(7, body)
+
+    def attend_next(pair, k):
+        if k == 2:
+            span = got_a.at[pair, pl.ds(384, 112)]
+            remote(span, span, send.at[S_A + pair * 3 + 2], recv.at[S_A + pair * 3 + 2], sibling).wait()
+            here = aligned(low_row, 16)
+            total = acc_a[pair, here, :].astype(F32)
+            for i in range(1, 8):
+                total = total + got_a[pair, 368 + i * 16 : 384 + i * 16, :].astype(F32)
+            acc_a[pair, here, :] = total.astype(LOW)
+            return
         attend_copy(pair, k).wait()
         _, size, keep, _ = spans[k]
-        step = min(size, 64)
 
         def body(i):
-            here = aligned(keep + i * step, step)
-            come = aligned(512 - 2 * size + i * step, step)
+            here = aligned(keep + i * 64, 64)
+            come = aligned(512 - 2 * size + i * 64, 64)
             acc_a[pair, here, :] = (
                 acc_a[pair, here, :].astype(F32) + got_a[pair, come, :].astype(F32)
             ).astype(LOW)
 
-        each(size // step, body)
-        if k < 4:
-            attend_start(pair, k + 1)
+        each(size // 64, body)
+        attend_start(pair, k + 1)
 
     def at(wanted, pair):
         return pl.when(pair == wanted)
 
     def back_body(pair):
-        attend_back_phase(pair, 0, mixed, pool, active, pair_grad)
+        attend_back_phase(pair, 0, mixed, pool, context, active)
 
         @at(0, pair)
         def _():
-            chunk_end(3, 1)
-            chunk_start(3, 2)
-            chunk_end(2, 2)
+            chunk_end(0, 2)
+            owner_start(0)
+            chunk_end(2, 1)
+            chunk_start(2, 2)
 
         @at(1, pair)
         def _():
             attend_next(0, 0)
+            chunk_end(3, 1)
+            chunk_start(3, 2)
 
         @at(2, pair)
         def _():
@@ -747,35 +789,31 @@
         def _():
             attend_next(2, 0)
             attend_next(1, 1)
-            attend_next(0, 3)
-
-        attend_back_phase(pair, 1, mixed, pool, active, pair_grad)
-        qkv_phase(pair, pair_grad, second_t, acc_a)
+
+        attend_back_phase(pair, 1, mixed, pool, context, active)
+        qkv_phase(pair, mixed, second_t, acc_a)
         attend_start(pair, 0)
 
         @at(0, pair)
         def _():
-            chunk_end(3, 2)
-            last_step(0, False)
+            chunk_end(1, 2)
+            owner_start(1)
 
         @at(1, pair)
         def _():
-            last_step(0, True)
-            last_step(1, False)
+            chunk_end(2, 2)
+            owner_start(2)
 
         @at(2, pair)
         def _():
-            last_step(1, True)
-            attend_next(0, 2)
-
-        first_grad_phase(pair, pair_grad, wqkv, result)
+            chunk_end(3, 2)
+            owner_start(3)
 
     each(PAIRS, back_body)
     attend_next(3, 0)
     attend_next(2, 1)
-    attend_next(1, 2)
-    attend_next(0, 4)
-    input_phase(params, tokens, result, input_grad, norm_got.at[me])
+    attend_next(0, 2)
+    input_phase(params, tokens, mixed, wqkv, input_grad, norm_got.at[me])
 
     def tell_norm(i):
         other = (me + 1 + i) % 32
@@ -785,8 +823,10 @@
 
     attend_next(3, 1)
     each(31, tell_norm)
-    attend_next(2, 2)
-    attend_next(1, 3)
+    attend_next(1, 2)
+    for q in range(4):
+        owner_sent(q)
+    owner_end()
     moment_copy(0, m_up).wait()
     moment_copy(1, m_down).wait()
     keep_half = pl.ds(pl.multiple_of(bits["c"] * 256, 256), 256)
@@ -810,11 +850,8 @@
     for m, (moment, grad) in enumerate(((mom_u[...], grad_u), (mom_d[...], grad_d))):
         for i, product in enumerate((moment * moment, moment * grad, grad * grad)):
             stats = jnp.where(lane == 6 + 3 * m + i, total_of(product), stats)
+    attend_next(2, 2)
     attend_next(3, 2)
-    attend_next(2, 3)
-    attend_next(1, 4)
-    attend_next(3, 3)
-    attend_next(2, 4)
     span = norm_got.at[pl.ds(0, 31)]
     remote(span, span, send.at[S_NORM], recv.at[S_NORM], sibling).wait()
     vector = norm_got[0]
@@ -822,7 +859,6 @@
         vector = vector + norm_got[i]
     norm_sum[...] = vector
     vector_total = total_of(vector * vector)
-    attend_next(3, 4)
     my_rows = aligned(low_row, 16)
     for i in range(3):
         inside = jnp.zeros((1, 512), F32)
@@ -889,15 +925,18 @@
         return remote(part, part, send.at[S_START + 3 * k], recv.at[S_START + 3 * k], peers[name])
 
     tiles = ((got_u, STARTS[1]), (got_d, STARTS[2]))
-    for k in range(4):
-        start_copy(k).start()
+    for k in range(5):
+        if k > 0:
+            start_copy(k - 1).wait()
+        if k < 4:
+            start_copy(k).start()
         for m, (got, order) in enumerate(tiles):
-            gather_start(
-                got, 0, order[:k], order[k], bits, peers[order[k]], sems, S_START + 3 * k + 1 + m
-            )
-        start_copy(k).wait()
-        for m, (got, order) in enumerate(tiles):
-            gather_end(got, 0, order[:k], peers[order[k]], sems, S_START + 3 * k + 1 + m)
+            if k > 0:
+                gather_end(got, order[: k - 1], peers[order[k - 1]], sems, S_START + 3 * k - 2 + m)
+            if k < 4:
+                gather_start(
+                    got, order[:k], order[k], bits, peers[order[k]], sems, S_START + 3 * k + 1 + m
+                )
     half_rows = aligned(spans[0][2], 256)
     pair_part = pool.at[pl.ds(head + 1 - 2 * bits["c"], 1), half_rows]
     all_part = pool.at[pl.ds(0, 4), half_rows]
@@ -937,7 +976,7 @@
         for x, (got, order) in enumerate(tiles):
             @pl.when(bits["x"] == x)
             def _(got=got, order=order):
-                gather_start(got, 0, order[:4], "c", bits, sibling, sems, S_START + 13)
+                gather_start(got, order[:4], "c", bits, sibling, sems, S_START + 13)
 
         core_copy(pair_part).start()
         core_copy(all_part).wait_recv()
@@ -1059,7 +1098,6 @@
         ((ROWS, CHUNK), LOW),
         ((ROWS, 512), F32),
         ((ROWS, 512), F32),
-        ((ROWS, 384), LOW),
         ((PAIRS, 512, 512), LOW),
         ((32, 256, 128), LOW),
         ((32, 256, 128), LOW),
@@ -1082,7 +1120,7 @@
         in_specs=[vmem] * len(args),
         out_specs=(vmem,) * len(outs),
         scratch_shapes=[pltpu.VMEM(*v) for v in scratch]
-        + [pltpu.SemaphoreType.DMA((104,)), pltpu.SemaphoreType.DMA((104,))],
+        + [pltpu.SemaphoreType.DMA((128,)), pltpu.SemaphoreType.DMA((128,))],
         compiler_params=pltpu.CompilerParams(
             collective_id=1, has_side_effects=True, vmem_limit_bytes=VMEM_BYTES
         ),

time: 196 us -> 182 us (0.929)
  Pallas kernels: 190 us -> 176 us
    pallas_call x1, Pallas kernels: 186 us -> 172 us  [layer_call(): pl.pallas_call(layer_kernel, out_shape=outs, in_specs=[vmem] * len(args),...]
where the time goes in v4:
time: 182 us; the launch traced here: 180 us
  Pallas kernels  176 us (97%)
  local copies, waits for them, and re-layouts  3.63 us (2%)
    pallas_call x1, Pallas kernels, layer_call(): pl.pallas_call(layer_kernel, out_shape=outs, in_specs=[vmem] * len(args),...  172 us
    pallas_call x1, Pallas kernels, local_call(): pl.pallas_call(kernel, out_shape=tuple((jax.ShapeDtypeStruct(*o) for o in...  3.85 us

profile of v4, /device:TPU:19, one launch (start us, length us, event | category | flops | bytes accessed | tf_op | source)
XLA Modules:
  0.0 180.4 jit_solution(12653282380076616882)
XLA Ops:
  0.6 1.3 reshape.34.segments
  2.0 172.2 %layer.1 = (bf16[1024,512]{1,0:T(8,128)(2,1)}, f32[1024,512]{1,0:T(8,128)}, bf16[512,512]{1,0:T(8,128)(2,1)}, bf16[512,128]{1,0:T(8,128)(2,1)}, bf16[512,128]{1,...) custom-call(bf16[1024,512]{1,0:T(8,128)(2,1)} %tokens.1, ...), custom_call_target="tpu_custom_call" | custom-call | tf_op jit(solution)/shard_map/layer/pallas_call | solution.py:1117
  174.2 0.0 copy-start.1
  174.2 0.0 copy-start
  174.2 3.9 %update.1 = (f32[512,384]{1,0:T(8,128)}, f32[512,384]{1,0:T(8,128)}, f32[128,512]{1,0:T(8,128)}, f32[128,512]{1,0:T(8,128)}, f32[64,512]{1,0:T(8,128)}, /*index=...) custom-call(bf16[512,512]{1,0:T(8,128)(2,1)} %get-tuple-element.39.s, ...), custom_call_target="tpu_custom_call" | custom-call | tf_op jit(solution)/shard_map/update/pallas_call | solution.py:339
  178.1 0.0 copy-done.1
  178.1 1.0 copy.30
  179.1 0.0 copy-done
  179.1 1.3 copy.31
Async XLA Ops:
  174.2 3.9 %copy-start.1 = (bf16[1024,512]{1,0:T(8,128)(2,1)S(1)}, bf16[1024,512]{1,0:T(8,128)(2,1)}, u32[]{:S(2)}) copy-start(bf16[1024,512]{1,0:T(8,128)(2,1)} %get-tuple-element.74) | copy-start | bytes 3145732
  174.2 4.9 %copy-start = (f32[1024,512]{1,0:T(8,128)S(1)}, f32[1024,512]{1,0:T(8,128)}, u32[]{:S(2)}) copy-start(f32[1024,512]{1,0:T(8,128)} %get-tuple-element.75) | copy-start | bytes 6291460

commit v5 on v4

--- a/solution.py
+++ b/solution.py
@@ -450,21 +450,25 @@
 
 
 def update_step(pool, now, later, count, blocks, lanes, gram, mix):
-    def gram_body(i):
-        rows = rows_at(i, TILE)
-        total = dot_back(pool[now, rows, :], pool[now])
+    for low, high in ((0, 512), (256, 512)):
+        rows = slice(low, low + 256)
+        cols = slice(low, high)
+        total = dot_back(pool[now, rows, :], pool[now, cols, :])
         for b in range(1, count):
-            total = total + dot_back(pool[now + b, rows, :], pool[now + b])
-        gram[rows, :] = total.astype(LOW)
-
-    each(512 // TILE, gram_body)
-
-    def mix_body(i):
-        rows = rows_at(i, TILE)
-        own = gram[rows, :]
-        mix[rows, :] = (ns_b * own.astype(F32) + ns_c * dot(own, gram[...])).astype(LOW)
-
-    each(512 // TILE, mix_body)
+            total = total + dot_back(pool[now + b, rows, :], pool[now + b, cols, :])
+        made = total.astype(LOW)
+        gram[rows, cols] = made
+        if low == 0:
+            gram[256:512, 0:256] = made[:, 256:512].T
+    for low, high in ((0, 512), (256, 512)):
+        rows = slice(low, low + 256)
+        cols = slice(low, high)
+        made = (
+            ns_b * gram[rows, cols].astype(F32) + ns_c * dot(gram[rows, :], gram[:, cols])
+        ).astype(LOW)
+        mix[rows, cols] = made
+        if low == 0:
+            mix[256:512, 0:256] = made[:, 256:512].T
 
     def next_body(i):
         b = blocks[0] + i
@@ -479,7 +483,7 @@
     layer_out, input_grad, start_a, start_u, start_d, ortho_q, ortho_o, ortho_u, ortho_d, norm_sum, scal,
     first, mixed, context, bias, wqkv, wout, wup, wdown, pool, middle, second, second_t, out_grad_t,
     active, hidden_grad, result, second_grad, acc_a, acc_u, acc_d, got_a, got_u, got_d,
-    mom_full, mom_x, mom_u, mom_d, mom_a, norm_got, stat_got, gram, mix, send, recv,
+    mom_full, mom_x, mom_u, mom_d, mom_a, norm_got, norm_far, stat_got, stat_far, gram, mix, send, recv,
 ):
     dp, head, bits, peers = coordinates()
     me = dp * 4 + head
@@ -490,23 +494,27 @@
     S_Q, S_O, S_M, S_MA = slots(4), slots(4), slots(2), slots(4)
     S_W, S_CORE, S_CHUNK, S_LG = slots(16), slots(20), slots(24), slots(16)
     S_A, S_NORM, S_STAT, S_START, S_SIDE, S_ORTHO = (
-        slots(12), slots(1), slots(1), slots(15), slots(2), slots(8)
+        slots(12), slots(2), slots(2), slots(15), slots(2), slots(8)
     )
     barrier = pltpu.get_barrier_semaphore()
 
-    def greet(i):
-        other = (me + 1 + i) % 32
-        pl.semaphore_signal(
-            barrier, inc=1, device_id=(other // 4, other % 4), device_id_type=pl.DeviceIdType.MESH
-        )
-
-    each(31, greet)
+    partners = (sibling, peers["x"], across)
+
+    def along(i):
+        return ((dp + 1 + i) % 8, head)
+
+    def greet(peer):
+        pl.semaphore_signal(barrier, inc=1, device_id=peer, device_id_type=pl.DeviceIdType.MESH)
+
+    for peer in partners:
+        greet(peer)
+    each(7, lambda i: greet(along(i)))
     wqkv[head] = paired(w_qkv[...].astype(LOW))
     wout[pl.ds(pl.multiple_of(head * 128, 128), 128), :] = w_out[...].astype(LOW)
     mine = pl.ds(pl.multiple_of(me * 64, 64), 64)
     wup[mine, :] = w_up[...].astype(LOW)
     wdown[mine, :] = w_down[...].astype(LOW)
-    pl.semaphore_wait(barrier, 31)
+    pl.semaphore_wait(barrier, 10)
 
     def block_q(who):
         return wqkv.at[who]
@@ -517,6 +525,27 @@
     def weight_copy(block, who, slot, peer):
         return remote(block(who), block(who), send.at[slot], recv.at[slot], peer)
 
+    def weight_tiles(i, k, far):
+        matrix, start, count, order = GATHERS[i]
+        done = order[: max(k, 0)]
+        fixed = {d: bits[d] for d in STEP_DIMS if d not in done}
+        if far and k >= 0:
+            fixed[order[k]] = 1 - bits[order[k]]
+        name = "c" if far else order[k]
+        slot = S_CORE + i * 5 + k + 1 if far else S_W + i * 4 + k
+        for place in range(2 ** len(done)):
+            row = pl.multiple_of(tile_of(fixed, done, place) * 64, 64)
+            part = (wup, wdown)[matrix].at[pl.ds(row, 64), pl.ds(start, count)]
+            remote(part, part, send.at[slot], recv.at[slot], peers[name]).start()
+
+    def weight_wait(i, k, far):
+        matrix, start, count, _ = GATHERS[i]
+        slot = S_CORE + i * 5 + k + 1 if far else S_W + i * 4 + k
+        span = (wup, wdown)[matrix].at[pl.ds(0, 64 * 2 ** max(k, 0)), pl.ds(start, count)]
+        remote(span, span, send.at[slot], recv.at[slot], sibling).wait()
+
+    for i in range(len(GATHERS)):
+        weight_tiles(i, 0, False)
     weight_copy(block_q, head, S_Q + 1, sibling).start()
     weight_copy(block_q, head, S_Q + 2, peers["x"]).start()
     other_half = pl.ds(pl.multiple_of((1 - bits["c"]) * 256, 256), 256)
@@ -527,35 +556,20 @@
     moment_copy(0, m_up).start()
     moment_copy(1, m_down).start()
 
-    def weight_tiles(k, far):
-        for i, (matrix, start, count, order) in enumerate(GATHERS):
-            done = order[: max(k, 0)]
-            fixed = {d: bits[d] for d in STEP_DIMS if d not in done}
-            if far and k >= 0:
-                fixed[order[k]] = 1 - bits[order[k]]
-            name = "c" if far else order[k]
-            slot = S_CORE + i * 5 + k + 1 if far else S_W + i * 4 + k
-            for place in range(2 ** len(done)):
-                row = pl.multiple_of(tile_of(fixed, done, place) * 64, 64)
-                part = (wup, wdown)[matrix].at[pl.ds(row, 64), pl.ds(start, count)]
-                remote(part, part, send.at[slot], recv.at[slot], peers[name]).start()
-
-    def weight_wait(k, far):
-        for i, (matrix, start, count, order) in enumerate(GATHERS):
-            slot = S_CORE + i * 5 + k + 1 if far else S_W + i * 4 + k
-            span = (wup, wdown)[matrix].at[pl.ds(0, 64 * 2 ** max(k, 0)), pl.ds(start, count)]
-            remote(span, span, send.at[slot], recv.at[slot], sibling).wait()
+    parts = range(len(GATHERS))
 
     def weight_step(k):
-        weight_wait(k, False)
-        if k < 3:
-            weight_tiles(k + 1, False)
-        weight_tiles(k, True)
-
-    weight_tiles(0, False)
-    weight_tiles(-1, True)
+        for i in parts:
+            weight_wait(i, k, False)
+            if k < 3:
+                weight_tiles(i, k + 1, False)
+        for i in parts:
+            weight_tiles(i, k, True)
+
     weight_copy(block_o, head, S_O + 1, sibling).start()
     weight_copy(block_o, head, S_O + 2, peers["x"]).start()
+    for i in parts:
+        weight_tiles(i, -1, True)
     first_phase(tokens, params, first)
     bias_phase(segments, head, bias)
     mom_full[:, 0:384] = paired(m_qkv[...])
@@ -566,8 +580,6 @@
 
     def rank_rows(who):
         return pl.ds(pl.multiple_of(rank_of(who % 2, who // 2) * 16, 16), 16)
-
-    partners = (sibling, peers["x"], across)
 
     def rows_copy(j):
         who = partners[j][1]
@@ -612,7 +624,8 @@
     second_grad[...] = jnp.zeros_like(second_grad)
     weight_step(3)
     for k in range(-1, 4):
-        weight_wait(k, True)
+        for i in parts:
+            weight_wait(i, k, True)
 
     chunk_orders = ((acc_u, got_u, ("c", "x", "y")), (acc_d, got_d, ("c", "y", "x")))
 
@@ -658,7 +671,7 @@
     each(WIDE // CHUNK, feed_body)
     middle_phase(
         params, middle, result, second_grad, out_grad, wout,
-        layer_out, input_grad, second, active, norm_got.at[me],
+        layer_out, input_grad, second, active, norm_got.at[head],
     )
     chunk_end(3, 0)
     chunk_start(3, 1)
@@ -813,17 +826,33 @@
     attend_next(3, 0)
     attend_next(2, 1)
     attend_next(0, 2)
-    input_phase(params, tokens, mixed, wqkv, input_grad, norm_got.at[me])
-
-    def tell_norm(i):
-        other = (me + 1 + i) % 32
-        remote(
-            norm_got.at[me], norm_got.at[me], send.at[S_NORM], recv.at[S_NORM], (other // 4, other % 4)
-        ).start()
-
+    input_phase(params, tokens, mixed, wqkv, input_grad, norm_got.at[head])
+
+    def tell(ref, slot):
+        for peer in partners:
+            remote(ref.at[head], ref.at[head], send.at[slot], recv.at[slot], peer).start()
+
+    def tell_on(ref, far, slot):
+        span = ref.at[pl.ds(0, 3)]
+        remote(span, span, send.at[slot], recv.at[slot], sibling).wait()
+        far[dp] = (ref[0] + ref[1]) + (ref[2] + ref[3])
+
+        def body(i):
+            remote(
+                far.at[dp], far.at[dp], send.at[slot + 1], recv.at[slot + 1], along(i)
+            ).start()
+
+        each(7, body)
+
+    def told_of(far, slot):
+        span = far.at[pl.ds(0, 7)]
+        remote(span, span, send.at[slot + 1], recv.at[slot + 1], sibling).wait()
+        return jnp.sum(far[...], axis=0)
+
+    tell(norm_got, S_NORM)
     attend_next(3, 1)
-    each(31, tell_norm)
     attend_next(1, 2)
+    tell_on(norm_got, norm_far, S_NORM)
     for q in range(4):
         owner_sent(q)
     owner_end()
@@ -852,11 +881,7 @@
             stats = jnp.where(lane == 6 + 3 * m + i, total_of(product), stats)
     attend_next(2, 2)
     attend_next(3, 2)
-    span = norm_got.at[pl.ds(0, 31)]
-    remote(span, span, send.at[S_NORM], recv.at[S_NORM], sibling).wait()
-    vector = norm_got[0]
-    for i in range(1, 32):
-        vector = vector + norm_got[i]
+    vector = told_of(norm_far, S_NORM)
     norm_sum[...] = vector
     vector_total = total_of(vector * vector)
     my_rows = aligned(low_row, 16)
@@ -869,18 +894,10 @@
             inside = inside + jnp.sum(product, axis=0, keepdims=True)
         stats = jnp.where(lane == i, total_of(jnp.where(column < 384, inside, 0.0)), stats)
         stats = jnp.where(lane == 3 + i, total_of(jnp.where(column < 384, 0.0, inside)), stats)
-    stat_got[me] = stats
-
-    def tell(i):
-        other = (me + 1 + i) % 32
-        remote(
-            stat_got.at[me], stat_got.at[me], send.at[S_STAT], recv.at[S_STAT], (other // 4, other % 4)
-        ).start()
-
-    each(31, tell)
-    span = stat_got.at[pl.ds(0, 31)]
-    remote(span, span, send.at[S_STAT], recv.at[S_STAT], sibling).wait()
-    stats = jnp.sum(stat_got[...], axis=0)
+    stat_got[head] = stats
+    tell(stat_got, S_STAT)
+    tell_on(stat_got, stat_far, S_STAT)
+    stats = told_of(stat_far, S_STAT)
 
     def stat(i):
         return jnp.sum(jnp.where(lane == i, stats, 0.0), axis=1, keepdims=True)[0:1]
@@ -1109,8 +1126,10 @@
         ((256, 128), F32),
         ((256, 128), F32),
         ((PAIRS, 16, 512), F32),
-        ((32, 4, 512), F32),
-        ((32, 8, 128), F32),
+        ((4, 4, 512), F32),
+        ((8, 4, 512), F32),
+        ((4, 8, 128), F32),
+        ((8, 8, 128), F32),
         ((512, 512), LOW),
         ((512, 512), LOW),
     ]

time: 182 us -> 177 us (0.973); the launches traced: 180 us -> 174 us
  Pallas kernels: 176 us -> 169 us
    pallas_call x1, Pallas kernels: 172 us -> 165 us  [layer_call(): pl.pallas_call(layer_kernel, out_shape=outs, in_specs=[vmem] * len(args),...]
where the time goes in v5:
time: 177 us; the launch traced here: 174 us
  Pallas kernels  169 us (95%)
  local copies, waits for them, and re-layouts  3.63 us (2%)
    pallas_call x1, Pallas kernels, layer_call(): pl.pallas_call(layer_kernel, out_shape=outs, in_specs=[vmem] * len(args),...  165 us
    pallas_call x1, Pallas kernels, local_call(): pl.pallas_call(kernel, out_shape=tuple((jax.ShapeDtypeStruct(*o) for o in...  3.85 us

profile of v5, /device:TPU:19, one launch (start us, length us, event | category | flops | bytes accessed | tf_op | source)
XLA Modules:
  0.0 173.5 jit_solution(317110750083302407)
XLA Ops:
  0.6 1.3 reshape.34.segments
  2.0 165.4 %layer.1 = (bf16[1024,512]{1,0:T(8,128)(2,1)}, f32[1024,512]{1,0:T(8,128)}, bf16[512,512]{1,0:T(8,128)(2,1)}, bf16[512,128]{1,0:T(8,128)(2,1)}, bf16[512,128]{1,...) custom-call(bf16[1024,512]{1,0:T(8,128)(2,1)} %tokens.1, ...), custom_call_target="tpu_custom_call" | custom-call | tf_op jit(solution)/shard_map/layer/pallas_call | solution.py:1136
  167.4 0.0 copy-start.1
  167.4 0.0 copy-start
  167.4 3.9 %update.1 = (f32[512,384]{1,0:T(8,128)}, f32[512,384]{1,0:T(8,128)}, f32[128,512]{1,0:T(8,128)}, f32[128,512]{1,0:T(8,128)}, f32[64,512]{1,0:T(8,128)}, /*index=...) custom-call(bf16[512,512]{1,0:T(8,128)(2,1)} %get-tuple-element.39.s, ...), custom_call_target="tpu_custom_call" | custom-call | tf_op jit(solution)/shard_map/update/pallas_call | solution.py:339
  171.2 0.0 copy-done.1
  171.2 1.0 copy.30
  172.2 0.0 copy-done
  172.2 1.3 copy.31
Async XLA Ops:
  167.4 3.9 %copy-start.1 = (bf16[1024,512]{1,0:T(8,128)(2,1)S(1)}, bf16[1024,512]{1,0:T(8,128)(2,1)}, u32[]{:S(2)}) copy-start(bf16[1024,512]{1,0:T(8,128)(2,1)} %get-tuple-element.74) | copy-start | bytes 3145732
  167.4 4.9 %copy-start = (f32[1024,512]{1,0:T(8,128)S(1)}, f32[1024,512]{1,0:T(8,128)}, u32[]{:S(2)}) copy-start(f32[1024,512]{1,0:T(8,128)} %get-tuple-element.75) | copy-start | bytes 6291460

commit v6 on v5

--- a/solution.py
+++ b/solution.py
@@ -156,13 +156,12 @@
 
 
 def bias_phase(segments, head, bias):
-    turned = segments[...].astype(F32).T
-    lane = lax.broadcasted_iota(jnp.int32, (1, segments.shape[0]), 1)
-
     for seq in range(ROWS // SEQ):
-        which = head * (ROWS // SEQ) + seq
-        row = segments[pl.ds(which, 1), :].astype(F32)
-        column = jnp.sum(jnp.where(lane == which, turned, 0.0), axis=1, keepdims=True)
+        start = (head * (ROWS // SEQ) + seq) * (SEQ // 128)
+        row = jnp.concatenate(
+            [segments[pl.ds(start + i, 1), :] for i in range(SEQ // 128)], axis=1
+        ).astype(F32)
+        column = jnp.broadcast_to(row, (8, SEQ)).T[:, 0:1]
         bias[seq * SEQ : seq * SEQ + SEQ, :] = jnp.where(column == row, 0.0, neg_fill).astype(LOW)
 
 
@@ -348,13 +347,8 @@
 
 
 STEP_DIMS = {"c": 1, "x": 2, "y": 4, "l": 8, "g": 16}
-GATHERS = (
-    (0, 0, 256, ("g", "l", "y", "x")),
-    (0, 256, 256, ("g", "x", "l", "y")),
-    (1, 0, 128, ("g", "x", "l", "y")),
-    (1, 128, 384, ("g", "y", "x", "l")),
-)
-STARTS = (("g", "l", "y", "x", "c"), ("g", "x", "l", "y", "c"), ("g", "y", "x", "l", "c"))
+GATHERS = ((0, 0, 512, ("g", "l", "y", "x")), (1, 0, 512, ("g", "l", "x", "y")))
+STARTS = (("g", "l", "y", "x", "c"), ("x", "g", "l", "y", "c"), ("g", "y", "x", "l", "c"))
 ATTEND_ORDER = ("c", "x", "y", "l", "g")
 
 
@@ -942,6 +936,30 @@
         return remote(part, part, send.at[S_START + 3 * k], recv.at[S_START + 3 * k], peers[name])
 
     tiles = ((got_u, STARTS[1]), (got_d, STARTS[2]))
+    half_rows = aligned(spans[0][2], 256)
+    pair_part = pool.at[pl.ds(head + 1 - 2 * bits["c"], 1), half_rows]
+    all_part = pool.at[pl.ds(0, 4), half_rows]
+
+    def core_copy(part):
+        return remote(part, part, send.at[S_START + 12], recv.at[S_START + 12], sibling)
+
+    def core_tiles(late):
+        @pl.when(bits["c"] == 1)
+        def _():
+            row = spans[1][3] if late else spans[1][2]
+            core_copy(pool.at[pl.ds(0, 4), aligned(row, 128)]).start()
+
+        @pl.when(bits["c"] == 0)
+        def _():
+            for x, (got, order) in enumerate(tiles):
+                @pl.when(bits["x"] == x)
+                def _(got=got, order=order):
+                    flipped = {**bits, order[3]: 1 - bits[order[3]]} if late else bits
+                    gather_start(got, order[:3], "c", flipped, sibling, sems, S_START + 13)
+
+    def core_early():
+        core_tiles(False)
+
     for k in range(5):
         if k > 0:
             start_copy(k - 1).wait()
@@ -954,17 +972,12 @@
                 gather_start(
                     got, order[:k], order[k], bits, peers[order[k]], sems, S_START + 3 * k + 1 + m
                 )
-    half_rows = aligned(spans[0][2], 256)
-    pair_part = pool.at[pl.ds(head + 1 - 2 * bits["c"], 1), half_rows]
-    all_part = pool.at[pl.ds(0, 4), half_rows]
-
-    def core_copy(part):
-        return remote(part, part, send.at[S_START + 12], recv.at[S_START + 12], sibling)
+        if k == 3:
+            core_early()
+    core_tiles(True)
 
     @pl.when(bits["c"] == 1)
     def _():
-        core_copy(all_part).start()
-
         def slice_body(i):
             rows = rows_at(i, 256)
             start_a[rows, :] = pool[head, rows, :]
@@ -990,11 +1003,6 @@
 
     @pl.when(bits["c"] == 0)
     def _():
-        for x, (got, order) in enumerate(tiles):
-            @pl.when(bits["x"] == x)
-            def _(got=got, order=order):
-                gather_start(got, order[:4], "c", bits, sibling, sems, S_START + 13)
-
         core_copy(pair_part).start()
         core_copy(all_part).wait_recv()
 
@@ -1198,7 +1206,7 @@
     (
         layer_out, input_grad, start_a, start_u, start_d, ortho_q, ortho_o, ortho_u, ortho_d, norm_sum, scal
     ) = layer_call(
-        tokens, segments.reshape(segments.shape[0] // SEQ, SEQ), out_grad, norm_params,
+        tokens, segments.reshape(segments.shape[0] // 128, 128), out_grad, norm_params,
         qkv_weight, qkv_moment, out_weight, out_moment,
         up_weight.T, up_moment.T, down_weight.T, down_moment.T,
     )

time: 177 us -> 173 us (0.977)
  Pallas kernels: 169 us -> 167 us
    pallas_call x1, Pallas kernels: 165 us -> 163 us  [layer_call(): pl.pallas_call(layer_kernel, out_shape=outs, in_specs=[vmem] * len(args),...]
where the time goes in v6:
time: 173 us; the launch traced here: 170 us
  Pallas kernels  167 us (97%)
  local copies, waits for them, and re-layouts  2.3 us (1%)
    pallas_call x1, Pallas kernels, layer_call(): pl.pallas_call(layer_kernel, out_shape=outs, in_specs=[vmem] * len(args),...  163 us
    pallas_call x1, Pallas kernels, local_call(): pl.pallas_call(kernel, out_shape=tuple((jax.ShapeDtypeStruct(*o) for o in...  3.85 us

profile of v6, /device:TPU:19, one launch (start us, length us, event | category | flops | bytes accessed | tf_op | source)
XLA Modules:
  0.0 170.3 jit_solution(5463655083102348412)
XLA Ops:
  0.6 163.5 %layer.1 = (bf16[1024,512]{1,0:T(8,128)(2,1)}, f32[1024,512]{1,0:T(8,128)}, bf16[512,512]{1,0:T(8,128)(2,1)}, bf16[512,128]{1,0:T(8,128)(2,1)}, bf16[512,128]{1,...) custom-call(bf16[1024,512]{1,0:T(8,128)(2,1)} %tokens.1, ...), custom_call_target="tpu_custom_call" | custom-call | tf_op jit(solution)/shard_map/layer/pallas_call | solution.py:1144
  164.1 0.0 copy-start.1
  164.1 0.0 copy-start
  164.1 3.9 %update.1 = (f32[512,384]{1,0:T(8,128)}, f32[512,384]{1,0:T(8,128)}, f32[128,512]{1,0:T(8,128)}, f32[128,512]{1,0:T(8,128)}, f32[64,512]{1,0:T(8,128)}, /*index=...) custom-call(bf16[512,512]{1,0:T(8,128)(2,1)} %get-tuple-element.39.s, ...), custom_call_target="tpu_custom_call" | custom-call | tf_op jit(solution)/shard_map/update/pallas_call | solution.py:338
  168.0 0.0 copy-done.1
  168.0 1.0 copy.30
  169.0 0.0 copy-done
  169.0 1.3 copy.31
Async XLA Ops:
  164.1 3.9 %copy-start.1 = (bf16[1024,512]{1,0:T(8,128)(2,1)S(1)}, bf16[1024,512]{1,0:T(8,128)(2,1)}, u32[]{:S(2)}) copy-start(bf16[1024,512]{1,0:T(8,128)(2,1)} %get-tuple-element.74) | copy-start | bytes 3145732
  164.1 4.9 %copy-start = (f32[1024,512]{1,0:T(8,128)S(1)}, f32[1024,512]{1,0:T(8,128)}, u32[]{:S(2)}) copy-start(f32[1024,512]{1,0:T(8,128)} %get-tuple-element.75) | copy-start | bytes 6291460

commit v7 on v6

--- a/solution.py
+++ b/solution.py
@@ -519,7 +519,7 @@
     def weight_copy(block, who, slot, peer):
         return remote(block(who), block(who), send.at[slot], recv.at[slot], peer)
 
-    def weight_tiles(i, k, far):
+    def weight_tiles(i, k, far, half=None):
         matrix, start, count, order = GATHERS[i]
         done = order[: max(k, 0)]
         fixed = {d: bits[d] for d in STEP_DIMS if d not in done}
@@ -527,7 +527,10 @@
             fixed[order[k]] = 1 - bits[order[k]]
         name = "c" if far else order[k]
         slot = S_CORE + i * 5 + k + 1 if far else S_W + i * 4 + k
-        for place in range(2 ** len(done)):
+        if half == 1 and not far:
+            slot = S_W + 8 + i
+        places = range(2 ** len(done)) if half is None else range(half * 4, half * 4 + 4)
+        for place in places:
             row = pl.multiple_of(tile_of(fixed, done, place) * 64, 64)
             part = (wup, wdown)[matrix].at[pl.ds(row, 64), pl.ds(start, count)]
             remote(part, part, send.at[slot], recv.at[slot], peers[name]).start()
@@ -553,12 +556,20 @@
     parts = range(len(GATHERS))
 
     def weight_step(k):
-        for i in parts:
-            weight_wait(i, k, False)
-            if k < 3:
-                weight_tiles(i, k + 1, False)
-        for i in parts:
-            weight_tiles(i, k, True)
+        if k < 3:
+            for i in parts:
+                weight_wait(i, k, False)
+                for half in (None,) if k < 2 else (0, 1):
+                    weight_tiles(i, k + 1, False, half)
+            for i in parts:
+                weight_tiles(i, k, True)
+            return
+        for half in range(2):
+            for i in parts:
+                slot = S_W + 8 + i if half else S_W + i * 4 + 3
+                span = (wup, wdown)[GATHERS[i][0]].at[pl.ds(0, 256)]
+                remote(span, span, send.at[slot], recv.at[slot], sibling).wait()
+                weight_tiles(i, 3, True, half)
 
     weight_copy(block_o, head, S_O + 1, sibling).start()
     weight_copy(block_o, head, S_O + 2, peers["x"]).start()

time: 173 us -> 173 us (level)
  no operation moved by 1% of the time
where the time goes in v7:
time: 173 us; the launch traced here: 171 us
  Pallas kernels  168 us (97%)
  local copies, waits for them, and re-layouts  2.3 us (1%)
    pallas_call x1, Pallas kernels, layer_call(): pl.pallas_call(layer_kernel, out_shape=outs, in_specs=[vmem] * len(args),...  164 us
    pallas_call x1, Pallas kernels, local_call(): pl.pallas_call(kernel, out_shape=tuple((jax.ShapeDtypeStruct(*o) for o in...  3.85 us

profile of v7, /device:TPU:19, one launch (start us, length us, event | category | flops | bytes accessed | tf_op | source)
XLA Modules:
  0.0 170.7 jit_solution(3673964083215874035)
XLA Ops:
  0.6 163.9 %layer.1 = (bf16[1024,512]{1,0:T(8,128)(2,1)}, f32[1024,512]{1,0:T(8,128)}, bf16[512,512]{1,0:T(8,128)(2,1)}, bf16[512,128]{1,0:T(8,128)(2,1)}, bf16[512,128]{1,...) custom-call(bf16[1024,512]{1,0:T(8,128)(2,1)} %tokens.1, ...), custom_call_target="tpu_custom_call" | custom-call | tf_op jit(solution)/shard_map/layer/pallas_call | solution.py:1155
  164.5 0.0 copy-start.1
  164.6 0.0 copy-start
  164.6 3.9 %update.1 = (f32[512,384]{1,0:T(8,128)}, f32[512,384]{1,0:T(8,128)}, f32[128,512]{1,0:T(8,128)}, f32[128,512]{1,0:T(8,128)}, f32[64,512]{1,0:T(8,128)}, /*index=...) custom-call(bf16[512,512]{1,0:T(8,128)(2,1)} %get-tuple-element.39.s, ...), custom_call_target="tpu_custom_call" | custom-call | tf_op jit(solution)/shard_map/update/pallas_call | solution.py:338
  168.4 0.0 copy-done.1
  168.4 1.0 copy.30
  169.4 0.0 copy-done
  169.4 1.3 copy.31
Async XLA Ops:
  164.5 3.9 %copy-start.1 = (bf16[1024,512]{1,0:T(8,128)(2,1)S(1)}, bf16[1024,512]{1,0:T(8,128)(2,1)}, u32[]{:S(2)}) copy-start(bf16[1024,512]{1,0:T(8,128)(2,1)} %get-tuple-element.74) | copy-start | bytes 3145732
  164.6 4.9 %copy-start = (f32[1024,512]{1,0:T(8,128)S(1)}, f32[1024,512]{1,0:T(8,128)}, u32[]{:S(2)}) copy-start(f32[1024,512]{1,0:T(8,128)} %get-tuple-element.75) | copy-start | bytes 6291460
